TPU v7x, 32 devices: a whole 2x2x4 slice. The times are simulated.
32 devices in a mesh: ang: 8 (over y, x, core), ax: 4 (over z).
Axes of the slice: x: 2, y: 2, z: 4, core: 2. Of those that a mesh axis runs over, the one named last changes fastest.
Arguments:
- conserved: float32 [5, 96, 256, 256], P(None, 'ax', 'ang'), may hold values from -0.3 to 3.5, as said below
- deriv_matrix: float32 [512, 512], replicated, may hold values from -1 to 1
- filter_matrix: float32 [512, 512], replicated, may hold values from 0 to 1
Outputs:
- advanced: float32 [5, 96, 256, 256], P(None, 'ax', 'ang')
Inputs may be any that keep to these rules, and one draw needn't show every extreme that they name: `conserved`: component 0 (density) lies in 0.8 to 1.2, components 1 to 3 (momenta) in -0.3 to 0.3, and the energy exceeds the kinetic energy by 1.75 to 3.25.
All inputs are finite; a program needn't handle non-finite values.
Results may differ from a plain program's by a relative error of at most 0.0003.
Values sent between devices are 32-bit elements; how exact they have to be, the bound alone decides.
No kernel may reach another device: no remote copies, remote signals or barrier semaphores. Data moves between devices by JAX's collectives and lax.ppermute only.
A program may use at most 128 MiB of HBM per device.

v0:
```python
import functools
import math

import jax
import jax.numpy as jnp
from jax import lax
from jax.experimental import pallas as pl
from jax.experimental.pallas import tpu as pltpu
from jax.sharding import PartitionSpec as P

gamma_ratio = 1.4
courant = 0.15
highest = lax.Precision.HIGHEST
CHUNKS = 1


def split_kernel(w_ref, hi_ref, lo_ref):
    w = w_ref[...]
    hi = w.astype(jnp.bfloat16)
    hi_ref[...] = hi
    lo_ref[...] = (w - hi.astype(jnp.float32)).astype(jnp.bfloat16)


def split_weights(w):
    shape = jax.ShapeDtypeStruct(w.shape, jnp.bfloat16)
    return pl.pallas_call(split_kernel, out_shape=(shape, shape), name="split_weights")(w)


def speeds(q):
    rho, mx, my, mz, en = q
    inv = 1.0 / rho
    ux, uy, uz = mx * inv, my * inv, mz * inv
    pressure = (gamma_ratio - 1.0) * (en - 0.5 * (mx * ux + my * uy + mz * uz))
    return ux, uy, uz, pressure, en + pressure


def angular_of(q, state, cos, sin):
    rho, mx, my, mz, en = q
    ux, uy, uz, pressure, enthalpy = state
    us = uy * cos - ux * sin
    return (rho * us, mx * us - pressure * sin, my * us + pressure * cos, mz * us, enthalpy * us)


def radial_of(q, state, cos, sin, scale):
    rho, mx, my, mz, en = q
    ux, uy, uz, pressure, enthalpy = state
    ur = (ux * cos + uy * sin) * scale
    ps = pressure * scale
    return (rho * ur, mx * ur + ps * cos, my * ur + ps * sin, mz * ur, enthalpy * ur)


def axial_of(q, state):
    rho, mx, my, mz, en = q
    ux, uy, uz, pressure, enthalpy = state
    return (mz, mx * uz, my * uz, mz * uz + pressure, enthalpy * uz)


def section_kernel(
    dims, weight, twist, mixed,
    flags_ref, trig_ref, edge_trig_ref, radius_ref, q_ref, prev_ref, next_ref,
    left_ref, right_ref, base_ref, whi_ref, wlo_ref,
    out_ref, axial_s, part_s, ang_s, hi_s, lo_s,
):
    fields, planes, rows, radii = dims
    factor = weight * courant
    lane_halves = radii // 128
    ang_factor = factor * twist / 12.0

    def store_lhs(f, p, column, value):
        hi = value.astype(jnp.bfloat16)
        hi_s[f, p, :, column : column + radii] = hi
        lo_s[f, p, :, column : column + radii] = (value - hi.astype(jnp.float32)).astype(jnp.bfloat16)

    for s in range(2):
        for side, ref in ((0, prev_ref), (1, next_ref)):
            for k in range(2):
                q = tuple(ref[s, f, k] for f in range(fields))
                axial = axial_of(q, speeds(q))
                at = k + side * (planes + 2)
                for f in range(fields):
                    axial_s[s, f, at] = jnp.where(flags_ref[side] > 0, axial[f], 0.0)

    def first_pass(p, carry):
        edge = []
        for side, ref in ((0, left_ref), (1, right_ref)):
            q = tuple(ref[f, p] for f in range(fields))
            edge.append(angular_of(q, speeds(q), edge_trig_ref[0, side], edge_trig_ref[1, side]))
        scale = -factor * radius_ref[...]
        for s in range(2):
            q = tuple(q_ref[s, f, p] for f in range(fields))
            state = speeds(q)
            cos, sin = trig_ref[0, s], trig_ref[1, s]
            axial = axial_of(q, state)
            radial = radial_of(q, state, cos, sin, scale)
            angular = angular_of(q, state, cos, sin)
            for f in range(fields):
                axial_s[s, f, p + 2] = axial[f]
                store_lhs(f, p, 2 * radii + s * radii, radial[f])
                for l in range(lane_halves):
                    lanes = slice(l * 128, l * 128 + 128)
                    ang_s[s, f, l, 8 : 8 + rows] = angular[f][:, lanes]
                    ang_s[s, f, l, 6:8] = edge[0][f][2 * s : 2 * s + 2, lanes]
                    ang_s[s, f, l, 8 + rows : 10 + rows] = edge[1][f][2 * s : 2 * s + 2, lanes]
            for f in range(fields):
                for l in range(lane_halves):
                    lanes = slice(l * 128, l * 128 + 128)

                    def at(k):
                        return ang_s[s, f, l, 8 + k : 8 + k + rows]

                    slope = 8.0 * (at(1) - at(-1)) - (at(2) - at(-2))
                    own = q_ref[s, f, p, :, lanes]
                    if mixed:
                        own = 0.5 * base_ref[s, f, p, :, lanes] + 0.5 * own
                    part_s[s, f, p, :, lanes] = own - ang_factor * slope
        return carry

    lax.fori_loop(0, planes, first_pass, 0)

    def second_pass(p, carry):
        scale = (factor / 12.0) * radius_ref[...]
        for s in range(2):
            for f in range(fields):
                slope = 8.0 * (axial_s[s, f, p + 3] - axial_s[s, f, p + 1]) - (
                    axial_s[s, f, p + 4] - axial_s[s, f, p]
                )
                store_lhs(f, p, s * radii, part_s[s, f, p] - scale * slope)
        return carry

    lax.fori_loop(0, planes, second_pass, 0)

    def mapped(hi, lo, s):
        columns = slice(s * radii, s * radii + radii)
        whi = whi_ref[:, columns]
        dot = functools.partial(jnp.dot, preferred_element_type=jnp.float32)
        return dot(hi, whi) + dot(lo, whi) + dot(hi, wlo_ref[:, columns])

    if planes * rows >= 256:
        def one_field(f, carry):
            hi = hi_s[f].reshape(planes * rows, 4 * radii)
            lo = lo_s[f].reshape(planes * rows, 4 * radii)
            for s in range(2):
                out_ref[s, f] = mapped(hi, lo, s).reshape(planes, rows, radii)
            return carry

        lax.fori_loop(0, fields, one_field, 0)
    else:
        hi = hi_s[...].reshape(fields * planes * rows, 4 * radii)
        lo = lo_s[...].reshape(fields * planes * rows, 4 * radii)
        for s in range(2):
            out_ref[s] = mapped(hi, lo, s).reshape(fields, planes, rows, radii)


def section_chunk(consts, weight, twist, flags, q, prev, next_, left, right, base, name):
    trig, edge_trig, radius, whi, wlo = consts
    _, fields, planes, rows, radii = q.shape
    mixed = base is not None
    whole = pl.BlockSpec(memory_space=pltpu.VMEM)
    lines = fields * planes * rows

    def two_planes(array, last):
        at = array.shape[2] // 2 - 1 if last else 0
        return pl.BlockSpec((2, fields, 2, rows, radii), lambda i: (0, 0, at, 0, 0))

    def full(array):
        zeros = (0,) * array.ndim
        return pl.BlockSpec(array.shape, lambda i: zeros)

    if not mixed:
        base = radius
    return pl.pallas_call(
        functools.partial(section_kernel, (fields, planes, rows, radii), weight, twist, mixed),
        grid=(1,),
        out_shape=jax.ShapeDtypeStruct(q.shape, jnp.float32),
        in_specs=[
            pl.BlockSpec(memory_space=pltpu.SMEM), full(trig), full(edge_trig), full(radius), full(q),
            two_planes(prev, True), two_planes(next_, False), full(left), full(right), full(base),
            full(whi), full(wlo),
        ],
        out_specs=full(q),
        scratch_shapes=[
            pltpu.VMEM((2, fields, planes + 4, rows, radii), jnp.float32),
            pltpu.VMEM((2, fields, planes, rows, radii), jnp.float32),
            pltpu.VMEM((2, fields, radii // 128, rows + 16, 128), jnp.float32),
            pltpu.VMEM((fields, planes, rows, 4 * radii), jnp.bfloat16),
            pltpu.VMEM((fields, planes, rows, 4 * radii), jnp.bfloat16),
        ],
        cost_estimate=pl.CostEstimate(
            flops=2 * lines * 4 * radii * 2 * radii * 3, bytes_accessed=8 * lines * radii * 4,
            transcendentals=0,
        ),
        name=name,
    )(flags, trig, edge_trig, radius, q, prev, next_, left, right, base, whi, wlo)


def folded(matrix, radii):
    tall = jnp.concatenate([matrix[radii:], matrix[:radii][::-1]], axis=0)
    return jnp.concatenate([tall[:, radii:], tall[:, :radii][:, ::-1]], axis=1)


def per_device(conserved, deriv_matrix, filter_matrix):
    n = lax.axis_size("ang")
    count = lax.axis_size("ax")
    fields, planes, ang_dev, radii = conserved.shape
    rows = ang_dev // 2
    half = n // 2
    total = ang_dev * n
    twist = total / (2.0 * math.pi * radii)
    pos = lax.axis_index("ang")
    h, j, c = pos // half, (pos % half) // 2, pos % 2
    ring = 4 * j + 2 * (h ^ (j & 1)) + c
    keeps = h == (c ^ (j & 1))

    def dev(hh, jj, cc):
        return hh * half + 2 * jj + cc

    spots = [(hh, jj, cc) for hh in range(2) for jj in range(n // 4) for cc in range(2)]
    givers = [(hh, jj, cc) for hh, jj, cc in spots if hh != (cc ^ (jj & 1))]
    keepers = [(hh, jj, cc) for hh, jj, cc in spots if hh == (cc ^ (jj & 1))]
    to_even = [(dev(*g), dev(1 - g[0], g[1], 0)) for g in givers]
    to_odd = [(dev(*g), dev(1 - g[0], g[1], 1)) for g in givers]
    to_core = [(dev(*k), dev(k[0], k[1], 1 - k[2])) for k in keepers]
    order = [dev((r % 4 // 2) ^ (r // 4 & 1), r // 4, r % 2) for r in range(n)]
    to_left = [(order[r], order[(r - 1) % n]) for r in range(n)]
    to_right = [(order[r], order[(r + 1) % n]) for r in range(n)]
    up = [(i, i + 1) for i in range(count - 1)]
    down = [(i + 1, i) for i in range(count - 1)]

    def back(table):
        return [(b, a) for a, b in table]

    def angles(offsets):
        index = (ring * rows + offsets) % total
        return index.astype(jnp.float32) * (2.0 * math.pi / total)

    seg = jnp.arange(2, dtype=jnp.int32)[:, None] * (total // 2)
    centre = angles(seg + jnp.arange(rows, dtype=jnp.int32))
    left_rows = angles((seg + jnp.arange(-2, 0, dtype=jnp.int32)).reshape(4))
    right_rows = angles((seg + jnp.arange(rows, rows + 2, dtype=jnp.int32)).reshape(4))
    edges = jnp.stack([left_rows, right_rows])

    def spread(values):
        return jnp.broadcast_to(values[..., None], values.shape + (radii,))

    trig = spread(jnp.stack([jnp.cos(centre), jnp.sin(centre)]))
    edge_trig = spread(jnp.stack([jnp.cos(edges), jnp.sin(edges)]))
    radius = ((jnp.arange(radii, dtype=jnp.int32).astype(jnp.float32) + 0.5) / radii)[None]
    signs = jnp.where(jnp.arange(2 * radii, dtype=jnp.int32) < radii, -1.0, 1.0).astype(jnp.float32)
    composite = jnp.dot(filter_matrix, signs[:, None] * deriv_matrix, precision=highest)
    weights = jnp.concatenate(
        [folded(filter_matrix, radii).T, folded(composite, radii).T], axis=0
    )
    whi, wlo = split_weights(weights)
    consts = (trig, edge_trig, radius, whi, wlo)

    chunks = CHUNKS
    step = planes // chunks
    layer = lax.axis_index("ax")
    low_ok = (layer > 0).astype(jnp.int32)
    high_ok = (layer < count - 1).astype(jnp.int32)
    one = jnp.ones((), jnp.int32)

    def take(k):
        block = lax.slice_in_dim(conserved, k * step, (k + 1) * step, axis=1)
        first_half, second_half = block[:, :, :rows], block[:, :, rows:]
        from_even = lax.ppermute(first_half, "ang", to_even)
        from_odd = lax.ppermute(second_half, "ang", to_odd)
        own = jnp.where(c == 0, first_half, second_half)
        other = jnp.where(c == 0, second_half, first_half)
        near = jnp.where(keeps, own, lax.ppermute(other, "ang", to_core))
        far = jnp.where(c == 0, from_even, from_odd)
        return jnp.stack([jnp.where(h == 0, near, far), jnp.where(h == 0, far, near)])

    def edge_rows(q, start, swap):
        piece = q[:, :, :, start : start + 2]
        pair = (piece[0], piece[1])
        return jnp.concatenate(
            [jnp.where(swap, pair[1], pair[0]), jnp.where(swap, pair[0], pair[1])], axis=2
        )

    def halos(q):
        left = lax.ppermute(edge_rows(q, rows - 2, ring == n - 1), "ang", to_right)
        right = lax.ppermute(edge_rows(q, 0, ring == 0), "ang", to_left)
        return left, right

    def section(qs, bases, weight, name):
        sides = [halos(q) for q in qs]
        low = lax.ppermute(qs[-1][:, :, step - 2 :], "ax", up)
        high = lax.ppermute(qs[0][:, :, :2], "ax", down)
        outs = []
        for k in range(chunks):
            flags = jnp.stack([low_ok if k == 0 else one, high_ok if k == chunks - 1 else one])
            outs.append(
                section_chunk(
                    consts, weight, twist, flags, qs[k],
                    low if k == 0 else qs[k - 1], high if k == chunks - 1 else qs[k + 1],
                    sides[k][0], sides[k][1], None if bases is None else bases[k], name,
                )
            )
        return outs

    def give_back(q):
        near = jnp.where(h == 0, q[0], q[1])
        far = jnp.where(h == 0, q[1], q[0])
        even = lax.ppermute(far, "ang", back(to_even))
        odd = lax.ppermute(far, "ang", back(to_odd))
        core = lax.ppermute(near, "ang", back(to_core))
        first_half = jnp.where(keeps, jnp.where(c == 0, near, core), even)
        second_half = jnp.where(keeps, jnp.where(c == 0, core, near), odd)
        return jnp.concatenate([first_half, second_half], axis=2)

    qs = [take(k) for k in range(chunks)]
    first = section(qs, None, 1.0, "section_one")
    advanced = section(first, qs, 0.5, "section_two")
    return jnp.concatenate([give_back(q) for q in advanced], axis=1)


def solution(mesh):
    placed = (P(None, "ax", "ang", None), P(), P())
    return jax.shard_map(
        per_device,
        mesh=mesh,
        in_specs=placed,
        out_specs=P(None, "ax", "ang", None),
        check_vma=False,
    )
```

profile of v0, /device:TPU:31, one launch (start us, length us, event | category | flops | bytes accessed | tf_op | source)
XLA Modules:
  0.0 188.9 jit_solution(1647925384128675362)
XLA Ops:
  0.0 5.3 %broadcast_select_fusion.1 = (f32[5,24,16,256]{3,2,1,0:T(8,128)}, f32[5,24,16,256]{3,2,1,0:T(8,128)}, f32[5,24,16,256]{3,2,1,0:T(8,128)}) fusion(pred[]{:T(512)S(6)} %eq.19, f32[5,24,32,256]{3,2,1,0:T(8,128)} %param.3), kind=kLoop, calls=%fused_computation.23 | loop fusion | flops 491520 | bytes 9830401 | tf_op jit(solution)/shard_map/jit(_where)/select_n | solution.py:269
  5.3 1.3 collective-permute-start
  6.6 4.7 %collective-permute-start.2 = (f32[5,24,16,256]{3,2,1,0:T(8,128)}, f32[5,24,16,256]{3,2,1,0:T(8,128)}, u32[]{:S(2)}, u32[]{:S(2)}) collective-permute-start(f32[5,24,16,256]{3,2,1,0:T(8,128)} %get-tuple-element.28), channel_id=1, source_target_pairs={{4,20},{8,28},{16,4},{28,12},{5,21},{9,29},{17,5},{29,13},{6,22},{... | collective-permute-start | bytes 5898248 | tf_op jit(solution)/shard_map/ppermute | solution.py:267
  11.2 3.5 %collective-permute-start.1 = (f32[5,24,16,256]{3,2,1,0:T(8,128)}, f32[5,24,16,256]{3,2,1,0:T(8,128)}, u32[]{:S(2)}, u32[]{:S(2)}) collective-permute-start(f32[5,24,16,256]{3,2,1,0:T(8,128)} %get-tuple-element.29), channel_id=1, source_target_pairs={{4,16},{8,24},{16,0},{28,8},{5,17},{9,25},{17,1},{29,9},{6,18},{10... | collective-permute-start | bytes 5898248 | tf_op jit(solution)/shard_map/ppermute | solution.py:266
  14.8 3.6 %convolution_bitcast_fusion = f32[512,512]{0,1:T(8,128)S(1)} fusion(f32[512,512]{1,0:T(8,128)S(1)} %copy-done.2, f32[512,512]{1,0:T(8,128)S(1)} %copy-done.3, f32[512]{0:T(512)S(1)} %fusion.6), kind=kOutput, calls=%fused_computation.14 | convolution fusion | flops 1610874880 | bytes 3147776 | tf_op jit(solution)/shard_map/dot_general | solution.py:249
  18.7 0.7 rev.14
  19.6 0.3 rev.15
  20.3 0.7 rev.12
  21.2 0.3 rev.13
  21.5 0.5 add_multiply_fusion.radius_ref.base_ref
  22.3 1.5 pad_maximum_fusion.2.w_ref
  23.9 9.2 %collective-permute-done.2 = f32[5,24,16,256]{3,2,1,0:T(8,128)} collective-permute-done((f32[5,24,16,256]{3,2,1,0:T(8,128)}, f32[5,24,16,256]{3,2,1,0:T(8,128)}, u32[]{:S(2)}, u32[]{:S(2)}) %collective-permute-start.2) | collective-permute-done | bytes 1966112 | tf_op jit(solution)/shard_map/ppermute | solution.py:267
  33.1 21.1 %collective-permute-done.1 = f32[5,24,16,256]{3,2,1,0:T(8,128)} collective-permute-done((f32[5,24,16,256]{3,2,1,0:T(8,128)}, f32[5,24,16,256]{3,2,1,0:T(8,128)}, u32[]{:S(2)}, u32[]{:S(2)}) %collective-permute-start.1) | collective-permute-done | bytes 1966112 | tf_op jit(solution)/shard_map/ppermute | solution.py:266
  54.2 3.4 %select_bitcast_fusion.3 = (f32[1,5,24,16,256]{4,3,2,1,0:T(8,128)S(1)}, f32[1,5,24,16,256]{4,3,2,1,0:T(8,128)S(1)}) fusion(pred[]{:T(512)S(6)} %eq.34, f32[5,24,16,256]{3,2,1,0:T(8,128)} %collective-permute-done.1, f32[5,24,16,256]{3,2,1,0:T(8,128)} %collective-permute-done.2, pred[]{:T(512)S(6)} %eq.19, f32[5,24,16,256]{3,2,1,0:T(8,128)} %collective-permute-done, ...), kind=kLoop, calls=%fused_computation.12 | loop fusion | flops 2457600 | bytes 13762563 | tf_op jit(solution)/shard_map/stack | solution.py:272
  57.6 0.5 select_bitcast_fusion.9
  58.1 0.2 pad_maximum_fusion.5
  58.3 2.5 %collective-permute-start.5 = (f32[5,24,4,256]{3,2,1,0:T(4,128)S(1)}, f32[5,24,4,256]{3,2,1,0:T(4,128)}, u32[]{:S(2)}, u32[]{:S(2)}) collective-permute-start(f32[5,24,4,256]{3,2,1,0:T(4,128)S(1)} %pad_maximum_fusion.5), channel_id=1, source_target_pairs={{0,4},{4,16},{16,20},{20,24},{24,28},{28,8},{8,12},{12,0},{1,5},{5... | collective-permute-start | bytes 1474568 | tf_op jit(solution)/shard_map/ppermute | solution.py:282
  60.8 0.2 pad_maximum_fusion.6
  61.1 0.8 fusion.5
  61.9 2.8 %collective-permute-start.4 = (f32[2,5,2,16,256]{4,3,2,1,0:T(8,128)}, f32[2,5,2,16,256]{4,3,2,1,0:T(8,128)}, u32[]{:S(2)}, u32[]{:S(2)}) collective-permute-start(f32[2,5,2,16,256]{4,3,2,1,0:T(8,128)} %get-tuple-element.25), channel_id=1, source_target_pairs={{1,0},{2,1},{3,2},{5,4},{6,5},{7,6},{9,8},{10,9},{11,10},{13,12},{... | collective-permute-start | bytes 983048 | tf_op jit(solution)/shard_map/ppermute | solution.py:289
  64.7 1.3 collective-permute-start.3
  66.0 0.7 add_convert_fusion.flags_ref
  66.6 3.1 %split_weights.1 = (bf16[1024,512]{1,0:T(8,128)(2,1)}, bf16[1024,512]{1,0:T(8,128)(2,1)}) custom-call(f32[1024,512]{1,0:T(8,128)} %pad_maximum_fusion.2.w_ref), custom_call_target="tpu_custom_call" | custom-call | tf_op jit(solution)/shard_map/split_weights/pallas_call | solution.py:26
  69.7 4.0 %pad_maximum_fusion.q_ref.base_ref = f32[2,5,24,16,256]{4,3,2,1,0:T(8,128)} fusion(f32[1,5,24,16,256]{4,3,2,1,0:T(8,128)} %copy-done, f32[1,5,24,16,256]{4,3,2,1,0:T(8,128)S(1)} %get-tuple-element.9), kind=kLoop, calls=%fused_computation.2 | loop fusion | flops 983040 | bytes 7864320 | tf_op jit(solution)/shard_map/stack | solution.py:272
  73.8 2.2 %collective-permute-done.3.prev_ref = f32[2,5,2,16,256]{4,3,2,1,0:T(8,128)} collective-permute-done((f32[2,5,2,16,256]{4,3,2,1,0:T(8,128)S(1)}, f32[2,5,2,16,256]{4,3,2,1,0:T(8,128)}, u32[]{:S(2)}, u32[]{:S(2)}) %collective-permute-start.3) | collective-permute-done | bytes 327712 | tf_op jit(solution)/shard_map/ppermute | solution.py:288
  76.0 0.7 broadcast_in_dim.11.edge_trig_ref
  76.7 0.7 broadcast_in_dim.10.trig_ref
  77.4 16.9 %section_one.1.q_ref = f32[2,5,24,16,256]{4,3,2,1,0:T(8,128)} custom-call(s32[2]{0:T(128)} %add_convert_fusion.flags_ref, f32[2,2,16,256]{3,2,1,0:T(8,128)} %broadcast_in_dim.10.trig_ref, f32[2,2,4,256]{3,2,1,0:T(4,128)} %broadcast_in_dim.11.edge_trig_ref, f32[1,256]{1,0:T(1,128)} %add_multiply_fusion.radius_ref.base_ref, ...), custom_call_target="tpu_custom_call" | custom-call | flops 6039797760 | bytes 15728640 | tf_op jit(solution)/shard_map/section_one/pallas_call | solution.py:171
  94.3 2.5 %select_bitcast_fusion.5 = (f32[5,24,2,256]{3,2,1,0:T(2,128)S(1)}, f32[5,24,2,256]{3,2,1,0:T(2,128)S(1)}, f32[5,24,2,256]{3,2,1,0:T(2,128)S(1)}, f32[5,24,2,256]{3,2,1,0:T(2,128)S(1)}) fusion(pred[]{:T(512)S(6)} %eq.36, f32[2,5,24,16,256]{4,3,2,1,0:T(8,128)} %section_one.1.q_ref, pred[]{:T(512)S(6)} %eq.35), kind=kLoop, calls=%fused_computation.36 | loop fusion | flops 245760 | bytes 1966082 | tf_op jit(solution)/shard_map/jit(_where)/select_n | solution.py:278
  96.8 0.2 pad_maximum_fusion.7
  97.0 0.8 collective-permute-start.9
  98.1 1.1 fusion.22
  99.3 3.3 %collective-permute-start.8 = (f32[2,5,2,16,256]{4,3,2,1,0:T(8,128)S(1)}, f32[2,5,2,16,256]{4,3,2,1,0:T(8,128)S(1)}, u32[]{:S(2)}, u32[]{:S(2)}) collective-permute-start(f32[2,5,2,16,256]{4,3,2,1,0:T(8,128)S(1)} %get-tuple-element.19), channel_id=1, source_target_pairs={{1,0},{2,1},{3,2},{5,4},{6,5},{7,6},{9,8},{10,9},{11,10},{13,12},{... | collective-permute-start | bytes 983048 | tf_op jit(solution)/shard_map/ppermute | solution.py:289
  102.5 1.5 collective-permute-start.7
  104.0 6.0 %collective-permute-done.8.next_ref = f32[2,5,2,16,256]{4,3,2,1,0:T(8,128)S(1)} collective-permute-done((f32[2,5,2,16,256]{4,3,2,1,0:T(8,128)S(1)}, f32[2,5,2,16,256]{4,3,2,1,0:T(8,128)S(1)}, u32[]{:S(2)}, u32[]{:S(2)}) %collective-permute-start.8) | collective-permute-done | bytes 327712 | tf_op jit(solution)/shard_map/ppermute | solution.py:289
  110.0 3.9 %collective-permute-done.7.prev_ref = f32[2,5,2,16,256]{4,3,2,1,0:T(8,128)S(1)} collective-permute-done((f32[2,5,2,16,256]{4,3,2,1,0:T(8,128)S(1)}, f32[2,5,2,16,256]{4,3,2,1,0:T(8,128)S(1)}, u32[]{:S(2)}, u32[]{:S(2)}) %collective-permute-start.7) | collective-permute-done | bytes 327712 | tf_op jit(solution)/shard_map/ppermute | solution.py:288
  114.0 0.7 copy-done.7
  114.9 0.8 copy-done.5
  115.7 18.3 %section_two.1 = f32[2,5,24,16,256]{4,3,2,1,0:T(8,128)} custom-call(s32[2]{0:T(128)} %add_convert_fusion.flags_ref, f32[2,2,16,256]{3,2,1,0:T(8,128)} %broadcast_in_dim.10.trig_ref, f32[2,2,4,256]{3,2,1,0:T(4,128)} %broadcast_in_dim.11.edge_trig_ref, f32[1,256]{1,0:T(1,128)} %add_multiply_fusion.radius_ref.base_ref, ...), custom_call_target="tpu_custom_call" | custom-call | flops 6039797760 | bytes 15728640 | tf_op jit(solution)/shard_map/section_two/pallas_call | solution.py:171
  134.0 2.6 %select_bitcast_fusion.1 = (f32[5,24,16,256]{3,2,1,0:T(8,128)S(1)}, f32[5,24,16,256]{3,2,1,0:T(8,128)S(1)}) fusion(f32[2,5,24,16,256]{4,3,2,1,0:T(8,128)} %section_two.1, pred[]{:T(512)S(6)} %eq.34), kind=kLoop, calls=%fused_computation.10 | loop fusion | flops 983040 | bytes 7864321 | tf_op jit(solution)/shard_map/jit(_where)/select_n | solution.py:303
  136.6 2.6 %collective-permute-start.11 = (f32[5,24,16,256]{3,2,1,0:T(8,128)S(1)}, f32[5,24,16,256]{3,2,1,0:T(8,128)S(1)}, u32[]{:S(2)}, u32[]{:S(2)}) collective-permute-start(f32[5,24,16,256]{3,2,1,0:T(8,128)S(1)} %get-tuple-element.13), channel_id=1, source_target_pairs={{4,0},{8,12},{16,20},{28,24},{5,1},{9,13},{17,21},{29,25},{6,2},{1... | collective-permute-start | bytes 5898248 | tf_op jit(solution)/shard_map/ppermute | solution.py:307
  139.2 1.9 %collective-permute-start.13 = (f32[5,24,16,256]{3,2,1,0:T(8,128)S(1)}, f32[5,24,16,256]{3,2,1,0:T(8,128)S(1)}, u32[]{:S(2)}, u32[]{:S(2)}) collective-permute-start(f32[5,24,16,256]{3,2,1,0:T(8,128)S(1)} %get-tuple-element.14), channel_id=1, source_target_pairs={{20,4},{28,8},{4,16},{12,28},{21,5},{29,9},{5,17},{13,29},{22,6},{... | collective-permute-start | bytes 5898248 | tf_op jit(solution)/shard_map/ppermute | solution.py:306
  141.1 1.3 collective-permute-start.12
  142.4 0.2 collective-permute-done.11
  142.7 40.5 %collective-permute-done.13 = f32[5,24,16,256]{3,2,1,0:T(8,128)S(1)} collective-permute-done((f32[5,24,16,256]{3,2,1,0:T(8,128)S(1)}, f32[5,24,16,256]{3,2,1,0:T(8,128)S(1)}, u32[]{:S(2)}, u32[]{:S(2)}) %collective-permute-start.13) | collective-permute-done | bytes 1966112 | tf_op jit(solution)/shard_map/ppermute | solution.py:306
  183.1 2.5 %collective-permute-done.12 = f32[5,24,16,256]{3,2,1,0:T(8,128)S(1)} collective-permute-done((f32[5,24,16,256]{3,2,1,0:T(8,128)S(1)}, f32[5,24,16,256]{3,2,1,0:T(8,128)S(1)}, u32[]{:S(2)}, u32[]{:S(2)}) %collective-permute-start.12) | collective-permute-done | bytes 1966112 | tf_op jit(solution)/shard_map/ppermute | solution.py:305
  185.6 1.0 select_select_fusion.1
  186.6 2.3 %pad_maximum_fusion.1 = f32[5,24,32,256]{3,2,1,0:T(8,128)} fusion(f32[5,24,16,256]{3,2,1,0:T(8,128)S(1)} %get-tuple-element.12, f32[5,24,16,256]{3,2,1,0:T(8,128)S(1)} %get-tuple-element.11), kind=kLoop, calls=%fused_computation.5 | loop fusion | flops 983040 | bytes 7864320 | tf_op jit(solution)/shard_map/concatenate | solution.py:310
  (42 shorter events, 2.0 us)
Async XLA Ops:
  0.0 14.8 %copy-start.2 = (f32[512,512]{1,0:T(8,128)S(1)}, f32[512,512]{1,0:T(8,128)}, u32[]{:S(2)}) copy-start(f32[512,512]{1,0:T(8,128)} %param.5) | copy-start | bytes 3145732
  0.0 14.8 %copy-start.3 = (f32[512,512]{1,0:T(8,128)S(1)}, f32[512,512]{1,0:T(8,128)}, u32[]{:S(2)}) copy-start(f32[512,512]{1,0:T(8,128)} %param.4) | copy-start | bytes 3145732
  5.3 18.6 %collective-permute-start = (f32[5,24,16,256]{3,2,1,0:T(8,128)}, f32[5,24,16,256]{3,2,1,0:T(8,128)}, u32[]{:S(2)}, u32[]{:S(2)}) collective-permute-start(f32[5,24,16,256]{3,2,1,0:T(8,128)} %get-tuple-element.27), channel_id=1, source_target_pairs={{0,4},{12,8},{20,16},{24,28},{1,5},{13,9},{21,17},{25,29},{2,6},{1... | collective-permute-start | bytes 5898248 | tf_op jit(solution)/shard_map/ppermute | solution.py:270
  6.6 26.5 %collective-permute-start.2 = (f32[5,24,16,256]{3,2,1,0:T(8,128)}, f32[5,24,16,256]{3,2,1,0:T(8,128)}, u32[]{:S(2)}, u32[]{:S(2)}) collective-permute-start(f32[5,24,16,256]{3,2,1,0:T(8,128)} %get-tuple-element.28), channel_id=1, source_target_pairs={{4,20},{8,28},{16,4},{28,12},{5,21},{9,29},{17,5},{29,13},{6,22},{... | collective-permute-start | bytes 5898248 | tf_op jit(solution)/shard_map/ppermute | solution.py:267
  11.2 42.9 %collective-permute-start.1 = (f32[5,24,16,256]{3,2,1,0:T(8,128)}, f32[5,24,16,256]{3,2,1,0:T(8,128)}, u32[]{:S(2)}, u32[]{:S(2)}) collective-permute-start(f32[5,24,16,256]{3,2,1,0:T(8,128)} %get-tuple-element.29), channel_id=1, source_target_pairs={{4,16},{8,24},{16,0},{28,8},{5,17},{9,25},{17,1},{29,9},{6,18},{10... | collective-permute-start | bytes 5898248 | tf_op jit(solution)/shard_map/ppermute | solution.py:266
  22.3 31.9 %copy-start.1 = (f32[5,24,32,256]{3,2,1,0:T(8,128)S(1)}, f32[5,24,32,256]{3,2,1,0:T(8,128)}, u32[]{:S(2)}) copy-start(f32[5,24,32,256]{3,2,1,0:T(8,128)} %param.3) | copy-start | bytes 11796484
  57.5 3.6 %copy-start = (f32[1,5,24,16,256]{4,3,2,1,0:T(8,128)}, f32[1,5,24,16,256]{4,3,2,1,0:T(8,128)S(1)}, u32[]{:S(2)}) copy-start(f32[1,5,24,16,256]{4,3,2,1,0:T(8,128)S(1)} %get-tuple-element.10) | copy-start | bytes 5898244
  58.3 17.7 %collective-permute-start.5 = (f32[5,24,4,256]{3,2,1,0:T(4,128)S(1)}, f32[5,24,4,256]{3,2,1,0:T(4,128)}, u32[]{:S(2)}, u32[]{:S(2)}) collective-permute-start(f32[5,24,4,256]{3,2,1,0:T(4,128)S(1)} %pad_maximum_fusion.5), channel_id=1, source_target_pairs={{0,4},{4,16},{16,20},{20,24},{24,28},{28,8},{8,12},{12,0},{1,5},{5... | collective-permute-start | bytes 1474568 | tf_op jit(solution)/shard_map/ppermute | solution.py:282
  61.0 15.0 %collective-permute-start.6 = (f32[5,24,4,256]{3,2,1,0:T(4,128)S(1)}, f32[5,24,4,256]{3,2,1,0:T(4,128)}, u32[]{:S(2)}, u32[]{:S(2)}) collective-permute-start(f32[5,24,4,256]{3,2,1,0:T(4,128)S(1)} %pad_maximum_fusion.6), channel_id=1, source_target_pairs={{0,12},{4,0},{16,4},{20,16},{24,20},{28,24},{8,28},{12,8},{1,13},{... | collective-permute-start | bytes 1474568 | tf_op jit(solution)/shard_map/ppermute | solution.py:283
  61.9 11.9 %collective-permute-start.4 = (f32[2,5,2,16,256]{4,3,2,1,0:T(8,128)}, f32[2,5,2,16,256]{4,3,2,1,0:T(8,128)}, u32[]{:S(2)}, u32[]{:S(2)}) collective-permute-start(f32[2,5,2,16,256]{4,3,2,1,0:T(8,128)} %get-tuple-element.25), channel_id=1, source_target_pairs={{1,0},{2,1},{3,2},{5,4},{6,5},{7,6},{9,8},{10,9},{11,10},{13,12},{... | collective-permute-start | bytes 983048 | tf_op jit(solution)/shard_map/ppermute | solution.py:289
  64.7 11.3 %collective-permute-start.3 = (f32[2,5,2,16,256]{4,3,2,1,0:T(8,128)S(1)}, f32[2,5,2,16,256]{4,3,2,1,0:T(8,128)}, u32[]{:S(2)}, u32[]{:S(2)}) collective-permute-start(f32[2,5,2,16,256]{4,3,2,1,0:T(8,128)S(1)} %get-tuple-element.26), channel_id=1, source_target_pairs={{0,1},{1,2},{2,3},{4,5},{5,6},{6,7},{8,9},{9,10},{10,11},{12,13},{... | collective-permute-start | bytes 983048 | tf_op jit(solution)/shard_map/ppermute | solution.py:288
  97.0 17.0 %collective-permute-start.9 = (f32[5,24,4,256]{3,2,1,0:T(4,128)S(1)}, f32[5,24,4,256]{3,2,1,0:T(4,128)S(1)}, u32[]{:S(2)}, u32[]{:S(2)}) collective-permute-start(f32[5,24,4,256]{3,2,1,0:T(4,128)S(1)} %pad_maximum_fusion.7), channel_id=1, source_target_pairs={{0,4},{4,16},{16,20},{20,24},{24,28},{28,8},{8,12},{12,0},{1,5},{5... | collective-permute-start | bytes 1474568 | tf_op jit(solution)/shard_map/ppermute | solution.py:282
  98.1 15.9 %collective-permute-start.10 = (f32[5,24,4,256]{3,2,1,0:T(4,128)S(1)}, f32[5,24,4,256]{3,2,1,0:T(4,128)S(1)}, u32[]{:S(2)}, u32[]{:S(2)}) collective-permute-start(f32[5,24,4,256]{3,2,1,0:T(4,128)S(1)} %pad_maximum_fusion.8), channel_id=1, source_target_pairs={{0,12},{4,0},{16,4},{20,16},{24,20},{28,24},{8,28},{12,8},{1,13},{... | collective-permute-start | bytes 1474568 | tf_op jit(solution)/shard_map/ppermute | solution.py:283
  99.3 10.8 %collective-permute-start.8 = (f32[2,5,2,16,256]{4,3,2,1,0:T(8,128)S(1)}, f32[2,5,2,16,256]{4,3,2,1,0:T(8,128)S(1)}, u32[]{:S(2)}, u32[]{:S(2)}) collective-permute-start(f32[2,5,2,16,256]{4,3,2,1,0:T(8,128)S(1)} %get-tuple-element.19), channel_id=1, source_target_pairs={{1,0},{2,1},{3,2},{5,4},{6,5},{7,6},{9,8},{10,9},{11,10},{13,12},{... | collective-permute-start | bytes 983048 | tf_op jit(solution)/shard_map/ppermute | solution.py:289
  102.5 11.4 %collective-permute-start.7 = (f32[2,5,2,16,256]{4,3,2,1,0:T(8,128)S(1)}, f32[2,5,2,16,256]{4,3,2,1,0:T(8,128)S(1)}, u32[]{:S(2)}, u32[]{:S(2)}) collective-permute-start(f32[2,5,2,16,256]{4,3,2,1,0:T(8,128)S(1)} %get-tuple-element.20), channel_id=1, source_target_pairs={{0,1},{1,2},{2,3},{4,5},{5,6},{6,7},{8,9},{9,10},{10,11},{12,13},{... | collective-permute-start | bytes 983048 | tf_op jit(solution)/shard_map/ppermute | solution.py:288
  110.0 4.0 %copy-start.6 = (f32[2,5,2,16,256]{4,3,2,1,0:T(8,128)}, f32[2,5,2,16,256]{4,3,2,1,0:T(8,128)S(1)}, u32[]{:S(2)}) copy-start(f32[2,5,2,16,256]{4,3,2,1,0:T(8,128)S(1)} %collective-permute-done.8.next_ref) | copy-start | bytes 983044
  114.0 0.7 copy-start.7
  114.0 0.9 copy-start.4
  114.9 0.8 copy-start.5
  136.6 6.1 %collective-permute-start.11 = (f32[5,24,16,256]{3,2,1,0:T(8,128)S(1)}, f32[5,24,16,256]{3,2,1,0:T(8,128)S(1)}, u32[]{:S(2)}, u32[]{:S(2)}) collective-permute-start(f32[5,24,16,256]{3,2,1,0:T(8,128)S(1)} %get-tuple-element.13), channel_id=1, source_target_pairs={{4,0},{8,12},{16,20},{28,24},{5,1},{9,13},{17,21},{29,25},{6,2},{1... | collective-permute-start | bytes 5898248 | tf_op jit(solution)/shard_map/ppermute | solution.py:307
  139.2 43.9 %collective-permute-start.13 = (f32[5,24,16,256]{3,2,1,0:T(8,128)S(1)}, f32[5,24,16,256]{3,2,1,0:T(8,128)S(1)}, u32[]{:S(2)}, u32[]{:S(2)}) collective-permute-start(f32[5,24,16,256]{3,2,1,0:T(8,128)S(1)} %get-tuple-element.14), channel_id=1, source_target_pairs={{20,4},{28,8},{4,16},{12,28},{21,5},{29,9},{5,17},{13,29},{22,6},{... | collective-permute-start | bytes 5898248 | tf_op jit(solution)/shard_map/ppermute | solution.py:306
  141.1 44.5 %collective-permute-start.12 = (f32[5,24,16,256]{3,2,1,0:T(8,128)S(1)}, f32[5,24,16,256]{3,2,1,0:T(8,128)S(1)}, u32[]{:S(2)}, u32[]{:S(2)}) collective-permute-start(f32[5,24,16,256]{3,2,1,0:T(8,128)S(1)} %get-tuple-element.14), channel_id=1, source_target_pairs={{16,4},{24,8},{0,16},{8,28},{17,5},{25,9},{1,17},{9,29},{18,6},{26... | collective-permute-start | bytes 5898248 | tf_op jit(solution)/shard_map/ppermute | solution.py:305
where the time goes:
time: 189 us
  waiting for transfers between devices  85.7 us (45%)
  Pallas kernels  38.3 us (20%)
  starting transfers between devices  27.6 us (15%)
  other arithmetic  26.6 us (14%)
  local copies, waits for them, and re-layouts  6.87 us (4%)
  matrix products  3.56 us (2%)
    ppermute x1, waiting for transfers between devices, give_back(): odd = lax.ppermute(far, 'ang', back(to_odd))  40.5 us
    pallas_call x2, Pallas kernels, section_chunk(): pl.pallas_call(functools.partial(section_kernel, (fields, planes, rows, r...  35.2 us
    ppermute x1, waiting for transfers between devices, take(): from_even = lax.ppermute(first_half, 'ang', to_even)  21.1 us
    ppermute x1, waiting for transfers between devices, take(): from_odd = lax.ppermute(second_half, 'ang', to_odd)  9.18 us
    another operation x3, other arithmetic, take(): jnp.stack([jnp.where(h == 0, near, far), jnp.where(h == 0, far, near)])  8.16 us
    ppermute x2, waiting for transfers between devices, section(): low = lax.ppermute(qs[-1][:, :, step - 2:], 'ax', up)  6.19 us
    ppermute x2, starting transfers between devices, section(): high = lax.ppermute(qs[0][:, :, :2], 'ax', down)  6.06 us
    ppermute x2, waiting for transfers between devices, section(): high = lax.ppermute(qs[0][:, :, :2], 'ax', down)  6.01 us
  transfers between devices with their start and end apart: 14, of which 8 were waited for; matrix products, arithmetic and copies ran while one was open for 8% of the time, Pallas kernels for 2%

commit v1 on v0

v1 whole, which is shorter than its diff:
```python
import functools
import math

import jax
import jax.numpy as jnp
from jax import lax
from jax.experimental import pallas as pl
from jax.experimental.pallas import tpu as pltpu
from jax.sharding import PartitionSpec as P

gamma_ratio = 1.4
courant = 0.15
highest = lax.Precision.HIGHEST
anywhere = pl.BlockSpec(memory_space=pl.ANY)
scalars = pl.BlockSpec(memory_space=pltpu.SMEM)
vector = pl.BlockSpec(memory_space=pltpu.VMEM)
GROUP = 4


def split_kernel(w_ref, hi_ref, lo_ref):
    w = w_ref[...]
    hi = w.astype(jnp.bfloat16)
    hi_ref[...] = hi
    lo_ref[...] = (w - hi.astype(jnp.float32)).astype(jnp.bfloat16)


def split_weights(w):
    shape = jax.ShapeDtypeStruct(w.shape, jnp.bfloat16)
    return pl.pallas_call(split_kernel, out_shape=(shape, shape), name="split_weights")(w)


def speeds(q):
    rho, mx, my, mz, en = q
    inv = 1.0 / rho
    ux, uy, uz = mx * inv, my * inv, mz * inv
    pressure = (gamma_ratio - 1.0) * (en - 0.5 * (mx * ux + my * uy + mz * uz))
    return ux, uy, uz, pressure, en + pressure


def angular_of(q, state, cos, sin):
    rho, mx, my, mz, en = q
    ux, uy, uz, pressure, enthalpy = state
    us = uy * cos - ux * sin
    return (rho * us, mx * us - pressure * sin, my * us + pressure * cos, mz * us, enthalpy * us)


def radial_of(q, state, cos, sin, scale):
    rho, mx, my, mz, en = q
    ux, uy, uz, pressure, enthalpy = state
    ur = (ux * cos + uy * sin) * scale
    ps = pressure * scale
    return (rho * ur, mx * ur + ps * cos, my * ur + ps * sin, mz * ur, enthalpy * ur)


def axial_of(q, state, scale):
    rho, mx, my, mz, en = q
    ux, uy, uz, pressure, enthalpy = state
    uz = uz * scale
    return (mz * scale, mx * uz, my * uz, mz * uz + pressure * scale, enthalpy * uz)


def merged(sources):
    spans = []
    for array, at in sources:
        if spans and spans[-1][0] == array and spans[-1][1] + spans[-1][2] == at:
            spans[-1][2] += 1
        else:
            spans.append([array, at, 1])
    return spans


def run_copies(copies):
    for copy in copies:
        copy.start()


def wait_copies(copies):
    for copy in copies:
        copy.wait()


def section_kernel(plan, factor, *refs):
    fields, rows, radii = plan["dims"]
    lengths, mixed, final = plan["lengths"], plan["mixed"], plan["final"]
    total = sum(lengths)
    counts = plan["counts"]
    refs = list(refs)
    flags_ref, trig_ref, edge_trig_ref, radius_ref, whi_hbm, wlo_hbm = refs[:6]
    del refs[:6]
    groups = []
    for count in counts:
        groups.append(refs[:count])
        del refs[:count]
    q_in, base_in, left_in, right_in = groups
    outs = refs[: plan["outs"]]
    del refs[: plan["outs"]]
    q_s, base_s, left_s, right_s, whi_s, wlo_s, axial_s, ang_s, hi_s, lo_s, res_s, sems = refs
    lane_halves = radii // 128

    used = [0]

    def copy(src, dst):
        used[0] += 1
        return pltpu.make_async_copy(src, dst, sems.at[used[0] - 1])

    def gathered(spans_of_runs, sources, target):
        made, at = [], 0
        for spans in spans_of_runs:
            for array, start, count in spans:
                source = sources[array]
                if len(source.shape) == 5:
                    made.append(copy(source.at[:, :, start : start + count], target.at[:, :, at : at + count]))
                else:
                    made.append(copy(source.at[:, start : start + count], target.at[:, at : at + count]))
                at += count
        return made

    early = gathered(plan["q"], q_in, q_s)
    early += gathered(plan["left"], left_in, left_s) + gathered(plan["right"], right_in, right_s)
    base_copies = gathered(plan["base"], base_in, base_s) if mixed else []
    weight_copies = [copy(whi_hbm, whi_s), copy(wlo_hbm, wlo_s)]
    run_copies(early)
    run_copies(base_copies)
    run_copies(weight_copies)
    wait_copies(early)
    wait_copies(base_copies)

    axial_scale = (factor / 12.0) * radius_ref[...]
    radial_scale = -factor * radius_ref[...]

    def put(u, f, column, value):
        lanes = slice(column, column + value.shape[-1])
        hi = value.astype(jnp.bfloat16)
        hi_s[u, f, :, lanes] = hi
        lo_s[u, f, :, lanes] = (value - hi.astype(jnp.float32)).astype(jnp.bfloat16)

    def flux(at, u, flag):
        inner = u is not None
        if inner:
            slot = u % 3
            edge = []
            for side, ref in ((0, left_s), (1, right_s)):
                q = tuple(ref[f, u] for f in range(fields))
                edge.append(angular_of(q, speeds(q), edge_trig_ref[0, side], edge_trig_ref[1, side]))
        for s in range(2):
            q = tuple(q_s[s, f, at] for f in range(fields))
            state = speeds(q)
            axial = axial_of(q, state, axial_scale)
            for f in range(fields):
                value = axial[f]
                if flag is not None:
                    value = jnp.where(flags_ref[flag] > 0, value, 0.0)
                axial_s[s, f, at] = value
            if not inner:
                continue
            radial = radial_of(q, state, trig_ref[0, s], trig_ref[1, s], radial_scale)
            for f in range(fields):
                put(u, f, 2 * radii + s * radii, radial[f])
            angular = angular_of(q, state, trig_ref[2, s], trig_ref[3, s])
            for f in range(fields):
                for l in range(lane_halves):
                    lanes = slice(l * 128, l * 128 + 128)
                    ang_s[slot, s, f, l, 8 : 8 + rows] = angular[f][:, lanes]
                    ang_s[slot, s, f, l, 6:8] = edge[0][f][2 * s : 2 * s + 2, lanes]
                    ang_s[slot, s, f, l, 8 + rows : 10 + rows] = edge[1][f][2 * s : 2 * s + 2, lanes]

    def finish(at, u):
        slot = u % 3
        for s in range(2):
            for f in range(fields):
                for l in range(lane_halves):
                    lanes = slice(l * 128, l * 128 + 128)

                    def ang(k):
                        return ang_s[slot, s, f, l, 8 + k : 8 + k + rows]

                    def axi(k):
                        return axial_s[s, f, at + k, :, lanes]

                    near = (ang(1) - ang(-1)) + (axi(1) - axi(-1))
                    far = (ang(2) - ang(-2)) + (axi(2) - axi(-2))
                    own = q_s[s, f, at, :, lanes]
                    if mixed:
                        own = 0.5 * base_s[s, f, u, :, lanes] + 0.5 * own
                    put(u, f, s * radii + l * 128, (own - 8.0 * near) + far)

    half_at = flags_ref[3]
    left_swap, right_swap = flags_ref[2], flags_ref[4]
    out_copies = []

    def multiply(first, count):
        hi = hi_s[first : first + count].reshape(count * fields * rows, 4 * radii)
        lo = lo_s[first : first + count].reshape(count * fields * rows, 4 * radii)
        dot = functools.partial(jnp.dot, preferred_element_type=jnp.float32)
        for s in range(2):
            columns = slice(s * radii, s * radii + radii)
            whi = whi_s[:, columns]
            res = dot(hi, whi) + dot(lo, whi) + dot(hi, wlo_s[:, columns])
            where = jnp.bitwise_xor(half_at, s) if final else s
            for i in range(count):
                for f in range(fields):
                    start = (i * fields + f) * rows
                    res_s[where, f, first + i] = res[start : start + rows]
        if final:
            pieces = [(res_s.at[0], outs[0]), (res_s.at[1], outs[1])]
            for source, target in pieces:
                out_copies.append(
                    copy(source.at[:, first : first + count], target.at[:, first : first + count])
                )
        else:
            out_copies.append(
                copy(res_s.at[:, :, first : first + count], outs[0].at[:, :, first : first + count])
            )
            for i in range(first, first + count):
                for f in range(fields):
                    for ref, flag, start in ((outs[1], left_swap, 0), (outs[2], right_swap, rows - 2)):
                        one = res_s[0, f, i, start : start + 2]
                        two = res_s[1, f, i, start : start + 2]
                        ref[f, i, 0:2] = jnp.where(flag > 0, two, one)
                        ref[f, i, 2:4] = jnp.where(flag > 0, one, two)
        out_copies[-1].start()
        if final:
            out_copies[-2].start()

    base_at, u0, ready, done = 0, 0, 0, 0
    waited = False
    pending = []
    for r, length in enumerate(lengths):
        for t in range(length + 4):
            flag = None
            if plan["low_flag"] == r and t < 2:
                flag = 0
            if plan["high_flag"] == r and t >= length + 2:
                flag = 1
            flux(base_at + t, u0 + t - 2 if 2 <= t < length + 2 else None, flag)
            if t >= 4:
                finish(base_at + t - 2, u0 + t - 4)
                ready += 1
                if ready - done == GROUP or (ready == total and ready > done):
                    pending.append((done, ready - done))
                    done = ready
                    if len(pending) == 2:
                        if not waited:
                            wait_copies(weight_copies)
                            waited = True
                        multiply(*pending.pop(0))
        base_at += length + 4
        u0 += length
    if not waited:
        wait_copies(weight_copies)
    for item in pending:
        multiply(*item)
    if plan["tips"]:
        for target, start in ((outs[3], 0), (outs[4], total - 2)):
            tip = copy(res_s.at[:, :, start : start + 2], target)
            tip.start()
            out_copies.append(tip)
    wait_copies(out_copies)


def section_task(consts, factor, ranges, q_map, base_map, left_map, right_map, flags, planes, dims, name, final, tips):
    fields, rows, radii = dims
    arrays = {}

    def spans(kind, table, lists):
        held = arrays.setdefault(kind, [])
        out = []
        for planes_of_run in lists:
            sources = []
            for p in planes_of_run:
                array, at = table[p]
                index = next((i for i, a in enumerate(held) if a is array), None)
                if index is None:
                    index = len(held)
                    held.append(array)
                sources.append((index, at))
            out.append(merged(sources))
        return out

    wide = [list(range(a - 2, b + 2)) for a, b in ranges]
    tight = [list(range(a, b)) for a, b in ranges]
    mixed = base_map is not None
    plan = dict(
        dims=dims, lengths=[b - a for a, b in ranges], mixed=mixed, final=final, tips=tips,
        low_flag=next((i for i, r in enumerate(ranges) if r[0] == 0), None),
        high_flag=next((i for i, r in enumerate(ranges) if r[1] == planes), None),
        q=spans("q", q_map, wide), base=spans("base", base_map, tight) if mixed else [],
        left=spans("left", left_map, tight), right=spans("right", right_map, tight),
    )
    arrays.setdefault("base", [])
    plan["counts"] = [len(arrays[k]) for k in ("q", "base", "left", "right")]
    total = sum(plan["lengths"])
    spread = total + 4 * len(ranges)
    real = jax.ShapeDtypeStruct
    f32 = jnp.float32
    if final:
        out_shape = [real((fields, total, rows, radii), f32)] * 2
        out_specs = [anywhere] * 2
    else:
        out_shape = [real((2, fields, total, rows, radii), f32)] + [real((fields, total, 4, radii), f32)] * 2
        out_specs = [anywhere, vector, vector]
        if tips:
            out_shape += [real((2, fields, 2, rows, radii), f32)] * 2
            out_specs += [anywhere] * 2
    plan["outs"] = len(out_shape)
    copies = sum(len(s) for k in ("q", "base", "left", "right") for s in plan[k])
    copies += 2 + 2 * (total // GROUP + 2) + 2
    trig, edge_trig, radius, whi, wlo = consts
    operands = [flags, trig, edge_trig, radius, whi, wlo]
    operands += [a for k in ("q", "base", "left", "right") for a in arrays[k]]
    lines = fields * total * rows
    return pl.pallas_call(
        functools.partial(section_kernel, plan, factor),
        out_shape=out_shape,
        in_specs=[scalars, vector, vector, vector] + [anywhere] * (len(operands) - 4),
        out_specs=out_specs,
        scratch_shapes=[
            pltpu.VMEM((2, fields, spread, rows, radii), f32),
            pltpu.VMEM((2, fields, total, rows, radii) if mixed else (8, 128), f32),
            pltpu.VMEM((fields, total, 4, radii), f32),
            pltpu.VMEM((fields, total, 4, radii), f32),
            pltpu.VMEM(whi.shape, jnp.bfloat16),
            pltpu.VMEM(wlo.shape, jnp.bfloat16),
            pltpu.VMEM((2, fields, spread, rows, radii), f32),
            pltpu.VMEM((3, 2, fields, radii // 128, rows + 16, 128), f32),
            pltpu.VMEM((total, fields, rows, 4 * radii), jnp.bfloat16),
            pltpu.VMEM((total, fields, rows, 4 * radii), jnp.bfloat16),
            pltpu.VMEM((2, fields, total, rows, radii), f32),
            pltpu.SemaphoreType.DMA((copies,)),
        ],
        cost_estimate=pl.CostEstimate(
            flops=2 * lines * 4 * radii * 2 * radii * 6, bytes_accessed=8 * lines * radii * 4,
            transcendentals=0,
        ),
        name=name,
    )(*operands)


def gather_kernel(spans, tips, flags_ref, own_ref, even_ref, odd_ref, core_ref, *refs):
    outs, (q_s, sems) = refs[:-2], refs[-2:]
    _, fields, planes, rows, _ = q_s.shape
    c, keeps, h = flags_ref[5], flags_ref[6], flags_ref[3]
    far = q_s.at[1 - h]
    near = q_s.at[h]

    @pl.when(c == 0)
    def _():
        pltpu.make_async_copy(even_ref, far, sems.at[0]).start()

    @pl.when(c != 0)
    def _():
        pltpu.make_async_copy(odd_ref, far, sems.at[0]).start()

    @pl.when(keeps > 0)
    def _():
        lines = pl.ds(pl.multiple_of((1 - c) * rows, rows), rows)
        at = 0
        for i, (start, count) in enumerate(spans):
            pltpu.make_async_copy(
                own_ref.at[:, start : start + count, lines], near.at[:, at : at + count], sems.at[1 + i]
            ).start()
            at += count

    @pl.when(keeps == 0)
    def _():
        at = 0
        for i, (start, count) in enumerate(spans):
            pltpu.make_async_copy(
                core_ref.at[:, at : at + count], near.at[:, at : at + count], sems.at[1 + i]
            ).start()
            at += count

    pltpu.make_async_copy(even_ref, far, sems.at[0]).wait()
    at = 0
    for i, (start, count) in enumerate(spans):
        pltpu.make_async_copy(
            core_ref.at[:, at : at + count], near.at[:, at : at + count], sems.at[1 + i]
        ).wait()
        at += count
    last = 1 + len(spans)
    copies = [pltpu.make_async_copy(q_s, outs[0], sems.at[last])]
    if tips:
        copies.append(pltpu.make_async_copy(q_s.at[:, :, 0:2], outs[3], sems.at[last + 1]))
        copies.append(pltpu.make_async_copy(q_s.at[:, :, planes - 2 : planes], outs[4], sems.at[last + 2]))
    run_copies(copies)

    def edges(p, carry):
        for f in range(fields):
            for ref, flag, start in ((outs[1], flags_ref[2], 0), (outs[2], flags_ref[4], rows - 2)):
                one = q_s[0, f, p, start : start + 2]
                two = q_s[1, f, p, start : start + 2]
                ref[f, p, 0:2] = jnp.where(flag > 0, two, one)
                ref[f, p, 2:4] = jnp.where(flag > 0, one, two)
        return carry

    lax.fori_loop(0, planes, edges, 0)
    wait_copies(copies)


def gather_task(spans, tips, flags, own, even, odd, core, dims, name):
    fields, rows, radii = dims
    planes = sum(count for _, count in spans)
    f32 = jnp.float32
    out_shape = [jax.ShapeDtypeStruct((2, fields, planes, rows, radii), f32)]
    out_shape += [jax.ShapeDtypeStruct((fields, planes, 4, radii), f32)] * 2
    out_specs = [anywhere, vector, vector]
    if tips:
        out_shape += [jax.ShapeDtypeStruct((2, fields, 2, rows, radii), f32)] * 2
        out_specs += [anywhere] * 2
    return pl.pallas_call(
        functools.partial(gather_kernel, spans, tips),
        out_shape=out_shape,
        in_specs=[scalars] + [anywhere] * 4,
        out_specs=out_specs,
        scratch_shapes=[
            pltpu.VMEM((2, fields, planes, rows, radii), f32),
            pltpu.SemaphoreType.DMA((len(spans) + 4,)),
        ],
        cost_estimate=pl.CostEstimate(
            flops=0, bytes_accessed=16 * fields * planes * rows * radii, transcendentals=0
        ),
        name=name,
    )(flags, own, even, odd, core)


def place_kernel(spans, chained, flags_ref, near_ref, even_ref, odd_ref, core_ref, *refs):
    if chained:
        refs = refs[1:]
    out_ref, buf, sems = refs
    _, planes, both, _ = buf.shape
    rows = both // 2
    c, keeps = flags_ref[5], flags_ref[6]
    halves = [buf.at[:, :, :rows], buf.at[:, :, rows:]]

    def start(refs_of_halves):
        for e in range(2):
            pltpu.make_async_copy(refs_of_halves[e], halves[e], sems.at[e]).start()

    @pl.when(keeps == 0)
    def _():
        start([odd_ref, even_ref])

    @pl.when((keeps > 0) & (c == 0))
    def _():
        start([core_ref, near_ref])

    @pl.when((keeps > 0) & (c != 0))
    def _():
        start([near_ref, core_ref])

    for e in range(2):
        pltpu.make_async_copy(near_ref, halves[e], sems.at[e]).wait()
    copies, at = [], 0
    for i, (first, count) in enumerate(spans):
        copies.append(
            pltpu.make_async_copy(
                buf.at[:, at : at + count], out_ref.at[:, first : first + count], sems.at[2 + i]
            )
        )
        at += count
    run_copies(copies)
    wait_copies(copies)


def place_task(spans, flags, near, even, odd, core, whole, shape, name):
    fields, planes, ang_dev, radii = shape
    count = sum(n for _, n in spans)
    operands = [flags, near, even, odd, core] + ([] if whole is None else [whole])
    return pl.pallas_call(
        functools.partial(place_kernel, spans, whole is not None),
        out_shape=jax.ShapeDtypeStruct(shape, jnp.float32),
        in_specs=[scalars] + [anywhere] * (len(operands) - 1),
        out_specs=anywhere,
        scratch_shapes=[
            pltpu.VMEM((fields, count, ang_dev, radii), jnp.float32),
            pltpu.SemaphoreType.DMA((len(spans) + 2,)),
        ],
        input_output_aliases={} if whole is None else {5: 0},
        cost_estimate=pl.CostEstimate(
            flops=0, bytes_accessed=8 * fields * count * ang_dev * radii, transcendentals=0
        ),
        name=name,
    )(*operands)


def folded(matrix, radii):
    tall = jnp.concatenate([matrix[radii:], matrix[:radii][::-1]], axis=0)
    return jnp.concatenate([tall[:, radii:], tall[:, :radii][:, ::-1]], axis=1)


def per_device(conserved, deriv_matrix, filter_matrix):
    n = lax.axis_size("ang")
    count = lax.axis_size("ax")
    fields, planes, ang_dev, radii = conserved.shape
    rows = ang_dev // 2
    dims = (fields, rows, radii)
    half = n // 2
    total = ang_dev * n
    twist = total / (2.0 * math.pi * radii)
    pos = lax.axis_index("ang")
    layer = lax.axis_index("ax")
    h, j, c = pos // half, (pos % half) // 2, pos % 2
    ring = 4 * j + 2 * (h ^ (j & 1)) + 1 - c
    keeps = h == (c ^ (j & 1))

    def dev(hh, jj, cc):
        return hh * half + 2 * jj + cc

    spots = [(hh, jj, cc) for hh in range(2) for jj in range(n // 4) for cc in range(2)]
    givers = [(hh, jj, cc) for hh, jj, cc in spots if hh != (cc ^ (jj & 1))]
    keepers = [(hh, jj, cc) for hh, jj, cc in spots if hh == (cc ^ (jj & 1))]
    to_even = [(dev(*g), dev(1 - g[0], g[1], 0)) for g in givers]
    to_odd = [(dev(*g), dev(1 - g[0], g[1], 1)) for g in givers]
    to_core = [(dev(*k), dev(k[0], k[1], 1 - k[2])) for k in keepers]
    order = [dev((r % 4 // 2) ^ (r // 4 & 1), r // 4, 1 - r % 2) for r in range(n)]
    to_left = [(order[r], order[(r - 1) % n]) for r in range(n)]
    to_right = [(order[r], order[(r + 1) % n]) for r in range(n)]
    up = [(i, i + 1) for i in range(count - 1)]
    down = [(i + 1, i) for i in range(count - 1)]

    def back(table):
        return [(b, a) for a, b in table]

    flags = jnp.stack(
        [layer > 0, layer < count - 1, ring == 0, h == 1, ring == n - 1, c == 1, keeps]
    ).astype(jnp.int32)

    def angles(offsets):
        index = (ring * rows + offsets) % total
        return index.astype(jnp.float32) * (2.0 * math.pi / total)

    seg = jnp.arange(2, dtype=jnp.int32)[:, None] * (total // 2)
    centre = angles(seg + jnp.arange(rows, dtype=jnp.int32))
    left_rows = angles((seg + jnp.arange(-2, 0, dtype=jnp.int32)).reshape(4))
    right_rows = angles((seg + jnp.arange(rows, rows + 2, dtype=jnp.int32)).reshape(4))
    edges = jnp.stack([left_rows, right_rows])

    def spread(values):
        return jnp.broadcast_to(values[..., None], values.shape + (radii,))

    plain = jnp.stack([jnp.cos(centre), jnp.sin(centre)])
    plain_edges = jnp.stack([jnp.cos(edges), jnp.sin(edges)])
    radius = ((jnp.arange(radii, dtype=jnp.int32).astype(jnp.float32) + 0.5) / radii)[None]
    signs = jnp.where(jnp.arange(2 * radii, dtype=jnp.int32) < radii, -1.0, 1.0).astype(jnp.float32)

    outer = planes // 3
    span_outer = ((0, outer), (planes - outer, outer))
    span_inner = ((outer, planes - 2 * outer),)

    def cut(spans):
        parts = [lax.slice_in_dim(conserved, a, a + m, axis=1) for a, m in spans]
        block = parts[0] if len(parts) == 1 else jnp.concatenate(parts, axis=1)
        return block[:, :, :rows], block[:, :, rows:]

    def send(spans):
        first_half, second_half = cut(spans)
        odd = lax.ppermute(first_half, "ang", to_odd)
        even = lax.ppermute(second_half, "ang", to_even)
        core = lax.ppermute(jnp.where(c == 0, first_half, second_half), "ang", to_core)
        return even, odd, core

    def trade(left_edge, right_edge):
        return lax.ppermute(right_edge, "ang", to_right), lax.ppermute(left_edge, "ang", to_left)

    def trade_tips(low_tip, high_tip):
        return lax.ppermute(high_tip, "ax", up), lax.ppermute(low_tip, "ax", down)

    def listed(array, ranges):
        at, table = 0, {}
        for a, b in ranges:
            for p in range(a, b):
                table[p] = (array, at)
                at += 1
        return table

    def tipped(low, high):
        table = {p - 2: (low, p) for p in range(2)}
        table.update({planes + p: (high, p) for p in range(2)})
        return table

    sent_outer = send(span_outer)
    sent_inner = send(span_inner)

    composite = jnp.dot(filter_matrix, signs[:, None] * deriv_matrix, precision=highest)
    weights = jnp.concatenate([folded(filter_matrix, radii).T, folded(composite, radii).T], axis=0)
    whi, wlo = split_weights(weights)

    def consts(weight):
        scale = weight * courant * twist / 12.0
        return (
            spread(jnp.concatenate([plain, scale * plain])), spread(scale * plain_edges), radius, whi, wlo,
        )

    ro = ((0, outer), (planes - outer, planes))
    ri = ((outer, planes - outer),)
    one_o = ((0, outer - 2), (planes - outer + 2, planes))
    one_i = ((outer - 2, planes - outer + 2),)
    two_o = ((0, outer - 4), (planes - outer + 4, planes))
    two_i = ((outer - 4, planes - outer + 4),)

    def section(weight, ranges, maps, base_map, name, final=False, tips=False):
        q_map, left_map, right_map = maps
        return section_task(
            consts(weight), weight * courant, ranges, q_map, base_map, left_map, right_map,
            flags, planes, dims, name, final, tips,
        )

    q_o, left_o, right_o, low_tip, high_tip = gather_task(
        span_outer, True, flags, conserved, *sent_outer, dims, "gather_outer"
    )
    halo_left, halo_right = trade(left_o, right_o)
    low, high = trade_tips(low_tip, high_tip)
    q_map = {**listed(q_o, ro), **tipped(low, high)}
    lefts, rights = listed(halo_left, ro), listed(halo_right, ro)
    f_o, left_f, right_f, low_tip, high_tip = section(
        1.0, one_o, (q_map, lefts, rights), None, "section_one_outer", tips=True
    )
    low, high = trade_tips(low_tip, high_tip)
    f_map = {**listed(f_o, one_o), **tipped(low, high)}
    halo_left, halo_right = trade(left_f, right_f)
    f_lefts, f_rights = listed(halo_left, one_o), listed(halo_right, one_o)

    q_i, left_i, right_i = gather_task(
        span_inner, False, flags, conserved, *sent_inner, dims, "gather_inner"
    )
    halo_left, halo_right = trade(left_i, right_i)
    q_map.update(listed(q_i, ri))
    lefts.update(listed(halo_left, ri))
    rights.update(listed(halo_right, ri))

    near_o, far_o = section(
        0.5, two_o, (f_map, f_lefts, f_rights), q_map, "section_two_outer", final=True
    )

    def give_back(near, far):
        even = lax.ppermute(far, "ang", back(to_even))
        odd = lax.ppermute(far, "ang", back(to_odd))
        core = lax.ppermute(near, "ang", back(to_core))
        return even, odd, core

    back_o = give_back(near_o, far_o)

    f_i, left_f, right_f = section(1.0, one_i, (q_map, lefts, rights), None, "section_one_inner")
    halo_left, halo_right = trade(left_f, right_f)
    f_map.update(listed(f_i, one_i))
    f_lefts.update(listed(halo_left, one_i))
    f_rights.update(listed(halo_right, one_i))
    near_i, far_i = section(
        0.5, two_i, (f_map, f_lefts, f_rights), q_map, "section_two_inner", final=True
    )
    back_i = give_back(near_i, far_i)

    def spans_of(ranges):
        return tuple((a, b - a) for a, b in ranges)

    out = place_task(spans_of(two_o), flags, near_o, *back_o, None, conserved.shape, "place_outer")
    return place_task(spans_of(two_i), flags, near_i, *back_i, out, conserved.shape, "place_inner")


def solution(mesh):
    placed = (P(None, "ax", "ang", None), P(), P())
    return jax.shard_map(
        per_device,
        mesh=mesh,
        in_specs=placed,
        out_specs=P(None, "ax", "ang", None),
        check_vma=False,
    )
```

time: 189 us -> 188 us (level); the launches traced: 189 us -> 186 us
  waiting for transfers between devices: 85.7 us -> 53.9 us
  Pallas kernels: 38.3 us -> 59.1 us
  starting transfers between devices: 27.6 us -> 48.4 us
  other arithmetic: 26.6 us -> 8.19 us
  local copies, waits for them, and re-layouts: 6.87 us -> 11.8 us
    ppermute x11 -> x18, waiting for transfers between devices: 42.5 us -> 17.2 us  [the longest x2 14 us: send(): even = lax.ppermute(second_half, 'ang', to_even)]
    pallas_call x2 -> x8, Pallas kernels: 35.2 us -> 56 us  [the longest x4 40.3 us: section_task(): pl.pallas_call(functools.partial(section_kernel, plan, factor), out_shape...]
    ppermute x11 -> x18, starting transfers between devices: 21.8 us -> 33.9 us  [the longest x4 10.6 us: trade_tips(): return (lax.ppermute(high_tip, 'ax', up), lax.ppermute(low_tip, 'ax', down))]
    another operation x6 -> x0, other arithmetic: 8.83 us -> none  [the longest x3 8.16 us: take(): jnp.stack([jnp.where(h == 0, near, far), jnp.where(h == 0, far, near)])]
    select_n x5 -> x2, other arithmetic: 11.8 us -> 4.85 us  [send(): jnp.where(c == 0, first_half, second_half)]
    ppermute x1 -> x2, waiting for transfers between devices: 40.5 us -> 34.2 us  [give_back(): odd = lax.ppermute(far, 'ang', back(to_odd))]
    ppermute x1 -> x2, starting transfers between devices: 1.92 us -> 7.37 us  [give_back(): odd = lax.ppermute(far, 'ang', back(to_odd))]
    concatenate x5 -> x1, other arithmetic: 3.18 us -> 0.01 us  [consts(): jnp.concatenate([plain, scale * plain])]
  transfers between devices with their start and end apart: 14 -> 24, of which waited for: 8 -> 5; matrix products, arithmetic and copies ran while one was open for 8% -> 9% of each run, Pallas kernels for 2% -> 25%
where the time goes in v1:
time: 188 us; the launch traced here: 186 us
  Pallas kernels  59.1 us (31%)
  waiting for transfers between devices  53.9 us (29%)
  starting transfers between devices  48.4 us (26%)
  local copies, waits for them, and re-layouts  11.8 us (6%)
  other arithmetic  8.19 us (4%)
  matrix products  3.56 us (2%)
    pallas_call x4, Pallas kernels, section_task(): pl.pallas_call(functools.partial(section_kernel, plan, factor), out_shape...  40.3 us
    ppermute x2, waiting for transfers between devices, give_back(): odd = lax.ppermute(far, 'ang', back(to_odd))  34.2 us
    ppermute x2, waiting for transfers between devices, send(): even = lax.ppermute(second_half, 'ang', to_even)  14 us
    ppermute x4, starting transfers between devices, trade_tips(): return (lax.ppermute(high_tip, 'ax', up), lax.ppermute(low_tip, 'ax', down))  10.6 us
    pallas_call x2, Pallas kernels, gather_task(): pl.pallas_call(functools.partial(gather_kernel, spans, tips), out_shape=o...  8.8 us
    ppermute x2, starting transfers between devices, send(): odd = lax.ppermute(first_half, 'ang', to_odd)  7.62 us
    ppermute x2, starting transfers between devices, give_back(): odd = lax.ppermute(far, 'ang', back(to_odd))  7.37 us
    pallas_call x2, Pallas kernels, place_task(): pl.pallas_call(functools.partial(place_kernel, spans, whole is not None),...  6.93 us
  transfers between devices with their start and end apart: 24, of which 5 were waited for; matrix products, arithmetic and copies ran while one was open for 9% of the time, Pallas kernels for 25%

profile of v1, /device:TPU:31, one launch (start us, length us, event | category | flops | bytes accessed | tf_op | source)
XLA Modules:
  0.0 185.8 jit_solution(4678968228721526423)
XLA Ops:
  0.0 2.7 %broadcast_select_fusion.1 = (f32[5,8,16,256]{3,2,1,0:T(8,128)}, f32[5,8,16,256]{3,2,1,0:T(8,128)}, f32[5,8,16,256]{3,2,1,0:T(8,128)}) fusion(pred[]{:T(512)S(6)} %eq.32, f32[5,24,32,256]{3,2,1,0:T(8,128)} %own_ref.3), kind=kLoop, calls=%fused_computation.19 | loop fusion | flops 163840 | bytes 3276801 | tf_op jit(solution)/shard_map/jit(_where)/select_n | solution.py:559
  2.7 1.3 collective-permute-start.9
  4.0 3.5 %collective-permute-start.7 = (f32[5,8,16,256]{3,2,1,0:T(8,128)}, f32[5,8,16,256]{3,2,1,0:T(8,128)}, u32[]{:S(2)}, u32[]{:S(2)}) collective-permute-start(f32[5,8,16,256]{3,2,1,0:T(8,128)} %get-tuple-element.53), channel_id=1, source_target_pairs={{4,16},{8,24},{16,0},{28,8},{5,17},{9,25},{17,1},{29,9},{6,18},{10... | collective-permute-start | bytes 1966088 | tf_op jit(solution)/shard_map/ppermute | solution.py:558
  7.5 1.9 %fusion.22 = (f32[5,8,32,256]{3,2,1,0:T(8,128)S(1)}, f32[5,8,32,256]{3,2,1,0:T(8,128)S(1)}) fusion(f32[5,24,32,256]{3,2,1,0:T(8,128)} %own_ref.3), kind=kLoop, calls=%fused_computation.62 | loop fusion | bytes 5242880 | tf_op jit(solution)/shard_map/slice | solution.py:551
  9.4 2.1 %broadcast_select_fusion = (f32[5,16,16,256]{3,2,1,0:T(8,128)}, f32[5,16,16,256]{3,2,1,0:T(8,128)}, f32[5,16,16,256]{3,2,1,0:T(8,128)}) fusion(pred[]{:T(512)S(6)} %eq.32, f32[5,8,32,256]{3,2,1,0:T(8,128)S(1)} %get-tuple-element.56, f32[5,8,32,256]{3,2,1,0:T(8,128)S(1)} %get-tuple-element.55), kind=kLoop, calls=%fused_computation.13 | loop fusion | flops 983040 | bytes 6553601 | tf_op jit(solution)/shard_map/jit(_where)/select_n | solution.py:559
  11.6 1.3 collective-permute-start.2
  12.9 5.7 %collective-permute-start.1 = (f32[5,16,16,256]{3,2,1,0:T(8,128)}, f32[5,16,16,256]{3,2,1,0:T(8,128)}, u32[]{:S(2)}, u32[]{:S(2)}) collective-permute-start(f32[5,16,16,256]{3,2,1,0:T(8,128)} %get-tuple-element.50), channel_id=1, source_target_pairs={{4,20},{8,28},{16,4},{28,12},{5,21},{9,29},{17,5},{29,13},{6,22},{... | collective-permute-start | bytes 3932168 | tf_op jit(solution)/shard_map/ppermute | solution.py:557
  18.6 2.4 %collective-permute-start = (f32[5,16,16,256]{3,2,1,0:T(8,128)}, f32[5,16,16,256]{3,2,1,0:T(8,128)}, u32[]{:S(2)}, u32[]{:S(2)}) collective-permute-start(f32[5,16,16,256]{3,2,1,0:T(8,128)} %get-tuple-element.51), channel_id=1, source_target_pairs={{4,16},{8,24},{16,0},{28,8},{5,17},{9,25},{17,1},{29,9},{6,18},{10... | collective-permute-start | bytes 3932168 | tf_op jit(solution)/shard_map/ppermute | solution.py:558
  21.0 3.6 %convolution_bitcast_fusion = f32[512,512]{0,1:T(8,128)S(1)} fusion(f32[512,512]{1,0:T(8,128)S(1)} %copy-done, f32[512,512]{1,0:T(8,128)S(1)} %copy-done.3, f32[512]{0:T(512)S(1)} %fusion.5), kind=kOutput, calls=%fused_computation.3 | convolution fusion | flops 1610874880 | bytes 3147776 | tf_op jit(solution)/shard_map/dot_general | solution.py:584
  28.4 1.9 %collective-permute-start.8 = (f32[5,8,16,256]{3,2,1,0:T(8,128)}, f32[5,8,16,256]{3,2,1,0:T(8,128)}, u32[]{:S(2)}, u32[]{:S(2)}) collective-permute-start(f32[5,8,16,256]{3,2,1,0:T(8,128)} %get-tuple-element.54), channel_id=1, source_target_pairs={{4,20},{8,28},{16,4},{28,12},{5,21},{9,29},{17,5},{29,13},{6,22},{... | collective-permute-start | bytes 1966088 | tf_op jit(solution)/shard_map/ppermute | solution.py:557
  30.5 1.5 pad_maximum_fusion.w_ref
  32.2 1.3 collective-permute-done.1.odd_ref
  33.4 14.0 %collective-permute-done.even_ref = f32[5,16,16,256]{3,2,1,0:T(8,128)} collective-permute-done((f32[5,16,16,256]{3,2,1,0:T(8,128)}, f32[5,16,16,256]{3,2,1,0:T(8,128)}, u32[]{:S(2)}, u32[]{:S(2)}) %collective-permute-start) | collective-permute-done | bytes 1310752 | tf_op jit(solution)/shard_map/ppermute | solution.py:558
  47.5 5.0 %gather_outer.1 = (f32[2,5,16,16,256]{4,3,2,1,0:T(8,128)}, f32[5,16,4,256]{3,2,1,0:T(4,128)}, f32[5,16,4,256]{3,2,1,0:T(4,128)}, f32[2,5,2,16,256]{4,3,2,1,0:T(8,128)}, f32[2,5,2,16,256]{4,3,2,1,0:T(8,128)}) custom-call(s32[7]{0:T(128)} %convert_element_type.71.flags_ref.refs_0_, f32[5,24,32,256]{3,2,1,0:T(8,128)} %own_ref.3, ...), custom_call_target="tpu_custom_call" | custom-call | bytes 5242880 | tf_op jit(solution)/shard_map/gather_outer/pallas_call | solution.py:410
  52.5 1.7 collective-permute-start.6
  54.3 1.8 collective-permute-done.8.odd_ref
  56.1 3.8 %gather_inner.1 = (f32[2,5,8,16,256]{4,3,2,1,0:T(8,128)}, f32[5,8,4,256]{3,2,1,0:T(4,128)}, f32[5,8,4,256]{3,2,1,0:T(4,128)}) custom-call(s32[7]{0:T(128)} %convert_element_type.71.flags_ref.refs_0_, f32[5,24,32,256]{3,2,1,0:T(8,128)} %own_ref.3, f32[5,8,16,256]{3,2,1,0:T(8,128)} %collective-permute-done.7.even_ref, ...), custom_call_target="tpu_custom_call" | custom-call | bytes 2621440 | tf_op jit(solution)/shard_map/gather_inner/pallas_call | solution.py:410
  60.0 1.7 collective-permute-start.11
  62.3 3.1 %split_weights.1 = (bf16[1024,512]{1,0:T(8,128)(2,1)}, bf16[1024,512]{1,0:T(8,128)(2,1)}) custom-call(f32[1024,512]{1,0:T(8,128)} %pad_maximum_fusion.w_ref), custom_call_target="tpu_custom_call" | custom-call | tf_op jit(solution)/shard_map/split_weights/pallas_call | solution.py:29
  65.4 1.3 collective-permute-start.3
  66.7 4.0 %collective-permute-start.4 = (f32[2,5,2,16,256]{4,3,2,1,0:T(8,128)S(1)}, f32[2,5,2,16,256]{4,3,2,1,0:T(8,128)S(1)}, u32[]{:S(2)}, u32[]{:S(2)}) collective-permute-start(f32[2,5,2,16,256]{4,3,2,1,0:T(8,128)S(1)} %copy-done.6), channel_id=1, source_target_pairs={{1,0},{2,1},{3,2},{5,4},{6,5},{7,6},{9,8},{10,9},{11,10},{13,12},{... | collective-permute-start | bytes 983048 | tf_op jit(solution)/shard_map/ppermute | solution.py:566
  70.8 0.8 broadcast_in_dim.21.refs_2_
  71.6 0.7 broadcast_in_dim.20.refs_1_
  72.4 9.9 %section_one_inner.1 = (f32[2,5,12,16,256]{4,3,2,1,0:T(8,128)}, f32[5,12,4,256]{3,2,1,0:T(4,128)}, f32[5,12,4,256]{3,2,1,0:T(4,128)}) custom-call(s32[7]{0:T(128)} %convert_element_type.71.flags_ref.refs_0_, f32[4,2,16,256]{3,2,1,0:T(8,128)} %broadcast_in_dim.20.refs_1_, f32[2,2,4,256]{3,2,1,0:T(4,128)} %broadcast_in_dim.21.refs_2_, ...), custom_call_target="tpu_custom_call" | custom-call | flops 6039797760 | bytes 7864320 | tf_op jit(solution)/shard_map/section_one_inner/pallas_call | solution.py:312
  82.3 1.4 collective-permute-start.13
  84.8 0.7 copy-done.11
  85.6 10.5 %section_one_outer.1 = (f32[2,5,12,16,256]{4,3,2,1,0:T(8,128)}, f32[5,12,4,256]{3,2,1,0:T(4,128)}, f32[5,12,4,256]{3,2,1,0:T(4,128)}, f32[2,5,2,16,256]{4,3,2,1,0:T(8,128)}, f32[2,5,2,16,256]{4,3,2,1,0:T(8,128)}) custom-call(s32[7]{0:T(128)} %convert_element_type.71.flags_ref.refs_0_, f32[4,2,16,256]{3,2,1,0:T(8,128)} %broadcast_in_dim.20.refs_1_, ...), custom_call_target="tpu_custom_call" | custom-call | flops 6039797760 | bytes 7864320 | tf_op jit(solution)/shard_map/section_one_outer/pallas_call | solution.py:312
  96.1 0.8 collective-permute-start.12
  96.8 1.0 collective-permute-start.14
  97.9 1.3 collective-permute-start.19
  99.2 4.0 %collective-permute-start.20 = (f32[2,5,2,16,256]{4,3,2,1,0:T(8,128)}, f32[2,5,2,16,256]{4,3,2,1,0:T(8,128)S(1)}, u32[]{:S(2)}, u32[]{:S(2)}) collective-permute-start(f32[2,5,2,16,256]{4,3,2,1,0:T(8,128)} %get-tuple-element.46), channel_id=1, source_target_pairs={{1,0},{2,1},{3,2},{5,4},{6,5},{7,6},{9,8},{10,9},{11,10},{13,12},{... | collective-permute-start | bytes 983048 | tf_op jit(solution)/shard_map/ppermute | solution.py:566
  103.2 0.8 broadcast_in_dim.17.refs_2_
  104.1 0.7 broadcast_in_dim.16.refs_1_
  104.8 11.8 %section_two_inner.1 = (f32[5,16,16,256]{3,2,1,0:T(8,128)}, f32[5,16,16,256]{3,2,1,0:T(8,128)}) custom-call(s32[7]{0:T(128)} %convert_element_type.71.flags_ref.refs_0_, f32[4,2,16,256]{3,2,1,0:T(8,128)} %broadcast_in_dim.16.refs_1_, f32[2,2,4,256]{3,2,1,0:T(4,128)} %broadcast_in_dim.17.refs_2_, f32[1,256]{1,0:T(1,128)} %add_multiply_fusion.refs_3_, ...), custom_call_target="tpu_custom_call" | custom-call | flops 8053063680 | bytes 10485760 | tf_op jit(solution)/shard_map/section_two_inner/pallas_call | solution.py:312
  116.7 0.7 copy-done.10
  117.4 0.7 copy-done.12
  118.1 8.1 %section_two_outer.1 = (f32[5,8,16,256]{3,2,1,0:T(8,128)}, f32[5,8,16,256]{3,2,1,0:T(8,128)}) custom-call(s32[7]{0:T(128)} %convert_element_type.71.flags_ref.refs_0_, f32[4,2,16,256]{3,2,1,0:T(8,128)} %broadcast_in_dim.16.refs_1_, f32[2,2,4,256]{3,2,1,0:T(4,128)} %broadcast_in_dim.17.refs_2_, f32[1,256]{1,0:T(1,128)} %add_multiply_fusion.refs_3_, ...), custom_call_target="tpu_custom_call" | custom-call | flops 4026531840 | bytes 5242880 | tf_op jit(solution)/shard_map/section_two_outer/pallas_call | solution.py:312
  126.2 3.2 %collective-permute-start.23 = (f32[5,8,16,256]{3,2,1,0:T(8,128)}, f32[5,8,16,256]{3,2,1,0:T(8,128)S(1)}, u32[]{:S(2)}, u32[]{:S(2)}) collective-permute-start(f32[5,8,16,256]{3,2,1,0:T(8,128)} %get-tuple-element.47.near_ref), channel_id=1, source_target_pairs={{4,0},{8,12},{16,20},{28,24},{5,1},{9,13},{17,21},{29,25},{6,2},{1... | collective-permute-start | bytes 1966088 | tf_op jit(solution)/shard_map/ppermute | solution.py:638
  129.5 1.4 collective-permute-start.18
  130.9 3.1 %collective-permute-start.17 = (f32[5,16,16,256]{3,2,1,0:T(8,128)}, f32[5,16,16,256]{3,2,1,0:T(8,128)}, u32[]{:S(2)}, u32[]{:S(2)}) collective-permute-start(f32[5,16,16,256]{3,2,1,0:T(8,128)} %get-tuple-element.44), channel_id=1, source_target_pairs={{20,4},{28,8},{4,16},{12,28},{21,5},{29,9},{5,17},{13,29},{22,6},{... | collective-permute-start | bytes 3932168 | tf_op jit(solution)/shard_map/ppermute | solution.py:637
  134.0 1.3 collective-permute-start.16
  135.3 4.3 %collective-permute-start.22 = (f32[5,8,16,256]{3,2,1,0:T(8,128)}, f32[5,8,16,256]{3,2,1,0:T(8,128)}, u32[]{:S(2)}, u32[]{:S(2)}) collective-permute-start(f32[5,8,16,256]{3,2,1,0:T(8,128)} %get-tuple-element.48), channel_id=1, source_target_pairs={{20,4},{28,8},{4,16},{12,28},{21,5},{29,9},{5,17},{13,29},{22,6},{... | collective-permute-start | bytes 1966088 | tf_op jit(solution)/shard_map/ppermute | solution.py:637
  139.6 1.3 collective-permute-start.21
  140.9 34.2 %collective-permute-done.22.odd_ref = f32[5,8,16,256]{3,2,1,0:T(8,128)} collective-permute-done((f32[5,8,16,256]{3,2,1,0:T(8,128)}, f32[5,8,16,256]{3,2,1,0:T(8,128)}, u32[]{:S(2)}, u32[]{:S(2)}) %collective-permute-start.22) | collective-permute-done | bytes 655392 | tf_op jit(solution)/shard_map/ppermute | solution.py:637
  175.0 2.6 %collective-permute-done.21.even_ref = f32[5,8,16,256]{3,2,1,0:T(8,128)} collective-permute-done((f32[5,8,16,256]{3,2,1,0:T(8,128)}, f32[5,8,16,256]{3,2,1,0:T(8,128)}, u32[]{:S(2)}, u32[]{:S(2)}) %collective-permute-start.21) | collective-permute-done | bytes 655392 | tf_op jit(solution)/shard_map/ppermute | solution.py:636
  177.6 3.0 %place_outer.1.refs_0_ = f32[5,24,32,256]{3,2,1,0:T(8,128)} custom-call(s32[7]{0:T(128)} %convert_element_type.71.flags_ref.refs_0_, f32[5,8,16,256]{3,2,1,0:T(8,128)} %get-tuple-element.47.near_ref, f32[5,8,16,256]{3,2,1,0:T(8,128)} %collective-permute-done.21.even_ref, f32[5,8,16,256]{3,2,1,0:T(8,128)} %collective-permute-done.22.odd_ref, ...), custom_call_target="tpu_custom_call" | custom-call | bytes 2621440 | tf_op jit(solution)/shard_map/place_outer/pallas_call | solution.py:469
  180.7 1.0 copy-done.2
  181.7 3.9 %place_inner.1 = f32[5,24,32,256]{3,2,1,0:T(8,128)} custom-call(s32[7]{0:T(128)} %convert_element_type.71.flags_ref.refs_0_, f32[5,16,16,256]{3,2,1,0:T(8,128)} %get-tuple-element.43.near_ref, f32[5,16,16,256]{3,2,1,0:T(8,128)} %collective-permute-done.16.even_ref, ...), custom_call_target="tpu_custom_call", output_to_operand_aliasing={{}: (5, {})} | custom-call | bytes 5242880 | tf_op jit(solution)/shard_map/place_inner/pallas_call | solution.py:469
  (83 shorter events, 6.0 us)
Async XLA Ops:
  2.7 51.5 %collective-permute-start.9 = (f32[5,8,16,256]{3,2,1,0:T(8,128)}, f32[5,8,16,256]{3,2,1,0:T(8,128)}, u32[]{:S(2)}, u32[]{:S(2)}) collective-permute-start(f32[5,8,16,256]{3,2,1,0:T(8,128)} %get-tuple-element.52), channel_id=1, source_target_pairs={{0,4},{12,8},{20,16},{24,28},{1,5},{13,9},{21,17},{25,29},{2,6},{1... | collective-permute-start | bytes 1966088 | tf_op jit(solution)/shard_map/ppermute | solution.py:559
  4.0 50.3 %collective-permute-start.7 = (f32[5,8,16,256]{3,2,1,0:T(8,128)}, f32[5,8,16,256]{3,2,1,0:T(8,128)}, u32[]{:S(2)}, u32[]{:S(2)}) collective-permute-start(f32[5,8,16,256]{3,2,1,0:T(8,128)} %get-tuple-element.53), channel_id=1, source_target_pairs={{4,16},{8,24},{16,0},{28,8},{5,17},{9,25},{17,1},{29,9},{6,18},{10... | collective-permute-start | bytes 1966088 | tf_op jit(solution)/shard_map/ppermute | solution.py:558
  9.4 11.6 %copy-start = (f32[512,512]{1,0:T(8,128)S(1)}, f32[512,512]{1,0:T(8,128)}, u32[]{:S(2)}) copy-start(f32[512,512]{1,0:T(8,128)} %param.5) | copy-start | bytes 3145732
  9.4 11.6 %copy-start.3 = (f32[512,512]{1,0:T(8,128)S(1)}, f32[512,512]{1,0:T(8,128)}, u32[]{:S(2)}) copy-start(f32[512,512]{1,0:T(8,128)} %param.4) | copy-start | bytes 3145732
  11.6 16.8 %collective-permute-start.2 = (f32[5,16,16,256]{3,2,1,0:T(8,128)}, f32[5,16,16,256]{3,2,1,0:T(8,128)}, u32[]{:S(2)}, u32[]{:S(2)}) collective-permute-start(f32[5,16,16,256]{3,2,1,0:T(8,128)} %get-tuple-element.49), channel_id=1, source_target_pairs={{0,4},{12,8},{20,16},{24,28},{1,5},{13,9},{21,17},{25,29},{2,6},{1... | collective-permute-start | bytes 3932168 | tf_op jit(solution)/shard_map/ppermute | solution.py:559
  12.9 20.5 %collective-permute-start.1 = (f32[5,16,16,256]{3,2,1,0:T(8,128)}, f32[5,16,16,256]{3,2,1,0:T(8,128)}, u32[]{:S(2)}, u32[]{:S(2)}) collective-permute-start(f32[5,16,16,256]{3,2,1,0:T(8,128)} %get-tuple-element.50), channel_id=1, source_target_pairs={{4,20},{8,28},{16,4},{28,12},{5,21},{9,29},{17,5},{29,13},{6,22},{... | collective-permute-start | bytes 3932168 | tf_op jit(solution)/shard_map/ppermute | solution.py:557
  18.6 28.9 %collective-permute-start = (f32[5,16,16,256]{3,2,1,0:T(8,128)}, f32[5,16,16,256]{3,2,1,0:T(8,128)}, u32[]{:S(2)}, u32[]{:S(2)}) collective-permute-start(f32[5,16,16,256]{3,2,1,0:T(8,128)} %get-tuple-element.51), channel_id=1, source_target_pairs={{4,16},{8,24},{16,0},{28,8},{5,17},{9,25},{17,1},{29,9},{6,18},{10... | collective-permute-start | bytes 3932168 | tf_op jit(solution)/shard_map/ppermute | solution.py:558
  28.4 27.7 %collective-permute-start.8 = (f32[5,8,16,256]{3,2,1,0:T(8,128)}, f32[5,8,16,256]{3,2,1,0:T(8,128)}, u32[]{:S(2)}, u32[]{:S(2)}) collective-permute-start(f32[5,8,16,256]{3,2,1,0:T(8,128)} %get-tuple-element.54), channel_id=1, source_target_pairs={{4,20},{8,28},{16,4},{28,12},{5,21},{9,29},{17,5},{29,13},{6,22},{... | collective-permute-start | bytes 1966088 | tf_op jit(solution)/shard_map/ppermute | solution.py:557
  52.4 18.3 %collective-permute-start.5 = (f32[5,16,4,256]{3,2,1,0:T(4,128)}, f32[5,16,4,256]{3,2,1,0:T(4,128)S(1)}, u32[]{:S(2)}, u32[]{:S(2)}) collective-permute-start(f32[5,16,4,256]{3,2,1,0:T(4,128)} %get-tuple-element.32), channel_id=1, source_target_pairs={{4,0},{0,20},{20,16},{16,28},{28,24},{24,12},{12,8},{8,4},{5,1},{1... | collective-permute-start | bytes 983048 | tf_op jit(solution)/shard_map/ppermute | solution.py:563
  52.5 18.3 %collective-permute-start.6 = (f32[5,16,4,256]{3,2,1,0:T(4,128)}, f32[5,16,4,256]{3,2,1,0:T(4,128)S(1)}, u32[]{:S(2)}, u32[]{:S(2)}) collective-permute-start(f32[5,16,4,256]{3,2,1,0:T(4,128)} %get-tuple-element.33), channel_id=1, source_target_pairs={{4,8},{0,4},{20,0},{16,20},{28,16},{24,28},{12,24},{8,12},{5,9},{1... | collective-permute-start | bytes 983048 | tf_op jit(solution)/shard_map/ppermute | solution.py:563
  59.9 5.5 %copy-start.8 = (f32[2,5,2,16,256]{4,3,2,1,0:T(8,128)S(1)}, f32[2,5,2,16,256]{4,3,2,1,0:T(8,128)}, u32[]{:S(2)}) copy-start(f32[2,5,2,16,256]{4,3,2,1,0:T(8,128)} %get-tuple-element.29) | copy-start | bytes 983044
  59.9 6.8 %copy-start.6 = (f32[2,5,2,16,256]{4,3,2,1,0:T(8,128)S(1)}, f32[2,5,2,16,256]{4,3,2,1,0:T(8,128)}, u32[]{:S(2)}) copy-start(f32[2,5,2,16,256]{4,3,2,1,0:T(8,128)} %get-tuple-element.31) | copy-start | bytes 983044
  59.9 6.8 %collective-permute-start.10 = (f32[5,8,4,256]{3,2,1,0:T(4,128)}, f32[5,8,4,256]{3,2,1,0:T(4,128)S(1)}, u32[]{:S(2)}, u32[]{:S(2)}) collective-permute-start(f32[5,8,4,256]{3,2,1,0:T(4,128)} %get-tuple-element.36), channel_id=1, source_target_pairs={{4,0},{0,20},{20,16},{16,28},{28,24},{24,12},{12,8},{8,4},{5,1},{1... | collective-permute-start | bytes 491528 | tf_op jit(solution)/shard_map/ppermute | solution.py:563
  60.0 10.7 %collective-permute-start.11 = (f32[5,8,4,256]{3,2,1,0:T(4,128)}, f32[5,8,4,256]{3,2,1,0:T(4,128)S(1)}, u32[]{:S(2)}, u32[]{:S(2)}) collective-permute-start(f32[5,8,4,256]{3,2,1,0:T(4,128)} %get-tuple-element.37), channel_id=1, source_target_pairs={{4,8},{0,4},{20,0},{16,20},{28,16},{24,28},{12,24},{8,12},{5,9},{1... | collective-permute-start | bytes 491528 | tf_op jit(solution)/shard_map/ppermute | solution.py:563
  65.4 18.7 %collective-permute-start.3 = (f32[2,5,2,16,256]{4,3,2,1,0:T(8,128)S(1)}, f32[2,5,2,16,256]{4,3,2,1,0:T(8,128)S(1)}, u32[]{:S(2)}, u32[]{:S(2)}) collective-permute-start(f32[2,5,2,16,256]{4,3,2,1,0:T(8,128)S(1)} %copy-done.8), channel_id=1, source_target_pairs={{0,1},{1,2},{2,3},{4,5},{5,6},{6,7},{8,9},{9,10},{10,11},{12,13},{... | collective-permute-start | bytes 983048 | tf_op jit(solution)/shard_map/ppermute | solution.py:566
  66.7 5.6 %copy-start.17 = (f32[5,8,4,256]{3,2,1,0:T(4,128)}, f32[5,8,4,256]{3,2,1,0:T(4,128)S(1)}, u32[]{:S(2)}) copy-start(f32[5,8,4,256]{3,2,1,0:T(4,128)S(1)} %collective-permute-done.10.refs_9_) | copy-start | bytes 491524
  66.7 17.4 %collective-permute-start.4 = (f32[2,5,2,16,256]{4,3,2,1,0:T(8,128)S(1)}, f32[2,5,2,16,256]{4,3,2,1,0:T(8,128)S(1)}, u32[]{:S(2)}, u32[]{:S(2)}) collective-permute-start(f32[2,5,2,16,256]{4,3,2,1,0:T(8,128)S(1)} %copy-done.6), channel_id=1, source_target_pairs={{1,0},{2,1},{3,2},{5,4},{6,5},{7,6},{9,8},{10,9},{11,10},{13,12},{... | collective-permute-start | bytes 983048 | tf_op jit(solution)/shard_map/ppermute | solution.py:566
  70.8 1.6 copy-start.18
  70.8 1.6 copy-start.5
  70.8 1.6 copy-start.7
  82.3 16.9 %collective-permute-start.13 = (f32[5,12,4,256]{3,2,1,0:T(4,128)}, f32[5,12,4,256]{3,2,1,0:T(4,128)S(1)}, u32[]{:S(2)}, u32[]{:S(2)}) collective-permute-start(f32[5,12,4,256]{3,2,1,0:T(4,128)} %get-tuple-element.40), channel_id=1, source_target_pairs={{4,0},{0,20},{20,16},{16,28},{28,24},{24,12},{12,8},{8,4},{5,1},{1... | collective-permute-start | bytes 737288 | tf_op jit(solution)/shard_map/ppermute | solution.py:563
  83.7 19.5 %collective-permute-start.15 = (f32[5,12,4,256]{3,2,1,0:T(4,128)}, f32[5,12,4,256]{3,2,1,0:T(4,128)S(1)}, u32[]{:S(2)}, u32[]{:S(2)}) collective-permute-start(f32[5,12,4,256]{3,2,1,0:T(4,128)} %get-tuple-element.42), channel_id=1, source_target_pairs={{4,8},{0,4},{20,0},{16,20},{28,16},{24,28},{12,24},{8,12},{5,9},{1... | collective-permute-start | bytes 737288 | tf_op jit(solution)/shard_map/ppermute | solution.py:563
  84.1 0.7 copy-start.9
  84.8 0.7 copy-start.11
  96.1 7.1 %collective-permute-start.12 = (f32[5,12,4,256]{3,2,1,0:T(4,128)}, f32[5,12,4,256]{3,2,1,0:T(4,128)S(1)}, u32[]{:S(2)}, u32[]{:S(2)}) collective-permute-start(f32[5,12,4,256]{3,2,1,0:T(4,128)} %get-tuple-element.39), channel_id=1, source_target_pairs={{4,0},{0,20},{20,16},{16,28},{28,24},{24,12},{12,8},{8,4},{5,1},{1... | collective-permute-start | bytes 737288 | tf_op jit(solution)/shard_map/ppermute | solution.py:563
  96.8 6.4 %collective-permute-start.14 = (f32[5,12,4,256]{3,2,1,0:T(4,128)}, f32[5,12,4,256]{3,2,1,0:T(4,128)S(1)}, u32[]{:S(2)}, u32[]{:S(2)}) collective-permute-start(f32[5,12,4,256]{3,2,1,0:T(4,128)} %get-tuple-element.41), channel_id=1, source_target_pairs={{4,8},{0,4},{20,0},{16,20},{28,16},{24,28},{12,24},{8,12},{5,9},{1... | collective-permute-start | bytes 737288 | tf_op jit(solution)/shard_map/ppermute | solution.py:563
  97.9 18.8 %collective-permute-start.19 = (f32[2,5,2,16,256]{4,3,2,1,0:T(8,128)}, f32[2,5,2,16,256]{4,3,2,1,0:T(8,128)S(1)}, u32[]{:S(2)}, u32[]{:S(2)}) collective-permute-start(f32[2,5,2,16,256]{4,3,2,1,0:T(8,128)} %get-tuple-element.45), channel_id=1, source_target_pairs={{0,1},{1,2},{2,3},{4,5},{5,6},{6,7},{8,9},{9,10},{10,11},{12,13},{... | collective-permute-start | bytes 983048 | tf_op jit(solution)/shard_map/ppermute | solution.py:566
  99.2 5.6 %copy-start.13 = (f32[5,12,4,256]{3,2,1,0:T(4,128)}, f32[5,12,4,256]{3,2,1,0:T(4,128)S(1)}, u32[]{:S(2)}) copy-start(f32[5,12,4,256]{3,2,1,0:T(4,128)S(1)} %collective-permute-done.13.refs_11_) | copy-start | bytes 737284
  99.2 17.5 %collective-permute-start.20 = (f32[2,5,2,16,256]{4,3,2,1,0:T(8,128)}, f32[2,5,2,16,256]{4,3,2,1,0:T(8,128)S(1)}, u32[]{:S(2)}, u32[]{:S(2)}) collective-permute-start(f32[2,5,2,16,256]{4,3,2,1,0:T(8,128)} %get-tuple-element.46), channel_id=1, source_target_pairs={{1,0},{2,1},{3,2},{5,4},{6,5},{7,6},{9,8},{10,9},{11,10},{13,12},{... | collective-permute-start | bytes 983048 | tf_op jit(solution)/shard_map/ppermute | solution.py:566
  103.2 1.6 copy-start.14
  103.2 1.6 copy-start.15
  103.2 1.6 copy-start.16
  116.6 12.8 %copy-start.1 = (f32[5,16,16,256]{3,2,1,0:T(8,128)S(1)}, f32[5,16,16,256]{3,2,1,0:T(8,128)}, u32[]{:S(2)}) copy-start(f32[5,16,16,256]{3,2,1,0:T(8,128)} %get-tuple-element.43.near_ref) | copy-start | bytes 3932164
  116.7 0.8 copy-start.10
  117.4 0.7 copy-start.12
  126.2 13.3 %collective-permute-start.23 = (f32[5,8,16,256]{3,2,1,0:T(8,128)}, f32[5,8,16,256]{3,2,1,0:T(8,128)S(1)}, u32[]{:S(2)}, u32[]{:S(2)}) collective-permute-start(f32[5,8,16,256]{3,2,1,0:T(8,128)} %get-tuple-element.47.near_ref), channel_id=1, source_target_pairs={{4,0},{8,12},{16,20},{28,24},{5,1},{9,13},{17,21},{29,25},{6,2},{1... | collective-permute-start | bytes 1966088 | tf_op jit(solution)/shard_map/ppermute | solution.py:638
  129.5 51.2 %collective-permute-start.18 = (f32[5,16,16,256]{3,2,1,0:T(8,128)S(1)}, f32[5,16,16,256]{3,2,1,0:T(8,128)S(1)}, u32[]{:S(2)}, u32[]{:S(2)}) collective-permute-start(f32[5,16,16,256]{3,2,1,0:T(8,128)S(1)} %copy-done.1), channel_id=1, source_target_pairs={{4,0},{8,12},{16,20},{28,24},{5,1},{9,13},{17,21},{29,25},{6,2},{1... | collective-permute-start | bytes 3932168 | tf_op jit(solution)/shard_map/ppermute | solution.py:638
  130.9 49.8 %collective-permute-start.17 = (f32[5,16,16,256]{3,2,1,0:T(8,128)}, f32[5,16,16,256]{3,2,1,0:T(8,128)}, u32[]{:S(2)}, u32[]{:S(2)}) collective-permute-start(f32[5,16,16,256]{3,2,1,0:T(8,128)} %get-tuple-element.44), channel_id=1, source_target_pairs={{20,4},{28,8},{4,16},{12,28},{21,5},{29,9},{5,17},{13,29},{22,6},{... | collective-permute-start | bytes 3932168 | tf_op jit(solution)/shard_map/ppermute | solution.py:637
  134.0 46.7 %collective-permute-start.16 = (f32[5,16,16,256]{3,2,1,0:T(8,128)}, f32[5,16,16,256]{3,2,1,0:T(8,128)}, u32[]{:S(2)}, u32[]{:S(2)}) collective-permute-start(f32[5,16,16,256]{3,2,1,0:T(8,128)} %get-tuple-element.44), channel_id=1, source_target_pairs={{16,4},{24,8},{0,16},{8,28},{17,5},{25,9},{1,17},{9,29},{18,6},{26... | collective-permute-start | bytes 3932168 | tf_op jit(solution)/shard_map/ppermute | solution.py:636
  135.3 39.8 %collective-permute-start.22 = (f32[5,8,16,256]{3,2,1,0:T(8,128)}, f32[5,8,16,256]{3,2,1,0:T(8,128)}, u32[]{:S(2)}, u32[]{:S(2)}) collective-permute-start(f32[5,8,16,256]{3,2,1,0:T(8,128)} %get-tuple-element.48), channel_id=1, source_target_pairs={{20,4},{28,8},{4,16},{12,28},{21,5},{29,9},{5,17},{13,29},{22,6},{... | collective-permute-start | bytes 1966088 | tf_op jit(solution)/shard_map/ppermute | solution.py:637
  139.6 38.1 %copy-start.4 = (f32[5,8,16,256]{3,2,1,0:T(8,128)}, f32[5,8,16,256]{3,2,1,0:T(8,128)S(1)}, u32[]{:S(2)}) copy-start(f32[5,8,16,256]{3,2,1,0:T(8,128)S(1)} %collective-permute-done.23.core_ref) | copy-start | bytes 1966084
  139.6 38.1 %collective-permute-start.21 = (f32[5,8,16,256]{3,2,1,0:T(8,128)}, f32[5,8,16,256]{3,2,1,0:T(8,128)}, u32[]{:S(2)}, u32[]{:S(2)}) collective-permute-start(f32[5,8,16,256]{3,2,1,0:T(8,128)} %get-tuple-element.48), channel_id=1, source_target_pairs={{16,4},{24,8},{0,16},{8,28},{17,5},{25,9},{1,17},{9,29},{18,6},{26... | collective-permute-start | bytes 1966088 | tf_op jit(solution)/shard_map/ppermute | solution.py:636
  180.7 1.1 copy-start.2

commit v2 on v1

v2 whole, which is shorter than its diff:
```python
import functools
import math

import jax
import jax.numpy as jnp
from jax import lax
from jax.experimental import pallas as pl
from jax.experimental.pallas import tpu as pltpu
from jax.sharding import PartitionSpec as P


gamma_ratio = 1.4
courant = 0.15
anywhere = pl.BlockSpec(memory_space=pl.ANY)
scalars = pl.BlockSpec(memory_space=pltpu.SMEM)
vector = pl.BlockSpec(memory_space=pltpu.VMEM)
GROUP = 4
TAILS = 2


def ready(flags, *early):
    def copy_flags(flags_ref, *refs):
        for i in range(flags_ref.shape[0]):
            refs[-1][i] = flags_ref[i]

    return pl.pallas_call(
        copy_flags, out_shape=jax.ShapeDtypeStruct(flags.shape, flags.dtype),
        in_specs=[scalars] + [anywhere] * len(early), out_specs=scalars, name="ready",
    )(flags, *early)


def split_weights(w):
    high = lax.reduce_precision(w, 8, 7)
    return high.astype(jnp.bfloat16), (w - high).astype(jnp.bfloat16)


_, _, SWAP_LEFT, SWAP_RIGHT, SEG, ODD, HALF = range(7)


def speeds(q):
    rho, mx, my, mz, en = q
    inv = 1.0 / rho
    ux, uy, uz = mx * inv, my * inv, mz * inv
    pressure = (gamma_ratio - 1.0) * (en - 0.5 * (mx * ux + my * uy + mz * uz))
    return ux, uy, uz, pressure, en + pressure


def angular_of(q, state, cos, sin):
    rho, mx, my, mz, _ = q
    ux, uy, _, pressure, enthalpy = state
    us = uy * cos - ux * sin
    return (rho * us, mx * us - pressure * sin, my * us + pressure * cos, mz * us, enthalpy * us)


def radial_of(q, state, cos, sin, scale):
    rho, mx, my, mz, _ = q
    ux, uy, _, pressure, enthalpy = state
    ur = (ux * cos + uy * sin) * scale
    ps = pressure * scale
    return (rho * ur, mx * ur + ps * cos, my * ur + ps * sin, mz * ur, enthalpy * ur)


def axial_of(q, state, scale):
    _, mx, my, mz, _ = q
    _, _, uz, pressure, enthalpy = state
    uz = uz * scale
    return (mz * scale, mx * uz, my * uz, mz * uz + pressure * scale, enthalpy * uz)


def run_copies(copies):
    for copy in copies:
        copy.start()


def wait_copies(copies):
    for copy in copies:
        copy.wait()


def section_kernel(plan, factor, *refs):
    fields, rows, radii = plan["dims"]
    lengths, mixed, final = plan["lengths"], plan["mixed"], plan["final"]
    total = sum(lengths)
    counts = plan["counts"]
    refs = list(refs)
    flags_ref, table_ref, radius_ref, whi_hbm, wlo_hbm = refs[:5]
    del refs[:5]
    groups = []
    for count in counts:
        groups.append(refs[:count])
        del refs[:count]
    q_in, tip_in, base_in, left_in, right_in = groups
    outs = refs[: plan["outs"]]
    del refs[: plan["outs"]]
    q_s, base_s, whi_s, wlo_s, axial_s, ang_s, hi_s, lo_s, res_s, sems = refs
    lane_halves = radii // 128

    used = [0]

    def copy(src, dst):
        used[0] += 1
        return pltpu.make_async_copy(src, dst, sems.at[used[0] - 1])

    seg = flags_ref[SEG]

    def table(k, s):
        row = plan["table"] + (2 * k + s) * rows
        return jnp.concatenate([table_ref[row : row + rows]] * lane_halves, axis=1)

    def edge_table(k, side):
        row = plan["table"] + 8 * rows + (2 * k + side) * 8
        return jnp.concatenate([table_ref[row : row + 4]] * lane_halves, axis=1)

    loads, q_wait, base_wait = [], {}, {}

    def load(source, target, start, at, size):
        if len(source) == 1:
            return [copy(source[0].at[:, :, start : start + size], target.at[:, :, at : at + size])]
        return [
            copy(source[0].at[:, start : start + size], target.at[seg, :, at : at + size]),
            copy(source[1].at[:, start : start + size], target.at[1 - seg, :, at : at + size]),
        ]

    def sources(kind, held):
        held, out = list(held), []
        for width in plan["widths"][kind]:
            out.append(held[:width])
            del held[:width]
        return out

    q_from, base_from = sources("q", q_in), sources("base", base_in)
    for array, start, at, size in plan["q"]:
        q_wait[at] = load(q_from[array], q_s, start, at, size)
        loads += [(at, one) for one in q_wait[at]]
    if mixed:
        for array, start, at, size in plan["base"]:
            base_wait[at] = load(base_from[array], base_s, start, at, size)
            loads += [(at + 4, one) for one in base_wait[at]]
    weight_copies = [copy(whi_hbm, whi_s), copy(wlo_hbm, wlo_s)]
    loads += [(9, one) for one in weight_copies]
    run_copies([one for _, one in sorted(loads, key=lambda item: item[0])])

    axial_scale = (factor / 12.0) * radius_ref[...]
    radial_scale = -factor * radius_ref[...]

    def put(u, f, column, value):
        lanes = slice(column, column + value.shape[-1])
        hi = value.astype(jnp.bfloat16)
        hi_s[u, f, :, lanes] = hi
        lo_s[u, f, :, lanes] = (value - hi.astype(jnp.float32)).astype(jnp.bfloat16)

    def flux(at, u, flag):
        inner = u is not None
        tip = plan["tip"].get(at)
        if at in q_wait:
            wait_copies(q_wait[at])
        if inner:
            slot = u % 3
            edge = []
            for side, (array, start) in ((0, plan["left"][u]), (1, plan["right"][u])):
                ref = (left_in, right_in)[side][array]
                q = tuple(ref[f, start] for f in range(fields))
                edge.append(angular_of(q, speeds(q), edge_table(0, side), edge_table(1, side)))
        for s in range(2):
            if tip is None:
                q = tuple(q_s[s, f, at] for f in range(fields))
            else:
                swap_tip, other_tip = (tip_in[0], tip_in[1]) if tip[0] == "high" else (tip_in[1], tip_in[0])
                q = tuple(
                    jnp.where(flags_ref[ODD] > 0, other_tip[s, f, tip[1]], swap_tip[s, f, tip[1]])
                    for f in range(fields)
                )
            state = speeds(q)
            axial = axial_of(q, state, axial_scale)
            for f in range(fields):
                value = axial[f]
                if flag is not None:
                    value = jnp.where(flags_ref[flag] > 0, value, 0.0)
                axial_s[s, f, at] = value
            if not inner:
                continue
            radial = radial_of(q, state, table(0, s), table(1, s), radial_scale)
            for f in range(fields):
                put(u, f, 2 * radii + s * radii, radial[f])
            angular = angular_of(q, state, table(2, s), table(3, s))
            for f in range(fields):
                for l in range(lane_halves):
                    lanes = slice(l * 128, l * 128 + 128)
                    ang_s[slot, s, f, l, 8 : 8 + rows] = angular[f][:, lanes]
                    ang_s[slot, s, f, l, 6:8] = edge[0][f][2 * s : 2 * s + 2, lanes]
                    ang_s[slot, s, f, l, 8 + rows : 10 + rows] = edge[1][f][2 * s : 2 * s + 2, lanes]

    def finish(at, u):
        slot = u % 3
        if u in base_wait:
            wait_copies(base_wait[u])
        for s in range(2):
            for f in range(fields):
                for l in range(lane_halves):
                    lanes = slice(l * 128, l * 128 + 128)

                    def ang(k):
                        return ang_s[slot, s, f, l, 8 + k : 8 + k + rows]

                    def axi(k):
                        return axial_s[s, f, at + k, :, lanes]

                    near = (ang(1) - ang(-1)) + (axi(1) - axi(-1))
                    far = (ang(2) - ang(-2)) + (axi(2) - axi(-2))
                    own = q_s[s, f, at, :, lanes]
                    if mixed:
                        own = 0.5 * base_s[s, f, u, :, lanes] + 0.5 * own
                    put(u, f, s * radii + l * 128, (own - 8.0 * near) + far)

    left_swap, right_swap = flags_ref[SWAP_LEFT], flags_ref[SWAP_RIGHT]
    out_copies = []

    def multiply(first, count):
        hi = hi_s[first : first + count].reshape(count * fields * rows, 4 * radii)
        lo = lo_s[first : first + count].reshape(count * fields * rows, 4 * radii)
        dot = functools.partial(jnp.dot, preferred_element_type=jnp.float32)
        for s in range(2):
            columns = slice(s * radii, s * radii + radii)
            whi = whi_s[:, columns]
            res = dot(hi, whi) + dot(lo, whi) + dot(hi, wlo_s[:, columns])
            where = jnp.bitwise_xor(seg, s) if final else s
            for i in range(count):
                for f in range(fields):
                    start = (i * fields + f) * rows
                    res_s[where, f, first + i] = res[start : start + rows]
        if final:
            pieces = [(res_s.at[0], outs[0]), (res_s.at[1], outs[1])]
            for source, target in pieces:
                out_copies.append(
                    copy(source.at[:, first : first + count], target.at[:, first : first + count])
                )
        else:
            out_copies.append(
                copy(res_s.at[:, :, first : first + count], outs[0].at[:, :, first : first + count])
            )
            for i in range(first, first + count):
                for f in range(fields):
                    for ref, flag, start in ((outs[1], left_swap, 0), (outs[2], right_swap, rows - 2)):
                        one = res_s[0, f, i, start : start + 2]
                        two = res_s[1, f, i, start : start + 2]
                        ref[f, i, 0:2] = jnp.where(flag > 0, two, one)
                        ref[f, i, 2:4] = jnp.where(flag > 0, one, two)
        out_copies[-1].start()
        if final:
            out_copies[-2].start()

    base_at, u0, ready, done = 0, 0, 0, 0
    waited = False
    pending = []
    for r, length in enumerate(lengths):
        for t in range(length + 4):
            flag = None
            if plan["low_flag"] == r and t < 2:
                flag = 0
            if plan["high_flag"] == r and t >= length + 2:
                flag = 1
            flux(base_at + t, u0 + t - 2 if 2 <= t < length + 2 else None, flag)
            if t >= 4:
                finish(base_at + t - 2, u0 + t - 4)
                ready += 1
                if ready - done == GROUP or (ready == total and ready > done):
                    pending.append((done, ready - done))
                    done = ready
                    if len(pending) == 2:
                        if not waited:
                            wait_copies(weight_copies)
                            waited = True
                        multiply(*pending.pop(0))
        base_at += length + 4
        u0 += length
    if not waited:
        wait_copies(weight_copies)
    for item in pending:
        multiply(*item)
    if plan["tips"]:
        last = jnp.where(flags_ref[ODD] > 0, 0, total - 2)
        for target, start in ((outs[3], last), (outs[4], total - 2 - last)):
            tip = copy(res_s.at[:, :, pl.ds(start, 2)], target)
            tip.start()
            out_copies.append(tip)
    wait_copies(out_copies)


def section_task(consts, factor, ranges, q_map, base_map, left_map, right_map, flags, planes, dims, final, tips):
    fields, rows, radii = dims
    arrays = {kind: [] for kind in ("q", "tip", "base", "left", "right")}

    def index_of(kind, array):
        held = arrays[kind]
        if not any(a is array for a in held):
            held.append(array)
        return next(i for i, a in enumerate(held) if a is array)

    def flat(kind):
        return [one for a in arrays[kind] for one in (a if isinstance(a, tuple) else (a,))]

    def pieces(kind, table, wanted):
        spans = []
        for at, p in enumerate(wanted):
            array, start = table[p]
            index = index_of(kind, array)
            last = spans[-1] if spans else None
            if last and last[0] == index and last[1] + last[3] == start and last[2] + last[3] == at and last[3] < GROUP:
                last[3] += 1
            else:
                spans.append([index, start, at, 1])
        return spans

    table_row = consts[1]
    wide = [p for a, b in ranges for p in range(a - 2, b + 2)]
    tight = [p for a, b in ranges for p in range(a, b)]
    mixed = base_map is not None
    tips_at = {at: p for at, p in enumerate(wide) if p < 0 or p >= planes}
    kept = [(at, p) for at, p in enumerate(wide) if at not in tips_at]
    q_spans = pieces("q", q_map, [p for _, p in kept])
    q_spans = [[i, start, kept[at][0], size] for i, start, at, size in q_spans]
    plan = dict(
        dims=dims, lengths=[b - a for a, b in ranges], mixed=mixed, final=final, tips=tips,
        low_flag=next((i for i, r in enumerate(ranges) if r[0] == 0), None),
        high_flag=next((i for i, r in enumerate(ranges) if r[1] == planes), None),
        q=q_spans, tip={at: ("low" if p < 0 else "high", p + 2 if p < 0 else p - planes) for at, p in tips_at.items()},
        table=table_row,
        base=pieces("base", base_map, tight) if mixed else [],
        left=[(index_of("left", left_map[p][0]), left_map[p][1]) for p in tight],
        right=[(index_of("right", right_map[p][0]), right_map[p][1]) for p in tight],
    )
    kinds = ("q", "tip", "base", "left", "right")
    if tips_at:
        arrays["tip"] = list(q_map["tips"])
    plan["counts"] = [len(flat(k)) for k in kinds]
    plan["widths"] = {k: [len(a) if isinstance(a, tuple) else 1 for a in arrays[k]] for k in ("q", "base")}
    total = sum(plan["lengths"])
    spread = total + 4 * len(ranges)
    real = jax.ShapeDtypeStruct
    f32 = jnp.float32
    if final:
        out_shape = [real((fields, total, rows, radii), f32)] * 2
        out_specs = [anywhere] * 2
    else:
        out_shape = [real((2, fields, total, rows, radii), f32)] + [real((fields, total, 4, radii), f32)] * 2
        out_specs = [anywhere, vector, vector]
        if tips:
            out_shape += [real((2, fields, 2, rows, radii), f32)] * 2
            out_specs += [anywhere] * 2
    plan["outs"] = len(out_shape)
    copies = 2 * len(plan["q"]) + 2 * len(plan["base"]) + 2 + 2 * (total // GROUP + 2) + 2
    table, table_row, radius, whi, wlo = consts
    operands = [flags, table, radius, whi, wlo]
    operands += [a for k in kinds for a in flat(k)]
    places = [scalars, vector, vector, anywhere, anywhere]
    places += [vector if k in ("tip", "left", "right") else anywhere for k in kinds for _ in flat(k)]
    lines = fields * total * rows
    return pl.pallas_call(
        functools.partial(section_kernel, plan, factor),
        out_shape=out_shape,
        in_specs=places,
        out_specs=out_specs,
        scratch_shapes=[
            pltpu.VMEM((2, fields, spread, rows, radii), f32),
            pltpu.VMEM((2, fields, total, rows, radii) if mixed else (8, 128), f32),
            pltpu.VMEM(whi.shape, jnp.bfloat16),
            pltpu.VMEM(wlo.shape, jnp.bfloat16),
            pltpu.VMEM((2, fields, spread, rows, radii), f32),
            pltpu.VMEM((3, 2, fields, radii // 128, rows + 16, 128), f32),
            pltpu.VMEM((total, fields, rows, 4 * radii), jnp.bfloat16),
            pltpu.VMEM((total, fields, rows, 4 * radii), jnp.bfloat16),
            pltpu.VMEM((2, fields, total, rows, radii), f32),
            pltpu.SemaphoreType.DMA((copies,)),
        ],
        cost_estimate=pl.CostEstimate(
            flops=2 * lines * 4 * radii * 2 * radii * 6, bytes_accessed=8 * lines * radii * 4,
            transcendentals=0,
        ),
    )(*operands)


def parts_of(spans):
    parts, at = [], 0
    for start, count in spans:
        for i in range(0, count, GROUP):
            size = min(GROUP, count - i)
            parts.append((start + i, at + i, size))
        at += count
    return parts


def edges_kernel(tips, flags_ref, one_ref, two_ref, *refs):
    outs, (q_s, sems) = refs[:-2], refs[-2:]
    _, fields, planes, rows, _ = q_s.shape
    seg = flags_ref[SEG]
    parts = parts_of(((0, planes),))
    loads = []
    for i, (_, at, size) in enumerate(parts):
        span = slice(at, at + size)
        loads.append(
            [
                pltpu.make_async_copy(one_ref.at[:, span], q_s.at[seg, :, span], sems.at[2 * i]),
                pltpu.make_async_copy(two_ref.at[:, span], q_s.at[1 - seg, :, span], sems.at[2 * i + 1]),
            ]
        )
        run_copies(loads[-1])

    def edges(p, carry):
        for f in range(fields):
            for ref, flag, start in (
                (outs[0], flags_ref[SWAP_LEFT], 0), (outs[1], flags_ref[SWAP_RIGHT], rows - 2)
            ):
                one = q_s[0, f, p, start : start + 2]
                two = q_s[1, f, p, start : start + 2]
                ref[f, p, 0:2] = jnp.where(flag > 0, two, one)
                ref[f, p, 2:4] = jnp.where(flag > 0, one, two)
        return carry

    for i, (_, at, size) in enumerate(parts):
        wait_copies(loads[i])
        lax.fori_loop(at, at + size, edges, 0)
    if tips:
        last = jnp.where(flags_ref[ODD] > 0, 0, planes - 2)
        copies = [
            pltpu.make_async_copy(
                q_s.at[:, :, pl.ds(start, 2)], outs[2 + i], sems.at[2 * len(parts) + i]
            )
            for i, start in enumerate((last, planes - 2 - last))
        ]
        run_copies(copies)
        wait_copies(copies)


def edges_task(tips, flags, one, two, dims):
    fields, rows, radii = dims
    planes = one.shape[1]
    f32 = jnp.float32
    out_shape = [jax.ShapeDtypeStruct((fields, planes, 4, radii), f32)] * 2
    out_specs = [vector, vector]
    if tips:
        out_shape += [jax.ShapeDtypeStruct((2, fields, 2, rows, radii), f32)] * 2
        out_specs += [anywhere] * 2
    return pl.pallas_call(
        functools.partial(edges_kernel, tips),
        out_shape=out_shape,
        in_specs=[scalars] + [anywhere] * 2,
        out_specs=out_specs,
        scratch_shapes=[
            pltpu.VMEM((2, fields, planes, rows, radii), f32),
            pltpu.SemaphoreType.DMA((2 * len(parts_of(((0, planes),))) + 2,)),
        ],
        cost_estimate=pl.CostEstimate(
            flops=0, bytes_accessed=8 * fields * planes * rows * radii, transcendentals=0
        ),
    )(flags, one, two)


def place_kernel(spans, chained, flags_ref, one_ref, two_ref, *refs):
    if chained:
        refs = refs[1:]
    out_ref, buf, sems = refs
    rows = buf.shape[2] // 2
    half = flags_ref[HALF]
    parts = parts_of(spans)
    loads = []
    for i, (_, at, size) in enumerate(parts):
        span = slice(at, at + size)
        loads.append(
            [
                pltpu.make_async_copy(
                    ref.at[:, span],
                    buf.at[:, span, pl.ds(pl.multiple_of(row * rows, rows), rows)], sems.at[2 * i + e],
                )
                for e, (ref, row) in enumerate(((one_ref, half), (two_ref, 1 - half)))
            ]
        )
        run_copies(loads[-1])
    copies = []
    for i, (first, at, size) in enumerate(parts):
        wait_copies(loads[i])
        one = pltpu.make_async_copy(
            buf.at[:, at : at + size], out_ref.at[:, first : first + size], sems.at[2 * len(parts) + i]
        )
        one.start()
        copies.append(one)
    wait_copies(copies)


def place_task(spans, flags, one, two, whole, shape):
    fields, _, ang_dev, radii = shape
    count = sum(n for _, n in spans)
    operands = [flags, one, two] + ([] if whole is None else [whole])
    return pl.pallas_call(
        functools.partial(place_kernel, spans, whole is not None),
        out_shape=jax.ShapeDtypeStruct(shape, jnp.float32),
        in_specs=[scalars] + [anywhere] * (len(operands) - 1),
        out_specs=anywhere,
        scratch_shapes=[
            pltpu.VMEM((fields, count, ang_dev, radii), jnp.float32),
            pltpu.SemaphoreType.DMA((3 * len(parts_of(spans)),)),
        ],
        input_output_aliases={} if whole is None else {3: 0},
        cost_estimate=pl.CostEstimate(
            flops=0, bytes_accessed=8 * fields * count * ang_dev * radii, transcendentals=0
        ),
    )(*operands)


def folded(matrix, radii):
    tall = jnp.concatenate([matrix[radii:], matrix[:radii][::-1]], axis=0)
    return jnp.concatenate([tall[:, radii:], tall[:, :radii][:, ::-1]], axis=1)


def per_device(conserved, deriv_matrix, filter_matrix):
    n = lax.axis_size("ang")
    count = lax.axis_size("ax")
    fields, planes, ang_dev, radii = conserved.shape
    rows = ang_dev // 2
    dims = (fields, rows, radii)
    half = n // 2
    total = ang_dev * n
    twist = total / (2.0 * math.pi * radii)
    pos = lax.axis_index("ang")
    layer = lax.axis_index("ax")
    h, j, c = pos // half, (pos % half) // 2, pos % 2
    ring = 4 * j + 2 * (h ^ (j & 1)) + 1 - c
    keeps = h == (c ^ (j & 1))

    def dev(hh, jj, cc):
        return hh * half + 2 * jj + cc

    cycle, swap = [], []
    for jj in range(n // 4):
        odd = jj & 1
        keeper = [dev(hh, jj, hh ^ odd) for hh in range(2)]
        giver = [dev(hh, jj, 1 - (hh ^ odd)) for hh in range(2)]
        ring_of_four = [giver[0], keeper[1], giver[1], keeper[0]]
        cycle += [(ring_of_four[i], ring_of_four[(i + 1) % 4]) for i in range(4)]
        swap += [(giver[0], giver[1]), (giver[1], giver[0]), (keeper[0], keeper[0]), (keeper[1], keeper[1])]
    order = [dev((r % 4 // 2) ^ (r // 4 & 1), r // 4, 1 - r % 2) for r in range(n)]
    to_left = [(order[r], order[(r - 1) % n]) for r in range(n)]
    to_right = [(order[r], order[(r + 1) % n]) for r in range(n)]

    def layer_swap(first):
        table = {i: i for i in range(count)}
        for i in range(first, count - 1, 2):
            table[i], table[i + 1] = i + 1, i
        return sorted(table.items())

    def back(table):
        return [(b, a) for a, b in table]

    sent_half = h ^ (j & 1)
    flags = jnp.stack(
        [layer > 0, layer < count - 1, ring == 0, ring == n - 1, (h == 1) ^ keeps, layer % 2 == 1, sent_half == 1]
    ).astype(jnp.int32)

    def angles(offsets):
        index = (ring * rows + offsets) % total
        return index.astype(jnp.float32) * (2.0 * math.pi / total)

    seg = jnp.arange(2, dtype=jnp.int32)[:, None] * (total // 2)
    centre = angles(seg + jnp.arange(rows, dtype=jnp.int32))
    left_rows = angles((seg + jnp.arange(-2, 0, dtype=jnp.int32)).reshape(4))
    right_rows = angles((seg + jnp.arange(rows, rows + 2, dtype=jnp.int32)).reshape(4))
    edges = jnp.stack([left_rows, right_rows])

    def trig_rows(weight):
        scale = weight * courant * twist / 12.0
        inner = jnp.stack([jnp.cos(centre), jnp.sin(centre)])
        outer_rows = jnp.pad(scale * jnp.stack([jnp.cos(edges), jnp.sin(edges)]), ((0, 0), (0, 0), (0, 4)))
        return jnp.concatenate([inner.reshape(-1), (scale * inner).reshape(-1), outer_rows.reshape(-1)])

    trig_values = jnp.concatenate([trig_rows(1.0), trig_rows(0.5)])
    table = jnp.broadcast_to(trig_values[:, None], (trig_values.shape[0], 128))
    radius = ((jnp.arange(radii, dtype=jnp.int32).astype(jnp.float32) + 0.5) / radii)[None]
    signs = jnp.where(jnp.arange(2 * radii, dtype=jnp.int32) < radii, -1.0, 1.0).astype(jnp.float32)

    outer = planes // 3
    span_outer = ((0, outer), (planes - outer, outer))
    span_inner = ((outer, planes - 2 * outer),)

    def cut(spans):
        parts = [lax.slice_in_dim(conserved, a, a + m, axis=1) for a, m in spans]
        block = parts[0] if len(parts) == 1 else jnp.concatenate(parts, axis=1)
        return block[:, :, :rows], block[:, :, rows:]

    def send(spans):
        first_half, second_half = cut(spans)
        one = jnp.where(sent_half == 0, first_half, second_half)
        two = jnp.where(sent_half == 0, second_half, first_half)
        return lax.ppermute(one, "ang", cycle), lax.ppermute(two, "ang", swap)

    def trade(left_edge, right_edge):
        left = lax.ppermute(right_edge, "ang", to_right)
        return left, lax.ppermute(left_edge, "ang", to_left)

    def trade_tips(one, two):
        one = lax.ppermute(one, "ax", layer_swap(0))
        return one, lax.ppermute(two, "ax", layer_swap(1))

    def listed(array, ranges):
        at, table = 0, {}
        for a, b in ranges:
            for p in range(a, b):
                table[p] = (array, at)
                at += 1
        return table

    sent_outer = send(span_outer)
    sent_inner = send(span_inner)

    composite = jnp.dot(filter_matrix, signs[:, None] * deriv_matrix, precision=lax.Precision.HIGH)
    weights = jnp.concatenate([folded(filter_matrix, radii).T, folded(composite, radii).T], axis=0)

    whi, wlo = split_weights(weights)
    flags = ready(flags, whi, wlo, table, radius)

    ro = ((0, outer), (planes - outer, planes))
    ri = ((outer, planes - outer),)
    one_o = ((0, outer - 2), (planes - outer + 2, planes))
    one_i = ((outer - 2, planes - outer + 2),)
    two_o = ((0, outer - 4), (planes - outer + 4, planes))
    cuts = [outer - 4 + (planes - 2 * outer + 8) * i // TAILS for i in range(TAILS + 1)]

    def section(weight, ranges, maps, base_map, final=False, tips=False):
        q_map, left_map, right_map = maps
        return section_task(
            (table, 0 if weight == 1.0 else trig_values.shape[0] // 2, radius, whi, wlo), weight * courant, ranges, q_map, base_map, left_map,
            right_map, flags, planes, dims, final, tips,
        )

    left_o, right_o, tip_one, tip_two = edges_task(True, flags, *sent_outer, dims)
    halo_left, halo_right = trade(left_o, right_o)
    q_map = listed(sent_outer, ro)
    q_map["tips"] = trade_tips(tip_one, tip_two)
    lefts, rights = listed(halo_left, ro), listed(halo_right, ro)
    f_o, left_f, right_f, tip_one, tip_two = section(1.0, one_o, (q_map, lefts, rights), None, tips=True)
    halo_left, halo_right = trade(left_f, right_f)
    f_map = listed(f_o, one_o)
    f_map["tips"] = trade_tips(tip_one, tip_two)
    f_lefts, f_rights = listed(halo_left, one_o), listed(halo_right, one_o)

    left_i, right_i = edges_task(False, flags, *sent_inner, dims)
    halo_left, halo_right = trade(left_i, right_i)
    q_map.update(listed(sent_inner, ri))
    lefts.update(listed(halo_left, ri))
    rights.update(listed(halo_right, ri))

    def give_back(one, two):
        one = lax.ppermute(one, "ang", back(cycle))
        return one, lax.ppermute(two, "ang", back(swap))

    backs = []
    near, far = section(0.5, two_o, (f_map, f_lefts, f_rights), q_map, final=True)
    backs.append((two_o, give_back(near, far)))

    f_i, left_f, right_f = section(1.0, one_i, (q_map, lefts, rights), None)
    halo_left, halo_right = trade(left_f, right_f)
    f_map.update(listed(f_i, one_i))
    f_lefts.update(listed(halo_left, one_i))
    f_rights.update(listed(halo_right, one_i))
    for i in range(TAILS):
        ranges = ((cuts[i], cuts[i + 1]),)
        near, far = section(0.5, ranges, (f_map, f_lefts, f_rights), q_map, final=True)
        backs.append((ranges, give_back(near, far)))

    out = None
    for ranges, arrived in backs:
        spans = tuple((a, b - a) for a, b in ranges)
        out = place_task(spans, flags, *arrived, out, conserved.shape)
    return out


def solution(mesh):
    placed = (P(None, "ax", "ang", None), P(), P())

    return jax.shard_map(
        per_device,
        mesh=mesh,
        in_specs=placed,
        out_specs=P(None, "ax", "ang", None),
        check_vma=False,
    )
```

time: 188 us -> 153 us (0.81)
  the two profiles are of different devices: /device:TPU:31 before, /device:TPU:9 now
where the time goes in v2:
time: 153 us; the launch traced here: 151 us
  Pallas kernels  58.8 us (38%)
  starting transfers between devices  45.5 us (30%)
  waiting for transfers between devices  23.6 us (15%)
  local copies, waits for them, and re-layouts  11.4 us (7%)
  other arithmetic  8.05 us (5%)
  matrix products  3.17 us (2%)
    pallas_call x5, Pallas kernels, section_task(): pl.pallas_call(functools.partial(section_kernel, plan, factor), out_shape...  42.1 us
    ppermute x4, starting transfers between devices, send(): return (lax.ppermute(one, 'ang', cycle), lax.ppermute(two, 'ang', swap))  15.6 us
    ppermute x3, waiting for transfers between devices, give_back(): return (one, lax.ppermute(two, 'ang', back(swap)))  12.2 us
    ppermute x4, waiting for transfers between devices, send(): return (lax.ppermute(one, 'ang', cycle), lax.ppermute(two, 'ang', swap))  9.05 us
    ppermute x2, starting transfers between devices, trade_tips(): return (one, lax.ppermute(two, 'ax', layer_swap(1)))  8.96 us
    pallas_call x3, Pallas kernels, place_task(): pl.pallas_call(functools.partial(place_kernel, spans, whole is not None),...  8.53 us
    ppermute x3, starting transfers between devices, give_back(): return (one, lax.ppermute(two, 'ang', back(swap)))  7.87 us
    pallas_call x2, Pallas kernels, edges_task(): pl.pallas_call(functools.partial(edges_kernel, tips), out_shape=out_shape...  6.95 us
  transfers between devices with their start and end apart: 22, of which 6 were waited for; matrix products, arithmetic and copies ran while one was open for 9% of the time, Pallas kernels for 37%

profile of v2, /device:TPU:9, one launch (start us, length us, event | category | flops | bytes accessed | tf_op | source)
XLA Modules:
  0.0 151.3 jit_solution(4101316782479361841)
XLA Ops:
  0.0 1.9 %fusion.22 = (f32[5,8,32,256]{3,2,1,0:T(8,128)S(1)}, f32[5,8,32,256]{3,2,1,0:T(8,128)S(1)}) fusion(f32[5,24,32,256]{3,2,1,0:T(8,128)} %param.3), kind=kLoop, calls=%fused_computation.64 | loop fusion | bytes 5242880 | tf_op jit(solution)/shard_map/slice | solution.py:584
  1.9 1.9 %broadcast_select_fusion = (f32[5,16,16,256]{3,2,1,0:T(8,128)}, f32[5,16,16,256]{3,2,1,0:T(8,128)}) fusion(pred[]{:T(512)S(6)} %eq.39, f32[5,8,32,256]{3,2,1,0:T(8,128)S(1)} %get-tuple-element.48, f32[5,8,32,256]{3,2,1,0:T(8,128)S(1)} %get-tuple-element.47), kind=kLoop, calls=%fused_computation.16 | loop fusion | flops 1638400 | bytes 5242881 | tf_op jit(solution)/shard_map/jit(_where)/select_n | solution.py:591
  3.9 1.2 collective-permute-start
  5.1 3.1 %collective-permute-start.1 = (f32[5,16,16,256]{3,2,1,0:T(8,128)}, f32[5,16,16,256]{3,2,1,0:T(8,128)}, u32[]{:S(2)}, u32[]{:S(2)}) collective-permute-start(f32[5,16,16,256]{3,2,1,0:T(8,128)} %get-tuple-element.49), channel_id=1, source_target_pairs={{4,16},{16,4},{0,0},{20,20},{8,28},{28,8},{12,12},{24,24},{5,17},{... | collective-permute-start | bytes 3932168 | tf_op jit(solution)/shard_map/ppermute | solution.py:592
  8.2 2.6 %slice_select_fusion = (f32[5,8,16,256]{3,2,1,0:T(8,128)}, f32[5,8,16,256]{3,2,1,0:T(8,128)}) fusion(f32[5,24,32,256]{3,2,1,0:T(8,128)} %param.3, pred[]{:T(512)S(6)} %eq.39), kind=kLoop, calls=%fused_computation.18 | loop fusion | flops 327680 | bytes 2621441 | tf_op jit(solution)/shard_map/jit(_where)/select_n | solution.py:591
  10.8 8.9 %collective-permute-start.2 = (f32[5,8,16,256]{3,2,1,0:T(8,128)}, f32[5,8,16,256]{3,2,1,0:T(8,128)}, u32[]{:S(2)}, u32[]{:S(2)}) collective-permute-start(f32[5,8,16,256]{3,2,1,0:T(8,128)} %get-tuple-element.46), channel_id=1, source_target_pairs={{4,20},{20,16},{16,0},{0,4},{8,24},{24,28},{28,12},{12,8},{5,21},{... | collective-permute-start | bytes 1966088 | tf_op jit(solution)/shard_map/ppermute | solution.py:592
  19.7 2.3 %collective-permute-start.3 = (f32[5,8,16,256]{3,2,1,0:T(8,128)}, f32[5,8,16,256]{3,2,1,0:T(8,128)}, u32[]{:S(2)}, u32[]{:S(2)}) collective-permute-start(f32[5,8,16,256]{3,2,1,0:T(8,128)} %get-tuple-element.45), channel_id=1, source_target_pairs={{4,16},{16,4},{0,0},{20,20},{8,28},{28,8},{12,12},{24,24},{5,17},{... | collective-permute-start | bytes 1966088 | tf_op jit(solution)/shard_map/ppermute | solution.py:592
  23.3 0.7 rev.12
  24.4 3.2 %convolution_bitcast_fusion = f32[512,512]{0,1:T(8,128)S(1)} fusion(f32[512,512]{1,0:T(8,128)S(1)} %copy-done, f32[512,512]{1,0:T(8,128)} %param.4, f32[512]{0:T(512)S(1)} %fusion.6), kind=kOutput, calls=%fused_computation.6 | convolution fusion | flops 805568512 | bytes 3147776 | tf_op jit(solution)/shard_map/dot_general | solution.py:613
  27.6 0.7 rev.14
  29.6 0.6 add_multiply_fusion.refs_3_.refs_2_
  30.4 1.7 %fusion = (bf16[1024,512]{1,0:T(8,128)(2,1)}, bf16[1024,512]{1,0:T(8,128)(2,1)}) fusion(f32[512,512]{1,0:T(8,128)S(1)} %get-tuple-element.72, f32[512,512]{1,0:T(8,128)S(1)} %get-tuple-element.71), kind=kLoop, calls=%fused_computation.4 | loop fusion | flops 2621440 | bytes 4194304 | tf_op jit(solution)/shard_map/convert_element_type | solution.py:34
  32.1 0.8 broadcast_in_dim.10.refs_2_.refs_1_
  32.8 1.2 ready.1.flags_ref.refs_0_
  34.0 1.8 %collective-permute-done.1.two_ref.refs_6_.refs_10_.refs_8_.refs_9_ = f32[5,16,16,256]{3,2,1,0:T(8,128)} collective-permute-done((f32[5,16,16,256]{3,2,1,0:T(8,128)}, f32[5,16,16,256]{3,2,1,0:T(8,128)}, u32[]{:S(2)}, u32[]{:S(2)}) %collective-permute-start.1) | collective-permute-done | bytes 1310752 | tf_op jit(solution)/shard_map/ppermute | solution.py:592
  35.8 4.2 %shard_map.37 = (f32[5,16,4,256]{3,2,1,0:T(4,128)}, f32[5,16,4,256]{3,2,1,0:T(4,128)}, f32[2,5,2,16,256]{4,3,2,1,0:T(8,128)}, f32[2,5,2,16,256]{4,3,2,1,0:T(8,128)}) custom-call(s32[7]{0:T(128)} %ready.1.flags_ref.refs_0_, f32[5,16,16,256]{3,2,1,0:T(8,128)} %collective-permute-done.one_ref.refs_5_.refs_9_.refs_7_.refs_8_, ...), custom_call_target="tpu_custom_call" | custom-call | bytes 2621440 | tf_op jit(solution)/shard_map/pallas_call | solution.py:443
  40.0 1.2 collective-permute-start.4
  41.8 4.5 %collective-permute-start.9 = (f32[2,5,2,16,256]{4,3,2,1,0:T(8,128)}, f32[2,5,2,16,256]{4,3,2,1,0:T(8,128)S(1)}, u32[]{:S(2)}, u32[]{:S(2)}) collective-permute-start(f32[2,5,2,16,256]{4,3,2,1,0:T(8,128)} %get-tuple-element.31), channel_id=1, source_target_pairs={{0,0},{1,2},{2,1},{3,3},{4,4},{5,6},{6,5},{7,7},{8,8},{9,10},{10,9... | collective-permute-start | bytes 983048 | tf_op jit(solution)/shard_map/ppermute | solution.py:600
  46.3 7.3 %collective-permute-done.3.two_ref.refs_8_.refs_10_ = f32[5,8,16,256]{3,2,1,0:T(8,128)} collective-permute-done((f32[5,8,16,256]{3,2,1,0:T(8,128)}, f32[5,8,16,256]{3,2,1,0:T(8,128)}, u32[]{:S(2)}, u32[]{:S(2)}) %collective-permute-start.3) | collective-permute-done | bytes 655392 | tf_op jit(solution)/shard_map/ppermute | solution.py:592
  53.5 2.8 %shard_map.38 = (f32[5,8,4,256]{3,2,1,0:T(4,128)}, f32[5,8,4,256]{3,2,1,0:T(4,128)}) custom-call(s32[7]{0:T(128)} %ready.1.flags_ref.refs_0_, f32[5,8,16,256]{3,2,1,0:T(8,128)} %collective-permute-done.2.one_ref.refs_7_.refs_9_, f32[5,8,16,256]{3,2,1,0:T(8,128)} %collective-permute-done.3.two_ref.refs_8_.refs_10_), custom_call_target="tpu_custom_call" | custom-call | bytes 1310720 | tf_op jit(solution)/shard_map/pallas_call | solution.py:443
  56.4 1.7 %collective-permute-start.7 = (f32[5,8,4,256]{3,2,1,0:T(4,128)}, f32[5,8,4,256]{3,2,1,0:T(4,128)S(1)}, u32[]{:S(2)}, u32[]{:S(2)}) collective-permute-start(f32[5,8,4,256]{3,2,1,0:T(4,128)} %get-tuple-element.28), channel_id=1, source_target_pairs={{4,8},{0,4},{20,0},{16,20},{28,16},{24,28},{12,24},{8,12},{5,9},{1... | collective-permute-start | bytes 491528 | tf_op jit(solution)/shard_map/ppermute | solution.py:596
  58.2 0.7 copy-done.7
  59.0 0.7 copy-done.11
  59.7 9.9 %shard_map.40 = (f32[2,5,12,16,256]{4,3,2,1,0:T(8,128)}, f32[5,12,4,256]{3,2,1,0:T(4,128)}, f32[5,12,4,256]{3,2,1,0:T(4,128)}, f32[2,5,2,16,256]{4,3,2,1,0:T(8,128)}, f32[2,5,2,16,256]{4,3,2,1,0:T(8,128)}) custom-call(s32[7]{0:T(128)} %ready.1.flags_ref.refs_0_, f32[320,128]{1,0:T(8,128)} %broadcast_in_dim.10.refs_2_.refs_1_, ...), custom_call_target="tpu_custom_call" | custom-call | flops 6039797760 | bytes 7864320 | tf_op jit(solution)/shard_map/pallas_call | solution.py:358
  69.7 1.7 %collective-permute-start.13 = (f32[5,12,4,256]{3,2,1,0:T(4,128)}, f32[5,12,4,256]{3,2,1,0:T(4,128)S(1)}, u32[]{:S(2)}, u32[]{:S(2)}) collective-permute-start(f32[5,12,4,256]{3,2,1,0:T(4,128)} %get-tuple-element.36), channel_id=1, source_target_pairs={{4,8},{0,4},{20,0},{16,20},{28,16},{24,28},{12,24},{8,12},{5,9},{1... | collective-permute-start | bytes 737288 | tf_op jit(solution)/shard_map/ppermute | solution.py:596
  71.4 4.5 %collective-permute-start.19 = (f32[2,5,2,16,256]{4,3,2,1,0:T(8,128)}, f32[2,5,2,16,256]{4,3,2,1,0:T(8,128)S(1)}, u32[]{:S(2)}, u32[]{:S(2)}) collective-permute-start(f32[2,5,2,16,256]{4,3,2,1,0:T(8,128)} %get-tuple-element.42), channel_id=1, source_target_pairs={{0,0},{1,2},{2,1},{3,3},{4,4},{5,6},{6,5},{7,7},{8,8},{9,10},{10,9... | collective-permute-start | bytes 983048 | tf_op jit(solution)/shard_map/ppermute | solution.py:600
  76.0 0.7 copy-done.17
  76.6 9.6 %shard_map.39 = (f32[2,5,12,16,256]{4,3,2,1,0:T(8,128)}, f32[5,12,4,256]{3,2,1,0:T(4,128)}, f32[5,12,4,256]{3,2,1,0:T(4,128)}) custom-call(s32[7]{0:T(128)} %ready.1.flags_ref.refs_0_, f32[320,128]{1,0:T(8,128)} %broadcast_in_dim.10.refs_2_.refs_1_, f32[1,256]{1,0:T(1,128)} %add_multiply_fusion.refs_3_.refs_2_, ...), custom_call_target="tpu_custom_call" | custom-call | flops 6039797760 | bytes 7864320 | tf_op jit(solution)/shard_map/pallas_call | solution.py:358
  86.3 1.7 %collective-permute-start.12 = (f32[5,12,4,256]{3,2,1,0:T(4,128)}, f32[5,12,4,256]{3,2,1,0:T(4,128)S(1)}, u32[]{:S(2)}, u32[]{:S(2)}) collective-permute-start(f32[5,12,4,256]{3,2,1,0:T(4,128)} %get-tuple-element.35), channel_id=1, source_target_pairs={{4,8},{0,4},{20,0},{16,20},{28,16},{24,28},{12,24},{8,12},{5,9},{1... | collective-permute-start | bytes 737288 | tf_op jit(solution)/shard_map/ppermute | solution.py:596
  88.1 0.7 copy-done.13
  89.0 7.9 %shard_map.43 = (f32[5,8,16,256]{3,2,1,0:T(8,128)}, f32[5,8,16,256]{3,2,1,0:T(8,128)}) custom-call(s32[7]{0:T(128)} %ready.1.flags_ref.refs_0_, f32[320,128]{1,0:T(8,128)} %broadcast_in_dim.10.refs_2_.refs_1_, f32[1,256]{1,0:T(1,128)} %add_multiply_fusion.refs_3_.refs_2_, bf16[1024,512]{1,0:T(8,128)(2,1)} %get-tuple-element.52.refs_0_.refs_3_, ...), custom_call_target="tpu_custom_call" | custom-call | flops 4026531840 | bytes 5242880 | tf_op jit(solution)/shard_map/pallas_call | solution.py:358
  97.0 0.7 copy-done.14
  97.8 7.4 %shard_map.41 = (f32[5,8,16,256]{3,2,1,0:T(8,128)}, f32[5,8,16,256]{3,2,1,0:T(8,128)}) custom-call(s32[7]{0:T(128)} %ready.1.flags_ref.refs_0_, f32[320,128]{1,0:T(8,128)} %broadcast_in_dim.10.refs_2_.refs_1_, f32[1,256]{1,0:T(1,128)} %add_multiply_fusion.refs_3_.refs_2_, bf16[1024,512]{1,0:T(8,128)(2,1)} %get-tuple-element.52.refs_0_.refs_3_, ...), custom_call_target="tpu_custom_call" | custom-call | flops 4026531840 | bytes 5242880 | tf_op jit(solution)/shard_map/pallas_call | solution.py:358
  105.2 1.7 %collective-permute-start.14 = (f32[5,8,16,256]{3,2,1,0:T(8,128)}, f32[5,8,16,256]{3,2,1,0:T(8,128)S(1)}, u32[]{:S(2)}, u32[]{:S(2)}) collective-permute-start(f32[5,8,16,256]{3,2,1,0:T(8,128)} %get-tuple-element.37), channel_id=1, source_target_pairs={{20,4},{16,20},{0,16},{4,0},{24,8},{28,24},{12,28},{8,12},{21,5},{... | collective-permute-start | bytes 1966088 | tf_op jit(solution)/shard_map/ppermute | solution.py:651
  106.9 7.3 %shard_map.42 = (f32[5,8,16,256]{3,2,1,0:T(8,128)}, f32[5,8,16,256]{3,2,1,0:T(8,128)}) custom-call(s32[7]{0:T(128)} %ready.1.flags_ref.refs_0_, f32[320,128]{1,0:T(8,128)} %broadcast_in_dim.10.refs_2_.refs_1_, f32[1,256]{1,0:T(1,128)} %add_multiply_fusion.refs_3_.refs_2_, bf16[1024,512]{1,0:T(8,128)(2,1)} %get-tuple-element.52.refs_0_.refs_3_, ...), custom_call_target="tpu_custom_call" | custom-call | flops 4026531840 | bytes 5242880 | tf_op jit(solution)/shard_map/pallas_call | solution.py:358
  114.2 2.3 %collective-permute-start.21 = (f32[5,8,16,256]{3,2,1,0:T(8,128)}, f32[5,8,16,256]{3,2,1,0:T(8,128)}, u32[]{:S(2)}, u32[]{:S(2)}) collective-permute-start(f32[5,8,16,256]{3,2,1,0:T(8,128)} %get-tuple-element.44), channel_id=1, source_target_pairs={{16,4},{4,16},{0,0},{20,20},{28,8},{8,28},{12,12},{24,24},{17,5},{... | collective-permute-start | bytes 1966088 | tf_op jit(solution)/shard_map/ppermute | solution.py:652
  116.6 4.2 %collective-permute-start.16 = (f32[5,8,16,256]{3,2,1,0:T(8,128)}, f32[5,8,16,256]{3,2,1,0:T(8,128)S(1)}, u32[]{:S(2)}, u32[]{:S(2)}) collective-permute-start(f32[5,8,16,256]{3,2,1,0:T(8,128)} %get-tuple-element.39), channel_id=1, source_target_pairs={{20,4},{16,20},{0,16},{4,0},{24,8},{28,24},{12,28},{8,12},{21,5},{... | collective-permute-start | bytes 1966088 | tf_op jit(solution)/shard_map/ppermute | solution.py:651
  120.8 2.3 %collective-permute-start.17 = (f32[5,8,16,256]{3,2,1,0:T(8,128)}, f32[5,8,16,256]{3,2,1,0:T(8,128)S(1)}, u32[]{:S(2)}, u32[]{:S(2)}) collective-permute-start(f32[5,8,16,256]{3,2,1,0:T(8,128)} %get-tuple-element.40), channel_id=1, source_target_pairs={{16,4},{4,16},{0,0},{20,20},{28,8},{8,28},{12,12},{24,24},{17,5},{... | collective-permute-start | bytes 1966088 | tf_op jit(solution)/shard_map/ppermute | solution.py:652
  123.1 3.2 %collective-permute-start.15 = (f32[5,8,16,256]{3,2,1,0:T(8,128)}, f32[5,8,16,256]{3,2,1,0:T(8,128)S(1)}, u32[]{:S(2)}, u32[]{:S(2)}) collective-permute-start(f32[5,8,16,256]{3,2,1,0:T(8,128)} %get-tuple-element.38), channel_id=1, source_target_pairs={{16,4},{4,16},{0,0},{20,20},{28,8},{8,28},{12,12},{24,24},{17,5},{... | collective-permute-start | bytes 1966088 | tf_op jit(solution)/shard_map/ppermute | solution.py:652
  126.3 4.5 %collective-permute-done.21.two_ref = f32[5,8,16,256]{3,2,1,0:T(8,128)} collective-permute-done((f32[5,8,16,256]{3,2,1,0:T(8,128)}, f32[5,8,16,256]{3,2,1,0:T(8,128)}, u32[]{:S(2)}, u32[]{:S(2)}) %collective-permute-start.21) | collective-permute-done | bytes 655392 | tf_op jit(solution)/shard_map/ppermute | solution.py:652
  130.9 2.8 %shard_map.44.refs_0_ = f32[5,24,32,256]{3,2,1,0:T(8,128)} custom-call(s32[7]{0:T(128)} %ready.1.flags_ref.refs_0_, f32[5,8,16,256]{3,2,1,0:T(8,128)} %copy-done.5, f32[5,8,16,256]{3,2,1,0:T(8,128)} %collective-permute-done.21.two_ref), custom_call_target="tpu_custom_call" | custom-call | bytes 2621440 | tf_op jit(solution)/shard_map/pallas_call | solution.py:493
  133.7 2.3 %collective-permute-done.16.one_ref = f32[5,8,16,256]{3,2,1,0:T(8,128)S(1)} collective-permute-done((f32[5,8,16,256]{3,2,1,0:T(8,128)}, f32[5,8,16,256]{3,2,1,0:T(8,128)S(1)}, u32[]{:S(2)}, u32[]{:S(2)}) %collective-permute-start.16) | collective-permute-done | bytes 655392 | tf_op jit(solution)/shard_map/ppermute | solution.py:651
  136.0 4.4 %collective-permute-done.17.two_ref = f32[5,8,16,256]{3,2,1,0:T(8,128)S(1)} collective-permute-done((f32[5,8,16,256]{3,2,1,0:T(8,128)}, f32[5,8,16,256]{3,2,1,0:T(8,128)S(1)}, u32[]{:S(2)}, u32[]{:S(2)}) %collective-permute-start.17) | collective-permute-done | bytes 655392 | tf_op jit(solution)/shard_map/ppermute | solution.py:652
  140.4 0.8 copy-done.4
  141.2 2.8 %shard_map.45.refs_0_ = f32[5,24,32,256]{3,2,1,0:T(8,128)} custom-call(s32[7]{0:T(128)} %ready.1.flags_ref.refs_0_, f32[5,8,16,256]{3,2,1,0:T(8,128)} %copy-done.2, f32[5,8,16,256]{3,2,1,0:T(8,128)} %copy-done.4, f32[5,24,32,256]{3,2,1,0:T(8,128)} %shard_map.44.refs_0_), custom_call_target="tpu_custom_call", output_to_operand_aliasing={{}: (3, {})} | custom-call | bytes 2621440 | tf_op jit(solution)/shard_map/pallas_call | solution.py:493
  144.1 3.3 %collective-permute-done.15.two_ref = f32[5,8,16,256]{3,2,1,0:T(8,128)S(1)} collective-permute-done((f32[5,8,16,256]{3,2,1,0:T(8,128)}, f32[5,8,16,256]{3,2,1,0:T(8,128)S(1)}, u32[]{:S(2)}, u32[]{:S(2)}) %collective-permute-start.15) | collective-permute-done | bytes 655392 | tf_op jit(solution)/shard_map/ppermute | solution.py:652
  147.4 0.8 copy-done.3
  148.3 2.8 %shard_map.46 = f32[5,24,32,256]{3,2,1,0:T(8,128)} custom-call(s32[7]{0:T(128)} %ready.1.flags_ref.refs_0_, f32[5,8,16,256]{3,2,1,0:T(8,128)} %copy-done.1, f32[5,8,16,256]{3,2,1,0:T(8,128)} %copy-done.3, f32[5,24,32,256]{3,2,1,0:T(8,128)} %shard_map.45.refs_0_), custom_call_target="tpu_custom_call", output_to_operand_aliasing={{}: (3, {})} | custom-call | bytes 2621440 | tf_op jit(solution)/shard_map/pallas_call | solution.py:493
  (82 shorter events, 4.3 us)
Async XLA Ops:
  3.9 30.2 %collective-permute-start = (f32[5,16,16,256]{3,2,1,0:T(8,128)}, f32[5,16,16,256]{3,2,1,0:T(8,128)}, u32[]{:S(2)}, u32[]{:S(2)}) collective-permute-start(f32[5,16,16,256]{3,2,1,0:T(8,128)} %get-tuple-element.50), channel_id=1, source_target_pairs={{4,20},{20,16},{16,0},{0,4},{8,24},{24,28},{28,12},{12,8},{5,21},{... | collective-permute-start | bytes 3932168 | tf_op jit(solution)/shard_map/ppermute | solution.py:592
  5.1 17.7 %copy-start = (f32[512,512]{1,0:T(8,128)S(1)}, f32[512,512]{1,0:T(8,128)}, u32[]{:S(2)}) copy-start(f32[512,512]{1,0:T(8,128)} %param.5) | copy-start | bytes 3145732
  5.1 30.7 %collective-permute-start.1 = (f32[5,16,16,256]{3,2,1,0:T(8,128)}, f32[5,16,16,256]{3,2,1,0:T(8,128)}, u32[]{:S(2)}, u32[]{:S(2)}) collective-permute-start(f32[5,16,16,256]{3,2,1,0:T(8,128)} %get-tuple-element.49), channel_id=1, source_target_pairs={{4,16},{16,4},{0,0},{20,20},{8,28},{28,8},{12,12},{24,24},{5,17},{... | collective-permute-start | bytes 3932168 | tf_op jit(solution)/shard_map/ppermute | solution.py:592
  10.8 31.0 %collective-permute-start.2 = (f32[5,8,16,256]{3,2,1,0:T(8,128)}, f32[5,8,16,256]{3,2,1,0:T(8,128)}, u32[]{:S(2)}, u32[]{:S(2)}) collective-permute-start(f32[5,8,16,256]{3,2,1,0:T(8,128)} %get-tuple-element.46), channel_id=1, source_target_pairs={{4,20},{20,16},{16,0},{0,4},{8,24},{24,28},{28,12},{12,8},{5,21},{... | collective-permute-start | bytes 1966088 | tf_op jit(solution)/shard_map/ppermute | solution.py:592
  19.7 33.8 %collective-permute-start.3 = (f32[5,8,16,256]{3,2,1,0:T(8,128)}, f32[5,8,16,256]{3,2,1,0:T(8,128)}, u32[]{:S(2)}, u32[]{:S(2)}) collective-permute-start(f32[5,8,16,256]{3,2,1,0:T(8,128)} %get-tuple-element.45), channel_id=1, source_target_pairs={{4,16},{16,4},{0,0},{20,20},{8,28},{28,8},{12,12},{24,24},{5,17},{... | collective-permute-start | bytes 1966088 | tf_op jit(solution)/shard_map/ppermute | solution.py:592
  40.0 16.4 %collective-permute-start.4 = (f32[5,16,4,256]{3,2,1,0:T(4,128)}, f32[5,16,4,256]{3,2,1,0:T(4,128)S(1)}, u32[]{:S(2)}, u32[]{:S(2)}) collective-permute-start(f32[5,16,4,256]{3,2,1,0:T(4,128)} %get-tuple-element.25), channel_id=1, source_target_pairs={{4,0},{0,20},{20,16},{16,28},{28,24},{24,12},{12,8},{8,4},{5,1},{1... | collective-permute-start | bytes 983048 | tf_op jit(solution)/shard_map/ppermute | solution.py:595
  41.2 16.9 %collective-permute-start.6 = (f32[5,16,4,256]{3,2,1,0:T(4,128)}, f32[5,16,4,256]{3,2,1,0:T(4,128)S(1)}, u32[]{:S(2)}, u32[]{:S(2)}) collective-permute-start(f32[5,16,4,256]{3,2,1,0:T(4,128)} %get-tuple-element.27), channel_id=1, source_target_pairs={{4,8},{0,4},{20,0},{16,20},{28,16},{24,28},{12,24},{8,12},{5,9},{1... | collective-permute-start | bytes 983048 | tf_op jit(solution)/shard_map/ppermute | solution.py:596
  41.8 16.4 %collective-permute-start.8 = (f32[2,5,2,16,256]{4,3,2,1,0:T(8,128)}, f32[2,5,2,16,256]{4,3,2,1,0:T(8,128)S(1)}, u32[]{:S(2)}, u32[]{:S(2)}) collective-permute-start(f32[2,5,2,16,256]{4,3,2,1,0:T(8,128)} %get-tuple-element.30), channel_id=1, source_target_pairs={{0,1},{1,0},{2,3},{3,2},{4,5},{5,4},{6,7},{7,6},{8,9},{9,8},{10,11... | collective-permute-start | bytes 983048 | tf_op jit(solution)/shard_map/ppermute | solution.py:599
  41.8 16.4 %collective-permute-start.9 = (f32[2,5,2,16,256]{4,3,2,1,0:T(8,128)}, f32[2,5,2,16,256]{4,3,2,1,0:T(8,128)S(1)}, u32[]{:S(2)}, u32[]{:S(2)}) collective-permute-start(f32[2,5,2,16,256]{4,3,2,1,0:T(8,128)} %get-tuple-element.31), channel_id=1, source_target_pairs={{0,0},{1,2},{2,1},{3,3},{4,4},{5,6},{6,5},{7,7},{8,8},{9,10},{10,9... | collective-permute-start | bytes 983048 | tf_op jit(solution)/shard_map/ppermute | solution.py:600
  56.3 15.1 %collective-permute-start.5 = (f32[5,8,4,256]{3,2,1,0:T(4,128)}, f32[5,8,4,256]{3,2,1,0:T(4,128)S(1)}, u32[]{:S(2)}, u32[]{:S(2)}) collective-permute-start(f32[5,8,4,256]{3,2,1,0:T(4,128)} %get-tuple-element.26), channel_id=1, source_target_pairs={{4,0},{0,20},{20,16},{16,28},{28,24},{24,12},{12,8},{8,4},{5,1},{1... | collective-permute-start | bytes 491528 | tf_op jit(solution)/shard_map/ppermute | solution.py:595
  56.4 1.8 %copy-start.6 = (f32[5,16,4,256]{3,2,1,0:T(4,128)}, f32[5,16,4,256]{3,2,1,0:T(4,128)S(1)}, u32[]{:S(2)}) copy-start(f32[5,16,4,256]{3,2,1,0:T(4,128)S(1)} %collective-permute-done.4.refs_9_) | copy-start | bytes 983044
  56.4 19.5 %collective-permute-start.7 = (f32[5,8,4,256]{3,2,1,0:T(4,128)}, f32[5,8,4,256]{3,2,1,0:T(4,128)S(1)}, u32[]{:S(2)}, u32[]{:S(2)}) collective-permute-start(f32[5,8,4,256]{3,2,1,0:T(4,128)} %get-tuple-element.28), channel_id=1, source_target_pairs={{4,8},{0,4},{20,0},{16,20},{28,16},{24,28},{12,24},{8,12},{5,9},{1... | collective-permute-start | bytes 491528 | tf_op jit(solution)/shard_map/ppermute | solution.py:596
  58.2 0.7 copy-start.7
  58.2 0.8 copy-start.9
  59.0 0.7 copy-start.11
  69.6 16.7 %collective-permute-start.11 = (f32[5,12,4,256]{3,2,1,0:T(4,128)}, f32[5,12,4,256]{3,2,1,0:T(4,128)S(1)}, u32[]{:S(2)}, u32[]{:S(2)}) collective-permute-start(f32[5,12,4,256]{3,2,1,0:T(4,128)} %get-tuple-element.34), channel_id=1, source_target_pairs={{4,0},{0,20},{20,16},{16,28},{28,24},{24,12},{12,8},{8,4},{5,1},{1... | collective-permute-start | bytes 737288 | tf_op jit(solution)/shard_map/ppermute | solution.py:595
  69.7 18.3 %collective-permute-start.13 = (f32[5,12,4,256]{3,2,1,0:T(4,128)}, f32[5,12,4,256]{3,2,1,0:T(4,128)S(1)}, u32[]{:S(2)}, u32[]{:S(2)}) collective-permute-start(f32[5,12,4,256]{3,2,1,0:T(4,128)} %get-tuple-element.36), channel_id=1, source_target_pairs={{4,8},{0,4},{20,0},{16,20},{28,16},{24,28},{12,24},{8,12},{5,9},{1... | collective-permute-start | bytes 737288 | tf_op jit(solution)/shard_map/ppermute | solution.py:596
  71.4 16.6 %collective-permute-start.18 = (f32[2,5,2,16,256]{4,3,2,1,0:T(8,128)}, f32[2,5,2,16,256]{4,3,2,1,0:T(8,128)S(1)}, u32[]{:S(2)}, u32[]{:S(2)}) collective-permute-start(f32[2,5,2,16,256]{4,3,2,1,0:T(8,128)} %get-tuple-element.41), channel_id=1, source_target_pairs={{0,1},{1,0},{2,3},{3,2},{4,5},{5,4},{6,7},{7,6},{8,9},{9,8},{10,11... | collective-permute-start | bytes 983048 | tf_op jit(solution)/shard_map/ppermute | solution.py:599
  71.4 4.5 %copy-start.16 = (f32[5,8,4,256]{3,2,1,0:T(4,128)}, f32[5,8,4,256]{3,2,1,0:T(4,128)S(1)}, u32[]{:S(2)}) copy-start(f32[5,8,4,256]{3,2,1,0:T(4,128)S(1)} %collective-permute-done.5.refs_10_) | copy-start | bytes 491524
  71.4 16.6 %collective-permute-start.19 = (f32[2,5,2,16,256]{4,3,2,1,0:T(8,128)}, f32[2,5,2,16,256]{4,3,2,1,0:T(8,128)S(1)}, u32[]{:S(2)}, u32[]{:S(2)}) collective-permute-start(f32[2,5,2,16,256]{4,3,2,1,0:T(8,128)} %get-tuple-element.42), channel_id=1, source_target_pairs={{0,0},{1,2},{2,1},{3,3},{4,4},{5,6},{6,5},{7,7},{8,8},{9,10},{10,9... | collective-permute-start | bytes 983048 | tf_op jit(solution)/shard_map/ppermute | solution.py:600
  75.9 0.7 copy-start.17
  86.2 10.8 %collective-permute-start.10 = (f32[5,12,4,256]{3,2,1,0:T(4,128)}, f32[5,12,4,256]{3,2,1,0:T(4,128)S(1)}, u32[]{:S(2)}, u32[]{:S(2)}) collective-permute-start(f32[5,12,4,256]{3,2,1,0:T(4,128)} %get-tuple-element.33), channel_id=1, source_target_pairs={{4,0},{0,20},{20,16},{16,28},{28,24},{24,12},{12,8},{8,4},{5,1},{1... | collective-permute-start | bytes 737288 | tf_op jit(solution)/shard_map/ppermute | solution.py:595
  86.3 1.8 %copy-start.12 = (f32[5,12,4,256]{3,2,1,0:T(4,128)}, f32[5,12,4,256]{3,2,1,0:T(4,128)S(1)}, u32[]{:S(2)}) copy-start(f32[5,12,4,256]{3,2,1,0:T(4,128)S(1)} %collective-permute-done.11.refs_12_.refs_11_.refs_10_) | copy-start | bytes 737284
  86.3 10.7 %collective-permute-start.12 = (f32[5,12,4,256]{3,2,1,0:T(4,128)}, f32[5,12,4,256]{3,2,1,0:T(4,128)S(1)}, u32[]{:S(2)}, u32[]{:S(2)}) collective-permute-start(f32[5,12,4,256]{3,2,1,0:T(4,128)} %get-tuple-element.35), channel_id=1, source_target_pairs={{4,8},{0,4},{20,0},{16,20},{28,16},{24,28},{12,24},{8,12},{5,9},{1... | collective-permute-start | bytes 737288 | tf_op jit(solution)/shard_map/ppermute | solution.py:596
  88.0 0.7 copy-start.13
  88.1 0.8 copy-start.8
  88.1 1.0 copy-start.10
  96.9 26.2 %collective-permute-start.20 = (f32[5,8,16,256]{3,2,1,0:T(8,128)}, f32[5,8,16,256]{3,2,1,0:T(8,128)S(1)}, u32[]{:S(2)}, u32[]{:S(2)}) collective-permute-start(f32[5,8,16,256]{3,2,1,0:T(8,128)} %get-tuple-element.43), channel_id=1, source_target_pairs={{20,4},{16,20},{0,16},{4,0},{24,8},{28,24},{12,28},{8,12},{21,5},{... | collective-permute-start | bytes 1966088 | tf_op jit(solution)/shard_map/ppermute | solution.py:651
  97.0 0.7 copy-start.14
  97.0 0.8 copy-start.15
  105.2 38.9 %collective-permute-start.14 = (f32[5,8,16,256]{3,2,1,0:T(8,128)}, f32[5,8,16,256]{3,2,1,0:T(8,128)S(1)}, u32[]{:S(2)}, u32[]{:S(2)}) collective-permute-start(f32[5,8,16,256]{3,2,1,0:T(8,128)} %get-tuple-element.37), channel_id=1, source_target_pairs={{20,4},{16,20},{0,16},{4,0},{24,8},{28,24},{12,28},{8,12},{21,5},{... | collective-permute-start | bytes 1966088 | tf_op jit(solution)/shard_map/ppermute | solution.py:651
  114.2 16.6 %collective-permute-start.21 = (f32[5,8,16,256]{3,2,1,0:T(8,128)}, f32[5,8,16,256]{3,2,1,0:T(8,128)}, u32[]{:S(2)}, u32[]{:S(2)}) collective-permute-start(f32[5,8,16,256]{3,2,1,0:T(8,128)} %get-tuple-element.44), channel_id=1, source_target_pairs={{16,4},{4,16},{0,0},{20,20},{28,8},{8,28},{12,12},{24,24},{17,5},{... | collective-permute-start | bytes 1966088 | tf_op jit(solution)/shard_map/ppermute | solution.py:652
  116.6 19.4 %collective-permute-start.16 = (f32[5,8,16,256]{3,2,1,0:T(8,128)}, f32[5,8,16,256]{3,2,1,0:T(8,128)S(1)}, u32[]{:S(2)}, u32[]{:S(2)}) collective-permute-start(f32[5,8,16,256]{3,2,1,0:T(8,128)} %get-tuple-element.39), channel_id=1, source_target_pairs={{20,4},{16,20},{0,16},{4,0},{24,8},{28,24},{12,28},{8,12},{21,5},{... | collective-permute-start | bytes 1966088 | tf_op jit(solution)/shard_map/ppermute | solution.py:651
  120.8 19.6 %collective-permute-start.17 = (f32[5,8,16,256]{3,2,1,0:T(8,128)}, f32[5,8,16,256]{3,2,1,0:T(8,128)S(1)}, u32[]{:S(2)}, u32[]{:S(2)}) collective-permute-start(f32[5,8,16,256]{3,2,1,0:T(8,128)} %get-tuple-element.40), channel_id=1, source_target_pairs={{16,4},{4,16},{0,0},{20,20},{28,8},{8,28},{12,12},{24,24},{17,5},{... | collective-permute-start | bytes 1966088 | tf_op jit(solution)/shard_map/ppermute | solution.py:652
  123.1 7.8 %copy-start.5 = (f32[5,8,16,256]{3,2,1,0:T(8,128)}, f32[5,8,16,256]{3,2,1,0:T(8,128)S(1)}, u32[]{:S(2)}) copy-start(f32[5,8,16,256]{3,2,1,0:T(8,128)S(1)} %collective-permute-done.20.one_ref) | copy-start | bytes 1966084
  123.1 24.3 %collective-permute-start.15 = (f32[5,8,16,256]{3,2,1,0:T(8,128)}, f32[5,8,16,256]{3,2,1,0:T(8,128)S(1)}, u32[]{:S(2)}, u32[]{:S(2)}) collective-permute-start(f32[5,8,16,256]{3,2,1,0:T(8,128)} %get-tuple-element.38), channel_id=1, source_target_pairs={{16,4},{4,16},{0,0},{20,20},{28,8},{8,28},{12,12},{24,24},{17,5},{... | collective-permute-start | bytes 1966088 | tf_op jit(solution)/shard_map/ppermute | solution.py:652
  136.0 4.4 %copy-start.2 = (f32[5,8,16,256]{3,2,1,0:T(8,128)}, f32[5,8,16,256]{3,2,1,0:T(8,128)S(1)}, u32[]{:S(2)}) copy-start(f32[5,8,16,256]{3,2,1,0:T(8,128)S(1)} %collective-permute-done.16.one_ref) | copy-start | bytes 1966084
  140.4 0.9 copy-start.4
  144.1 3.3 %copy-start.1 = (f32[5,8,16,256]{3,2,1,0:T(8,128)}, f32[5,8,16,256]{3,2,1,0:T(8,128)S(1)}, u32[]{:S(2)}) copy-start(f32[5,8,16,256]{3,2,1,0:T(8,128)S(1)} %collective-permute-done.14.one_ref) | copy-start | bytes 1966084
  147.4 0.8 copy-start.3

commit v3 on v2

--- a/solution.py
+++ b/solution.py
@@ -16,22 +16,90 @@
 vector = pl.BlockSpec(memory_space=pltpu.VMEM)
 GROUP = 4
 TAILS = 2
-
-
-def ready(flags, *early):
-    def copy_flags(flags_ref, *refs):
-        for i in range(flags_ref.shape[0]):
-            refs[-1][i] = flags_ref[i]
-
+OUTER = 8
+SECTION_VMEM = 28 << 20
+COPY_VMEM = 8 << 20
+
+
+def prepare_kernel(flags_ref, filter_ref, deriv_ref, table_ref, radius_ref, flags_out, hi_ref, lo_ref):
+    for i in range(flags_ref.shape[0]):
+        flags_out[i] = flags_ref[i]
+    size = filter_ref.shape[0]
+    half = size // 2
+    dot = functools.partial(jnp.dot, preferred_element_type=jnp.float32)
+
+    def fold(flip):
+        row = lax.broadcasted_iota(jnp.int32, (size, size), flip)
+        column = lax.broadcasted_iota(jnp.int32, (size, size), 1 - flip)
+        return (column == jnp.where(row < half, row + half, size - 1 - row)).astype(jnp.bfloat16)
+
+    into, back_out = fold(0), fold(1)
+
+    def split(value):
+        hi = value.astype(jnp.bfloat16)
+        return hi, (value - hi.astype(jnp.float32)).astype(jnp.bfloat16)
+
+    def folded(matrix):
+        turned = lax.dot_general(
+            into, matrix, (((1,), (1,)), ((), ())), preferred_element_type=jnp.float32
+        ).astype(jnp.bfloat16)
+        return dot(turned, back_out)
+
+    filter_hi, filter_lo = (folded(part) for part in split(filter_ref[...]))
+    deriv_hi, deriv_lo = (folded(part).astype(jnp.bfloat16) for part in split(deriv_ref[...]))
+    hi_ref[:size] = filter_hi.astype(jnp.bfloat16)
+    lo_ref[:size] = filter_lo.astype(jnp.bfloat16)
+    row = lax.broadcasted_iota(jnp.int32, (size, size), 0)
+    sign = jnp.where(row < half, 1.0, -1.0)
+    signed_hi = (sign * filter_hi).astype(jnp.bfloat16)
+    signed_lo = (sign * filter_lo).astype(jnp.bfloat16)
+    both = dot(deriv_hi, signed_hi) + dot(deriv_lo, signed_hi) + dot(deriv_hi, signed_lo)
+    hi, lo = split(both)
+    hi_ref[size:] = hi
+    lo_ref[size:] = lo
+
+
+def prepare(flags, filter_matrix, deriv_matrix, table, radius):
+    size = filter_matrix.shape[0]
+    half = jax.ShapeDtypeStruct((2 * size, size), jnp.bfloat16)
     return pl.pallas_call(
-        copy_flags, out_shape=jax.ShapeDtypeStruct(flags.shape, flags.dtype),
-        in_specs=[scalars] + [anywhere] * len(early), out_specs=scalars, name="ready",
-    )(flags, *early)
-
-
-def split_weights(w):
-    high = lax.reduce_precision(w, 8, 7)
-    return high.astype(jnp.bfloat16), (w - high).astype(jnp.bfloat16)
+        prepare_kernel,
+        out_shape=(jax.ShapeDtypeStruct(flags.shape, flags.dtype), half, half),
+        in_specs=[scalars, vector, vector, anywhere, anywhere],
+        out_specs=(scalars, vector, vector),
+        compiler_params=pltpu.CompilerParams(vmem_limit_bytes=3 * COPY_VMEM),
+        name="prepare",
+    )(flags, filter_matrix, deriv_matrix, table, radius)
+
+
+def cut_kernel(spans, flags_ref, own_ref, out_ref, sems):
+    rows = out_ref.shape[2]
+    half = 1 - flags_ref[HALF]
+    copies = []
+    for i, (start, at, size) in enumerate(parts_of(spans)):
+        copies.append(
+            pltpu.make_async_copy(
+                own_ref.at[:, start : start + size, pl.ds(pl.multiple_of(half * rows, rows), rows)],
+                out_ref.at[:, at : at + size], sems.at[i],
+            )
+        )
+    run_copies(copies)
+    wait_copies(copies)
+
+
+def cut_task(spans, flags, own):
+    fields, _, both, radii = own.shape
+    planes = sum(count for _, count in spans)
+    return pl.pallas_call(
+        functools.partial(cut_kernel, spans),
+        out_shape=jax.ShapeDtypeStruct((fields, planes, both // 2, radii), own.dtype),
+        in_specs=[scalars, pl.BlockSpec(memory_space=pltpu.HBM)], out_specs=vector,
+        scratch_shapes=[pltpu.SemaphoreType.DMA((len(parts_of(spans)),))],
+        compiler_params=pltpu.CompilerParams(vmem_limit_bytes=COPY_VMEM),
+        cost_estimate=pl.CostEstimate(
+            flops=0, bytes_accessed=4 * fields * planes * both * radii, transcendentals=0
+        ),
+    )(flags, own)
 
 
 _, _, SWAP_LEFT, SWAP_RIGHT, SEG, ODD, HALF = range(7)
@@ -113,11 +181,13 @@
 
     loads, q_wait, base_wait = [], {}, {}
 
-    def load(source, target, start, at, size):
+    kept = pl.ds(pl.multiple_of(flags_ref[HALF] * rows, rows), rows)
+
+    def load(source, target, start, plane, at, size):
         if len(source) == 1:
             return [copy(source[0].at[:, :, start : start + size], target.at[:, :, at : at + size])]
         return [
-            copy(source[0].at[:, start : start + size], target.at[seg, :, at : at + size]),
+            copy(source[0].at[:, plane : plane + size, kept], target.at[seg, :, at : at + size]),
             copy(source[1].at[:, start : start + size], target.at[1 - seg, :, at : at + size]),
         ]
 
@@ -129,12 +199,12 @@
         return out
 
     q_from, base_from = sources("q", q_in), sources("base", base_in)
-    for array, start, at, size in plan["q"]:
-        q_wait[at] = load(q_from[array], q_s, start, at, size)
+    for array, start, plane, at, size in plan["q"]:
+        q_wait[at] = load(q_from[array], q_s, start, plane, at, size)
         loads += [(at, one) for one in q_wait[at]]
     if mixed:
-        for array, start, at, size in plan["base"]:
-            base_wait[at] = load(base_from[array], base_s, start, at, size)
+        for array, start, plane, at, size in plan["base"]:
+            base_wait[at] = load(base_from[array], base_s, start, plane, at, size)
             loads += [(at + 4, one) for one in base_wait[at]]
     weight_copies = [copy(whi_hbm, whi_s), copy(wlo_hbm, wlo_s)]
     loads += [(9, one) for one in weight_copies]
@@ -305,10 +375,10 @@
             array, start = table[p]
             index = index_of(kind, array)
             last = spans[-1] if spans else None
-            if last and last[0] == index and last[1] + last[3] == start and last[2] + last[3] == at and last[3] < GROUP:
-                last[3] += 1
+            if last and last[4] < GROUP and last[:4] == [index, start - last[4], p - last[4], at - last[4]]:
+                last[4] += 1
             else:
-                spans.append([index, start, at, 1])
+                spans.append([index, start, p, at, 1])
         return spans
 
     table_row = consts[1]
@@ -318,7 +388,7 @@
     tips_at = {at: p for at, p in enumerate(wide) if p < 0 or p >= planes}
     kept = [(at, p) for at, p in enumerate(wide) if at not in tips_at]
     q_spans = pieces("q", q_map, [p for _, p in kept])
-    q_spans = [[i, start, kept[at][0], size] for i, start, at, size in q_spans]
+    q_spans = [[i, start, p, kept[at][0], size] for i, start, p, at, size in q_spans]
     plan = dict(
         dims=dims, lengths=[b - a for a, b in ranges], mixed=mixed, final=final, tips=tips,
         low_flag=next((i for i, r in enumerate(ranges) if r[0] == 0), None),
@@ -372,6 +442,7 @@
             pltpu.VMEM((2, fields, total, rows, radii), f32),
             pltpu.SemaphoreType.DMA((copies,)),
         ],
+        compiler_params=pltpu.CompilerParams(vmem_limit_bytes=SECTION_VMEM),
         cost_estimate=pl.CostEstimate(
             flops=2 * lines * 4 * radii * 2 * radii * 6, bytes_accessed=8 * lines * radii * 4,
             transcendentals=0,
@@ -389,18 +460,21 @@
     return parts
 
 
-def edges_kernel(tips, flags_ref, one_ref, two_ref, *refs):
+def edges_kernel(spans, tips, flags_ref, own_ref, far_ref, *refs):
     outs, (q_s, sems) = refs[:-2], refs[-2:]
     _, fields, planes, rows, _ = q_s.shape
     seg = flags_ref[SEG]
-    parts = parts_of(((0, planes),))
+    parts = parts_of(spans)
+    kept = pl.ds(pl.multiple_of(flags_ref[HALF] * rows, rows), rows)
     loads = []
-    for i, (_, at, size) in enumerate(parts):
+    for i, (start, at, size) in enumerate(parts):
         span = slice(at, at + size)
         loads.append(
             [
-                pltpu.make_async_copy(one_ref.at[:, span], q_s.at[seg, :, span], sems.at[2 * i]),
-                pltpu.make_async_copy(two_ref.at[:, span], q_s.at[1 - seg, :, span], sems.at[2 * i + 1]),
+                pltpu.make_async_copy(
+                    own_ref.at[:, start : start + size, kept], q_s.at[seg, :, span], sems.at[2 * i]
+                ),
+                pltpu.make_async_copy(far_ref.at[:, span], q_s.at[1 - seg, :, span], sems.at[2 * i + 1]),
             ]
         )
         run_copies(loads[-1])
@@ -431,9 +505,9 @@
         wait_copies(copies)
 
 
-def edges_task(tips, flags, one, two, dims):
+def edges_task(spans, tips, flags, own, far, dims):
     fields, rows, radii = dims
-    planes = one.shape[1]
+    planes = far.shape[1]
     f32 = jnp.float32
     out_shape = [jax.ShapeDtypeStruct((fields, planes, 4, radii), f32)] * 2
     out_specs = [vector, vector]
@@ -441,18 +515,19 @@
         out_shape += [jax.ShapeDtypeStruct((2, fields, 2, rows, radii), f32)] * 2
         out_specs += [anywhere] * 2
     return pl.pallas_call(
-        functools.partial(edges_kernel, tips),
+        functools.partial(edges_kernel, spans, tips),
         out_shape=out_shape,
         in_specs=[scalars] + [anywhere] * 2,
         out_specs=out_specs,
         scratch_shapes=[
             pltpu.VMEM((2, fields, planes, rows, radii), f32),
-            pltpu.SemaphoreType.DMA((2 * len(parts_of(((0, planes),))) + 2,)),
+            pltpu.SemaphoreType.DMA((2 * len(parts_of(spans)) + 2,)),
         ],
+        compiler_params=pltpu.CompilerParams(vmem_limit_bytes=COPY_VMEM),
         cost_estimate=pl.CostEstimate(
             flops=0, bytes_accessed=8 * fields * planes * rows * radii, transcendentals=0
         ),
-    )(flags, one, two)
+    )(flags, own, far)
 
 
 def place_kernel(spans, chained, flags_ref, one_ref, two_ref, *refs):
@@ -499,16 +574,12 @@
             pltpu.VMEM((fields, count, ang_dev, radii), jnp.float32),
             pltpu.SemaphoreType.DMA((3 * len(parts_of(spans)),)),
         ],
+        compiler_params=pltpu.CompilerParams(vmem_limit_bytes=COPY_VMEM),
         input_output_aliases={} if whole is None else {3: 0},
         cost_estimate=pl.CostEstimate(
             flops=0, bytes_accessed=8 * fields * count * ang_dev * radii, transcendentals=0
         ),
     )(*operands)
-
-
-def folded(matrix, radii):
-    tall = jnp.concatenate([matrix[radii:], matrix[:radii][::-1]], axis=0)
-    return jnp.concatenate([tall[:, radii:], tall[:, :radii][:, ::-1]], axis=1)
 
 
 def per_device(conserved, deriv_matrix, filter_matrix):
@@ -522,22 +593,11 @@
     twist = total / (2.0 * math.pi * radii)
     pos = lax.axis_index("ang")
     layer = lax.axis_index("ax")
-    h, j, c = pos // half, (pos % half) // 2, pos % 2
-    ring = 4 * j + 2 * (h ^ (j & 1)) + 1 - c
-    keeps = h == (c ^ (j & 1))
-
-    def dev(hh, jj, cc):
-        return hh * half + 2 * jj + cc
-
-    cycle, swap = [], []
-    for jj in range(n // 4):
-        odd = jj & 1
-        keeper = [dev(hh, jj, hh ^ odd) for hh in range(2)]
-        giver = [dev(hh, jj, 1 - (hh ^ odd)) for hh in range(2)]
-        ring_of_four = [giver[0], keeper[1], giver[1], keeper[0]]
-        cycle += [(ring_of_four[i], ring_of_four[(i + 1) % 4]) for i in range(4)]
-        swap += [(giver[0], giver[1]), (giver[1], giver[0]), (keeper[0], keeper[0]), (keeper[1], keeper[1])]
-    order = [dev((r % 4 // 2) ^ (r // 4 & 1), r // 4, 1 - r % 2) for r in range(n)]
+    h, pair = pos // half, pos % half
+    kept = h ^ (pair & 1)
+    ring = 2 * pair + kept
+    across = [(i, (i + half) % n) for i in range(n)]
+    order = [((r % 2) ^ (r // 2 & 1)) * half + r // 2 for r in range(n)]
     to_left = [(order[r], order[(r - 1) % n]) for r in range(n)]
     to_right = [(order[r], order[(r + 1) % n]) for r in range(n)]
 
@@ -547,12 +607,8 @@
             table[i], table[i + 1] = i + 1, i
         return sorted(table.items())
 
-    def back(table):
-        return [(b, a) for a, b in table]
-
-    sent_half = h ^ (j & 1)
     flags = jnp.stack(
-        [layer > 0, layer < count - 1, ring == 0, ring == n - 1, (h == 1) ^ keeps, layer % 2 == 1, sent_half == 1]
+        [layer > 0, layer < count - 1, ring == 0, ring == n - 1, h == 1, layer % 2 == 1, kept == 1]
     ).astype(jnp.int32)
 
     def angles(offsets):
@@ -574,22 +630,13 @@
     trig_values = jnp.concatenate([trig_rows(1.0), trig_rows(0.5)])
     table = jnp.broadcast_to(trig_values[:, None], (trig_values.shape[0], 128))
     radius = ((jnp.arange(radii, dtype=jnp.int32).astype(jnp.float32) + 0.5) / radii)[None]
-    signs = jnp.where(jnp.arange(2 * radii, dtype=jnp.int32) < radii, -1.0, 1.0).astype(jnp.float32)
-
-    outer = planes // 3
+    outer = OUTER * planes // 24
     span_outer = ((0, outer), (planes - outer, outer))
     span_inner = ((outer, planes - 2 * outer),)
 
-    def cut(spans):
-        parts = [lax.slice_in_dim(conserved, a, a + m, axis=1) for a, m in spans]
-        block = parts[0] if len(parts) == 1 else jnp.concatenate(parts, axis=1)
-        return block[:, :, :rows], block[:, :, rows:]
-
     def send(spans):
-        first_half, second_half = cut(spans)
-        one = jnp.where(sent_half == 0, first_half, second_half)
-        two = jnp.where(sent_half == 0, second_half, first_half)
-        return lax.ppermute(one, "ang", cycle), lax.ppermute(two, "ang", swap)
+        block = cut_task(spans, flags, conserved)
+        return lax.ppermute(block, "ang", across)
 
     def trade(left_edge, right_edge):
         left = lax.ppermute(right_edge, "ang", to_right)
@@ -610,11 +657,7 @@
     sent_outer = send(span_outer)
     sent_inner = send(span_inner)
 
-    composite = jnp.dot(filter_matrix, signs[:, None] * deriv_matrix, precision=lax.Precision.HIGH)
-    weights = jnp.concatenate([folded(filter_matrix, radii).T, folded(composite, radii).T], axis=0)
-
-    whi, wlo = split_weights(weights)
-    flags = ready(flags, whi, wlo, table, radius)
+    flags, whi, wlo = prepare(flags, filter_matrix, deriv_matrix, table, radius)
 
     ro = ((0, outer), (planes - outer, planes))
     ri = ((outer, planes - outer),)
@@ -630,9 +673,9 @@
             right_map, flags, planes, dims, final, tips,
         )
 
-    left_o, right_o, tip_one, tip_two = edges_task(True, flags, *sent_outer, dims)
+    left_o, right_o, tip_one, tip_two = edges_task(span_outer, True, flags, conserved, sent_outer, dims)
     halo_left, halo_right = trade(left_o, right_o)
-    q_map = listed(sent_outer, ro)
+    q_map = listed((conserved, sent_outer), ro)
     q_map["tips"] = trade_tips(tip_one, tip_two)
     lefts, rights = listed(halo_left, ro), listed(halo_right, ro)
     f_o, left_f, right_f, tip_one, tip_two = section(1.0, one_o, (q_map, lefts, rights), None, tips=True)
@@ -641,15 +684,14 @@
     f_map["tips"] = trade_tips(tip_one, tip_two)
     f_lefts, f_rights = listed(halo_left, one_o), listed(halo_right, one_o)
 
-    left_i, right_i = edges_task(False, flags, *sent_inner, dims)
+    left_i, right_i = edges_task(span_inner, False, flags, conserved, sent_inner, dims)
     halo_left, halo_right = trade(left_i, right_i)
-    q_map.update(listed(sent_inner, ri))
+    q_map.update(listed((conserved, sent_inner), ri))
     lefts.update(listed(halo_left, ri))
     rights.update(listed(halo_right, ri))
 
-    def give_back(one, two):
-        one = lax.ppermute(one, "ang", back(cycle))
-        return one, lax.ppermute(two, "ang", back(swap))
+    def give_back(near, far):
+        return near, lax.ppermute(far, "ang", across)
 
     backs = []
     near, far = section(0.5, two_o, (f_map, f_lefts, f_rights), q_map, final=True)

time: 153 us -> 141 us (0.922)
  waiting for transfers between devices: 23.6 us -> 68 us
  starting transfers between devices: 45.5 us -> 21.4 us
  Pallas kernels: 58.8 us -> 43 us
  other arithmetic: 8.05 us -> 0.3 us
  local copies, waits for them, and re-layouts: 11.4 us -> 7.39 us
  matrix products: 3.17 us -> 0 us
    ppermute x10 -> x5, waiting for transfers between devices: 23.5 us -> 55 us  [the longest x3 28.5 us: give_back(): return (near, lax.ppermute(far, 'ang', across))]
    ppermute x10 -> x5, starting transfers between devices: 29.4 us -> 3.59 us  [the longest x3 1.99 us: give_back(): return (near, lax.ppermute(far, 'ang', across))]
    pallas_call x5, Pallas kernels: 42.1 us -> 29.8 us  [section_task(): pl.pallas_call(functools.partial(section_kernel, plan, factor), out_shape...]
    ppermute x4, starting transfers between devices: 1.41 us -> 12.4 us  [trade(): left = lax.ppermute(right_edge, 'ang', to_right)]
    ppermute x4, waiting for transfers between devices: 0.01 us -> 8.53 us  [trade(): left = lax.ppermute(right_edge, 'ang', to_right)]
    ppermute x4, starting transfers between devices: 5.73 us -> 0.01 us  [trade(): return (left, lax.ppermute(left_edge, 'ang', to_left))]
    select_n x3 -> x0, other arithmetic: 4.51 us -> none  [the longest x2 4.51 us: send(): two = jnp.where(sent_half == 0, second_half, first_half)]
    ppermute x4, waiting for transfers between devices: 0.01 us -> 4.45 us  [trade(): return (left, lax.ppermute(left_edge, 'ang', to_left))]
  transfers between devices with their start and end apart: 22 -> 17, of which waited for: 6 -> 8; matrix products, arithmetic and copies ran while one was open for 9% -> 1% of each run, Pallas kernels for 37% -> 29%
where the time goes in v3:
time: 141 us; the launch traced here: 140 us
  waiting for transfers between devices  68 us (48%)
  Pallas kernels  43 us (30%)
  starting transfers between devices  21.4 us (15%)
  local copies, waits for them, and re-layouts  7.39 us (5%)
    pallas_call x5, Pallas kernels, section_task(): pl.pallas_call(functools.partial(section_kernel, plan, factor), out_shape...  29.8 us
    ppermute x3, waiting for transfers between devices, give_back(): return (near, lax.ppermute(far, 'ang', across))  28.5 us
    ppermute x2, waiting for transfers between devices, send(): return lax.ppermute(block, 'ang', across)  26.4 us
    ppermute x4, starting transfers between devices, trade(): left = lax.ppermute(right_edge, 'ang', to_right)  12.4 us
    ppermute x4, waiting for transfers between devices, trade(): left = lax.ppermute(right_edge, 'ang', to_right)  8.53 us
    unnamed x10, local copies, waits for them, and re-layouts  6.68 us
    ppermute x2, starting transfers between devices, trade_tips(): return (one, lax.ppermute(two, 'ax', layer_swap(1)))  5.27 us
    pallas_call x3, Pallas kernels, place_task(): pl.pallas_call(functools.partial(place_kernel, spans, whole is not None),...  5.23 us
  transfers between devices with their start and end apart: 17, of which 8 were waited for; matrix products, arithmetic and copies ran while one was open for 1% of the time, Pallas kernels for 29%

profile of v3, /device:TPU:9, one launch (start us, length us, event | category | flops | bytes accessed | tf_op | source)
XLA Modules:
  0.0 140.4 jit_solution(12026259614298285155)
XLA Ops:
  0.0 0.1 stack.56
  0.1 2.1 %copy-done = f32[5,24,32,256]{3,2,1,0:T(8,128)S(1)} copy-done((f32[5,24,32,256]{3,2,1,0:T(8,128)S(1)}, f32[5,24,32,256]{3,2,1,0:T(8,128)}, u32[]{:S(2)}) %copy-start) | copy-done | bytes 3932184
  2.2 0.7 shard_map.37
  2.9 1.3 collective-permute-start
  4.2 1.4 %shard_map.38 = f32[5,8,16,256]{3,2,1,0:T(8,128)} custom-call(s32[7]{0:T(128)S(1)} %convert_element_type.78.flags_ref, f32[5,24,32,256]{3,2,1,0:T(8,128)S(1)} %copy-done), custom_call_target="tpu_custom_call" | custom-call | bytes 1310720 | tf_op jit(solution)/shard_map/pallas_call | solution.py:93
  5.7 0.3 collective-permute-start.1
  6.0 0.1 add_add_fusion.1
  6.0 0.1 add.283
  6.1 0.1 add.277
  6.2 0.1 fusion.12
  6.4 0.1 reshape.341
  6.5 0.1 reshape.342
  6.6 0.1 reshape.343
  6.7 0.1 concatenate.17
  6.8 0.1 broadcast_in_dim.2.table_ref.refs_1_
  6.9 0.0 copy-start.3
  6.9 1.2 copy-done.3
  8.1 1.2 copy-done.4
  9.4 3.8 %prepare.1 = (s32[7]{0:T(128)S(1)}, bf16[1024,512]{1,0:T(8,128)(2,1)S(1)}, bf16[1024,512]{1,0:T(8,128)(2,1)S(1)}) custom-call(s32[7]{0:T(128)S(1)} %convert_element_type.78.flags_ref, f32[512,512]{1,0:T(8,128)S(1)} %copy-done.3, f32[512,512]{1,0:T(8,128)S(1)} %copy-done.4, f32[320,128]{1,0:T(8,128)S(1)} %broadcast_in_dim.2.table_ref.refs_1_, ...), custom_call_target="tpu_custom_call" | custom-call | tf_op jit(solution)/shard_map/prepare/pallas_call | solution.py:65
  13.1 19.5 %collective-permute-done.far_ref.refs_6_.refs_10_.refs_8_.refs_9_ = f32[5,16,16,256]{3,2,1,0:T(8,128)S(1)} collective-permute-done((f32[5,16,16,256]{3,2,1,0:T(8,128)S(1)}, f32[5,16,16,256]{3,2,1,0:T(8,128)S(1)}, u32[]{:S(2)}, u32[]{:S(2)}) %collective-permute-start) | collective-permute-done | bytes 1310752 | tf_op jit(solution)/shard_map/ppermute | solution.py:639
  32.6 2.1 %copy-done.1 = f32[5,24,32,256]{3,2,1,0:T(8,128)S(1)} copy-done((f32[5,24,32,256]{3,2,1,0:T(8,128)S(1)}, f32[5,24,32,256]{3,2,1,0:T(8,128)}, u32[]{:S(2)}) %copy-start.1) | copy-done | bytes 3932184
  34.8 1.2 shard_map.39
  35.9 3.8 %collective-permute-start.2 = (f32[5,16,4,256]{3,2,1,0:T(4,128)S(1)}, f32[5,16,4,256]{3,2,1,0:T(4,128)S(1)}, u32[]{:S(2)}, u32[]{:S(2)}) collective-permute-start(f32[5,16,4,256]{3,2,1,0:T(4,128)S(1)} %get-tuple-element.31), channel_id=1, source_target_pairs={{0,16},{16,20},{20,4},{4,8},{8,24},{24,28},{28,12},{12,0},{1,17},{... | collective-permute-start | bytes 983048 | tf_op jit(solution)/shard_map/ppermute | solution.py:642
  39.8 6.9 %collective-permute-done.1.far_ref.refs_8_.refs_10_ = f32[5,8,16,256]{3,2,1,0:T(8,128)S(1)} collective-permute-done((f32[5,8,16,256]{3,2,1,0:T(8,128)}, f32[5,8,16,256]{3,2,1,0:T(8,128)S(1)}, u32[]{:S(2)}, u32[]{:S(2)}) %collective-permute-start.1) | collective-permute-done | bytes 655392 | tf_op jit(solution)/shard_map/ppermute | solution.py:639
  46.7 0.8 shard_map.40
  47.5 3.8 %collective-permute-start.3 = (f32[5,8,4,256]{3,2,1,0:T(4,128)S(1)}, f32[5,8,4,256]{3,2,1,0:T(4,128)S(1)}, u32[]{:S(2)}, u32[]{:S(2)}) collective-permute-start(f32[5,8,4,256]{3,2,1,0:T(4,128)S(1)} %get-tuple-element.32), channel_id=1, source_target_pairs={{0,16},{16,20},{20,4},{4,8},{8,24},{24,28},{28,12},{12,0},{1,17},{... | collective-permute-start | bytes 491528 | tf_op jit(solution)/shard_map/ppermute | solution.py:642
  51.4 0.2 collective-permute-start.6
  51.5 5.7 %collective-permute-done.3.refs_10_ = f32[5,8,4,256]{3,2,1,0:T(4,128)S(1)} collective-permute-done((f32[5,8,4,256]{3,2,1,0:T(4,128)S(1)}, f32[5,8,4,256]{3,2,1,0:T(4,128)S(1)}, u32[]{:S(2)}, u32[]{:S(2)}) %collective-permute-start.3) | collective-permute-done | bytes 163872 | tf_op jit(solution)/shard_map/ppermute | solution.py:642
  57.2 3.2 %collective-permute-start.7 = (f32[2,5,2,16,256]{4,3,2,1,0:T(8,128)S(1)}, f32[2,5,2,16,256]{4,3,2,1,0:T(8,128)S(1)}, u32[]{:S(2)}, u32[]{:S(2)}) collective-permute-start(f32[2,5,2,16,256]{4,3,2,1,0:T(8,128)S(1)} %get-tuple-element.37), channel_id=1, source_target_pairs={{0,0},{1,2},{2,1},{3,3},{4,4},{5,6},{6,5},{7,7},{8,8},{9,10},{10,9... | collective-permute-start | bytes 983048 | tf_op jit(solution)/shard_map/ppermute | solution.py:647
  60.5 6.9 %shard_map.41 = (f32[2,5,12,16,256]{4,3,2,1,0:T(8,128)S(1)}, f32[5,12,4,256]{3,2,1,0:T(4,128)S(1)}, f32[5,12,4,256]{3,2,1,0:T(4,128)S(1)}) custom-call(s32[7]{0:T(128)S(1)} %get-tuple-element.28.flags_ref.refs_0_, f32[320,128]{1,0:T(8,128)S(1)} %broadcast_in_dim.2.table_ref.refs_1_, f32[1,256]{1,0:T(1,128)S(1)} %add_multiply_fusion.radius_ref.refs_2_, ...), custom_call_target="tpu_custom_call" | custom-call | flops 6039797760 | bytes 7864320 | tf_op jit(solution)/shard_map/pallas_call | solution.py:428
  67.4 2.2 %collective-permute-start.8 = (f32[5,12,4,256]{3,2,1,0:T(4,128)S(1)}, f32[5,12,4,256]{3,2,1,0:T(4,128)S(1)}, u32[]{:S(2)}, u32[]{:S(2)}) collective-permute-start(f32[5,12,4,256]{3,2,1,0:T(4,128)S(1)} %get-tuple-element.39), channel_id=1, source_target_pairs={{0,16},{16,20},{20,4},{4,8},{8,24},{24,28},{28,12},{12,0},{1,17},{... | collective-permute-start | bytes 737288 | tf_op jit(solution)/shard_map/ppermute | solution.py:642
  69.6 7.1 %shard_map.42 = (f32[2,5,12,16,256]{4,3,2,1,0:T(8,128)S(1)}, f32[5,12,4,256]{3,2,1,0:T(4,128)S(1)}, f32[5,12,4,256]{3,2,1,0:T(4,128)S(1)}, f32[2,5,2,16,256]{4,3,2,1,0:T(8,128)S(1)}, f32[2,5,2,16,256]{4,3,2,1,0:T(8,128)S(1)}) custom-call(s32[7]{0:T(128)S(1)} %get-tuple-element.28.flags_ref.refs_0_, f32[320,128]{1,0:T(8,128)S(1)} %broadcast_in_dim.2.table_ref.refs_1_, ...), custom_call_target="tpu_custom_call" | custom-call | flops 6039797760 | bytes 7864320 | tf_op jit(solution)/shard_map/pallas_call | solution.py:428
  76.7 2.5 %collective-permute-start.9 = (f32[5,12,4,256]{3,2,1,0:T(4,128)S(1)}, f32[5,12,4,256]{3,2,1,0:T(4,128)S(1)}, u32[]{:S(2)}, u32[]{:S(2)}) collective-permute-start(f32[5,12,4,256]{3,2,1,0:T(4,128)S(1)} %get-tuple-element.40), channel_id=1, source_target_pairs={{0,16},{16,20},{20,4},{4,8},{8,24},{24,28},{28,12},{12,0},{1,17},{... | collective-permute-start | bytes 737288 | tf_op jit(solution)/shard_map/ppermute | solution.py:642
  79.3 2.1 %collective-permute-start.15 = (f32[2,5,2,16,256]{4,3,2,1,0:T(8,128)S(1)}, f32[2,5,2,16,256]{4,3,2,1,0:T(8,128)S(1)}, u32[]{:S(2)}, u32[]{:S(2)}) collective-permute-start(f32[2,5,2,16,256]{4,3,2,1,0:T(8,128)S(1)} %get-tuple-element.48), channel_id=1, source_target_pairs={{0,0},{1,2},{2,1},{3,3},{4,4},{5,6},{6,5},{7,7},{8,8},{9,10},{10,9... | collective-permute-start | bytes 983048 | tf_op jit(solution)/shard_map/ppermute | solution.py:647
  81.4 2.8 %collective-permute-done.9.refs_12_.refs_11_.refs_10_ = f32[5,12,4,256]{3,2,1,0:T(4,128)S(1)} collective-permute-done((f32[5,12,4,256]{3,2,1,0:T(4,128)S(1)}, f32[5,12,4,256]{3,2,1,0:T(4,128)S(1)}, u32[]{:S(2)}, u32[]{:S(2)}) %collective-permute-start.9) | collective-permute-done | bytes 245792 | tf_op jit(solution)/shard_map/ppermute | solution.py:642
  84.2 1.8 %collective-permute-done.10.refs_13_.refs_14_ = f32[5,12,4,256]{3,2,1,0:T(4,128)S(1)} collective-permute-done((f32[5,12,4,256]{3,2,1,0:T(4,128)S(1)}, f32[5,12,4,256]{3,2,1,0:T(4,128)S(1)}, u32[]{:S(2)}, u32[]{:S(2)}) %collective-permute-start.10) | collective-permute-done | bytes 245792 | tf_op jit(solution)/shard_map/ppermute | solution.py:643
  86.0 2.6 %collective-permute-done.11.refs_14_.refs_13_.refs_11_ = f32[5,12,4,256]{3,2,1,0:T(4,128)S(1)} collective-permute-done((f32[5,12,4,256]{3,2,1,0:T(4,128)S(1)}, f32[5,12,4,256]{3,2,1,0:T(4,128)S(1)}, u32[]{:S(2)}, u32[]{:S(2)}) %collective-permute-start.11) | collective-permute-done | bytes 245792 | tf_op jit(solution)/shard_map/ppermute | solution.py:643
  88.7 5.2 %shard_map.44 = (f32[5,8,16,256]{3,2,1,0:T(8,128)S(1)}, f32[5,8,16,256]{3,2,1,0:T(8,128)S(1)}) custom-call(s32[7]{0:T(128)S(1)} %get-tuple-element.28.flags_ref.refs_0_, f32[320,128]{1,0:T(8,128)S(1)} %broadcast_in_dim.2.table_ref.refs_1_, f32[1,256]{1,0:T(1,128)S(1)} %add_multiply_fusion.radius_ref.refs_2_, ...), custom_call_target="tpu_custom_call" | custom-call | flops 4026531840 | bytes 5242880 | tf_op jit(solution)/shard_map/pallas_call | solution.py:428
  93.9 0.4 collective-permute-start.13
  94.3 5.4 %shard_map.45 = (f32[5,8,16,256]{3,2,1,0:T(8,128)S(1)}, f32[5,8,16,256]{3,2,1,0:T(8,128)S(1)}) custom-call(s32[7]{0:T(128)S(1)} %get-tuple-element.28.flags_ref.refs_0_, f32[320,128]{1,0:T(8,128)S(1)} %broadcast_in_dim.2.table_ref.refs_1_, f32[1,256]{1,0:T(1,128)S(1)} %add_multiply_fusion.radius_ref.refs_2_, ...), custom_call_target="tpu_custom_call" | custom-call | flops 4026531840 | bytes 5242880 | tf_op jit(solution)/shard_map/pallas_call | solution.py:428
  99.7 1.2 collective-permute-start.16
  100.9 5.2 %shard_map.43 = (f32[5,8,16,256]{3,2,1,0:T(8,128)S(1)}, f32[5,8,16,256]{3,2,1,0:T(8,128)S(1)}) custom-call(s32[7]{0:T(128)S(1)} %get-tuple-element.28.flags_ref.refs_0_, f32[320,128]{1,0:T(8,128)S(1)} %broadcast_in_dim.2.table_ref.refs_1_, f32[1,256]{1,0:T(1,128)S(1)} %add_multiply_fusion.radius_ref.refs_2_, ...), custom_call_target="tpu_custom_call" | custom-call | flops 4026531840 | bytes 5242880 | tf_op jit(solution)/shard_map/pallas_call | solution.py:428
  106.1 0.4 collective-permute-start.12
  106.5 18.3 %collective-permute-done.16.two_ref = f32[5,8,16,256]{3,2,1,0:T(8,128)S(1)} collective-permute-done((f32[5,8,16,256]{3,2,1,0:T(8,128)S(1)}, f32[5,8,16,256]{3,2,1,0:T(8,128)S(1)}, u32[]{:S(2)}, u32[]{:S(2)}) %collective-permute-start.16) | collective-permute-done | bytes 655392 | tf_op jit(solution)/shard_map/ppermute | solution.py:694
  124.7 1.7 %shard_map.46.refs_0_ = f32[5,24,32,256]{3,2,1,0:T(8,128)} custom-call(s32[7]{0:T(128)S(1)} %get-tuple-element.28.flags_ref.refs_0_, f32[5,8,16,256]{3,2,1,0:T(8,128)S(1)} %get-tuple-element.49.one_ref, f32[5,8,16,256]{3,2,1,0:T(8,128)S(1)} %collective-permute-done.16.two_ref), custom_call_target="tpu_custom_call" | custom-call | bytes 2621440 | tf_op jit(solution)/shard_map/pallas_call | solution.py:568
  126.5 1.7 %shard_map.47.refs_0_ = f32[5,24,32,256]{3,2,1,0:T(8,128)} custom-call(s32[7]{0:T(128)S(1)} %get-tuple-element.28.flags_ref.refs_0_, f32[5,8,16,256]{3,2,1,0:T(8,128)S(1)} %get-tuple-element.45.one_ref, f32[5,8,16,256]{3,2,1,0:T(8,128)S(1)} %collective-permute-done.13.two_ref, f32[5,24,32,256]{3,2,1,0:T(8,128)} %shard_map.46.refs_0_), custom_call_target="tpu_custom_call", output_to_operand_aliasing={{}: (3, {})} | custom-call | bytes 2621440 | tf_op jit(solution)/shard_map/pallas_call | solution.py:568
  128.3 10.3 %collective-permute-done.12.two_ref = f32[5,8,16,256]{3,2,1,0:T(8,128)S(1)} collective-permute-done((f32[5,8,16,256]{3,2,1,0:T(8,128)S(1)}, f32[5,8,16,256]{3,2,1,0:T(8,128)S(1)}, u32[]{:S(2)}, u32[]{:S(2)}) %collective-permute-start.12) | collective-permute-done | bytes 655392 | tf_op jit(solution)/shard_map/ppermute | solution.py:694
  138.5 1.7 %shard_map.48 = f32[5,24,32,256]{3,2,1,0:T(8,128)} custom-call(s32[7]{0:T(128)S(1)} %get-tuple-element.28.flags_ref.refs_0_, f32[5,8,16,256]{3,2,1,0:T(8,128)S(1)} %get-tuple-element.43.one_ref, f32[5,8,16,256]{3,2,1,0:T(8,128)S(1)} %collective-permute-done.12.two_ref, f32[5,24,32,256]{3,2,1,0:T(8,128)} %shard_map.47.refs_0_), custom_call_target="tpu_custom_call", output_to_operand_aliasing={{}: (3, {})} | custom-call | bytes 2621440 | tf_op jit(solution)/shard_map/pallas_call | solution.py:568
  (31 shorter events, 0.2 us)
Async XLA Ops:
  0.1 2.1 %copy-start = (f32[5,24,32,256]{3,2,1,0:T(8,128)S(1)}, f32[5,24,32,256]{3,2,1,0:T(8,128)}, u32[]{:S(2)}) copy-start(f32[5,24,32,256]{3,2,1,0:T(8,128)} %refs_8_.1) | copy-start | bytes 11796484
  2.9 29.7 %collective-permute-start = (f32[5,16,16,256]{3,2,1,0:T(8,128)S(1)}, f32[5,16,16,256]{3,2,1,0:T(8,128)S(1)}, u32[]{:S(2)}, u32[]{:S(2)}) collective-permute-start(f32[5,16,16,256]{3,2,1,0:T(8,128)S(1)} %shard_map.37), channel_id=1, source_target_pairs={{0,16},{4,20},{8,24},{12,28},{16,0},{20,4},{24,8},{28,12},{1,17},{... | collective-permute-start | bytes 3932168 | tf_op jit(solution)/shard_map/ppermute | solution.py:639
  5.7 41.0 %collective-permute-start.1 = (f32[5,8,16,256]{3,2,1,0:T(8,128)}, f32[5,8,16,256]{3,2,1,0:T(8,128)S(1)}, u32[]{:S(2)}, u32[]{:S(2)}) collective-permute-start(f32[5,8,16,256]{3,2,1,0:T(8,128)} %shard_map.38), channel_id=1, source_target_pairs={{0,16},{4,20},{8,24},{12,28},{16,0},{20,4},{24,8},{28,12},{1,17},{... | collective-permute-start | bytes 1966088 | tf_op jit(solution)/shard_map/ppermute | solution.py:639
  6.9 1.2 copy-start.3
  8.1 1.2 copy-start.4
  32.6 2.1 %copy-start.1 = (f32[5,24,32,256]{3,2,1,0:T(8,128)S(1)}, f32[5,24,32,256]{3,2,1,0:T(8,128)}, u32[]{:S(2)}) copy-start(f32[5,24,32,256]{3,2,1,0:T(8,128)} %refs_8_.1) | copy-start | bytes 11796484
  34.8 25.7 %copy-start.2 = (f32[5,24,32,256]{3,2,1,0:T(8,128)S(1)}, f32[5,24,32,256]{3,2,1,0:T(8,128)}, u32[]{:S(2)}) copy-start(f32[5,24,32,256]{3,2,1,0:T(8,128)} %refs_8_.1) | copy-start | bytes 11796484
  35.9 24.5 %collective-permute-start.2 = (f32[5,16,4,256]{3,2,1,0:T(4,128)S(1)}, f32[5,16,4,256]{3,2,1,0:T(4,128)S(1)}, u32[]{:S(2)}, u32[]{:S(2)}) collective-permute-start(f32[5,16,4,256]{3,2,1,0:T(4,128)S(1)} %get-tuple-element.31), channel_id=1, source_target_pairs={{0,16},{16,20},{20,4},{4,8},{8,24},{24,28},{28,12},{12,0},{1,17},{... | collective-permute-start | bytes 983048 | tf_op jit(solution)/shard_map/ppermute | solution.py:642
  39.8 20.7 %collective-permute-start.4 = (f32[5,16,4,256]{3,2,1,0:T(4,128)S(1)}, f32[5,16,4,256]{3,2,1,0:T(4,128)S(1)}, u32[]{:S(2)}, u32[]{:S(2)}) collective-permute-start(f32[5,16,4,256]{3,2,1,0:T(4,128)S(1)} %get-tuple-element.33), channel_id=1, source_target_pairs={{0,12},{16,0},{20,16},{4,20},{8,4},{24,8},{28,24},{12,28},{1,13},{... | collective-permute-start | bytes 983048 | tf_op jit(solution)/shard_map/ppermute | solution.py:643
  47.5 9.7 %collective-permute-start.3 = (f32[5,8,4,256]{3,2,1,0:T(4,128)S(1)}, f32[5,8,4,256]{3,2,1,0:T(4,128)S(1)}, u32[]{:S(2)}, u32[]{:S(2)}) collective-permute-start(f32[5,8,4,256]{3,2,1,0:T(4,128)S(1)} %get-tuple-element.32), channel_id=1, source_target_pairs={{0,16},{16,20},{20,4},{4,8},{8,24},{24,28},{28,12},{12,0},{1,17},{... | collective-permute-start | bytes 491528 | tf_op jit(solution)/shard_map/ppermute | solution.py:642
  51.4 9.1 %collective-permute-start.5 = (f32[5,8,4,256]{3,2,1,0:T(4,128)S(1)}, f32[5,8,4,256]{3,2,1,0:T(4,128)S(1)}, u32[]{:S(2)}, u32[]{:S(2)}) collective-permute-start(f32[5,8,4,256]{3,2,1,0:T(4,128)S(1)} %get-tuple-element.34), channel_id=1, source_target_pairs={{0,12},{16,0},{20,16},{4,20},{8,4},{24,8},{28,24},{12,28},{1,13},{... | collective-permute-start | bytes 491528 | tf_op jit(solution)/shard_map/ppermute | solution.py:643
  51.4 18.2 %collective-permute-start.6 = (f32[2,5,2,16,256]{4,3,2,1,0:T(8,128)S(1)}, f32[2,5,2,16,256]{4,3,2,1,0:T(8,128)S(1)}, u32[]{:S(2)}, u32[]{:S(2)}) collective-permute-start(f32[2,5,2,16,256]{4,3,2,1,0:T(8,128)S(1)} %get-tuple-element.36), channel_id=1, source_target_pairs={{0,1},{1,0},{2,3},{3,2},{4,5},{5,4},{6,7},{7,6},{8,9},{9,8},{10,11... | collective-permute-start | bytes 983048 | tf_op jit(solution)/shard_map/ppermute | solution.py:646
  57.2 12.4 %collective-permute-start.7 = (f32[2,5,2,16,256]{4,3,2,1,0:T(8,128)S(1)}, f32[2,5,2,16,256]{4,3,2,1,0:T(8,128)S(1)}, u32[]{:S(2)}, u32[]{:S(2)}) collective-permute-start(f32[2,5,2,16,256]{4,3,2,1,0:T(8,128)S(1)} %get-tuple-element.37), channel_id=1, source_target_pairs={{0,0},{1,2},{2,1},{3,3},{4,4},{5,6},{6,5},{7,7},{8,8},{9,10},{10,9... | collective-permute-start | bytes 983048 | tf_op jit(solution)/shard_map/ppermute | solution.py:647
  67.4 11.9 %collective-permute-start.8 = (f32[5,12,4,256]{3,2,1,0:T(4,128)S(1)}, f32[5,12,4,256]{3,2,1,0:T(4,128)S(1)}, u32[]{:S(2)}, u32[]{:S(2)}) collective-permute-start(f32[5,12,4,256]{3,2,1,0:T(4,128)S(1)} %get-tuple-element.39), channel_id=1, source_target_pairs={{0,16},{16,20},{20,4},{4,8},{8,24},{24,28},{28,12},{12,0},{1,17},{... | collective-permute-start | bytes 737288 | tf_op jit(solution)/shard_map/ppermute | solution.py:642
  76.7 7.5 %collective-permute-start.9 = (f32[5,12,4,256]{3,2,1,0:T(4,128)S(1)}, f32[5,12,4,256]{3,2,1,0:T(4,128)S(1)}, u32[]{:S(2)}, u32[]{:S(2)}) collective-permute-start(f32[5,12,4,256]{3,2,1,0:T(4,128)S(1)} %get-tuple-element.40), channel_id=1, source_target_pairs={{0,16},{16,20},{20,4},{4,8},{8,24},{24,28},{28,12},{12,0},{1,17},{... | collective-permute-start | bytes 737288 | tf_op jit(solution)/shard_map/ppermute | solution.py:642
  79.3 6.8 %collective-permute-start.10 = (f32[5,12,4,256]{3,2,1,0:T(4,128)S(1)}, f32[5,12,4,256]{3,2,1,0:T(4,128)S(1)}, u32[]{:S(2)}, u32[]{:S(2)}) collective-permute-start(f32[5,12,4,256]{3,2,1,0:T(4,128)S(1)} %get-tuple-element.41), channel_id=1, source_target_pairs={{0,12},{16,0},{20,16},{4,20},{8,4},{24,8},{28,24},{12,28},{1,13},{... | collective-permute-start | bytes 737288 | tf_op jit(solution)/shard_map/ppermute | solution.py:643
  79.3 9.4 %collective-permute-start.11 = (f32[5,12,4,256]{3,2,1,0:T(4,128)S(1)}, f32[5,12,4,256]{3,2,1,0:T(4,128)S(1)}, u32[]{:S(2)}, u32[]{:S(2)}) collective-permute-start(f32[5,12,4,256]{3,2,1,0:T(4,128)S(1)} %get-tuple-element.42), channel_id=1, source_target_pairs={{0,12},{16,0},{20,16},{4,20},{8,4},{24,8},{28,24},{12,28},{1,13},{... | collective-permute-start | bytes 737288 | tf_op jit(solution)/shard_map/ppermute | solution.py:643
  79.3 15.0 %collective-permute-start.14 = (f32[2,5,2,16,256]{4,3,2,1,0:T(8,128)S(1)}, f32[2,5,2,16,256]{4,3,2,1,0:T(8,128)S(1)}, u32[]{:S(2)}, u32[]{:S(2)}) collective-permute-start(f32[2,5,2,16,256]{4,3,2,1,0:T(8,128)S(1)} %get-tuple-element.47), channel_id=1, source_target_pairs={{0,1},{1,0},{2,3},{3,2},{4,5},{5,4},{6,7},{7,6},{8,9},{9,8},{10,11... | collective-permute-start | bytes 983048 | tf_op jit(solution)/shard_map/ppermute | solution.py:646
  79.3 15.0 %collective-permute-start.15 = (f32[2,5,2,16,256]{4,3,2,1,0:T(8,128)S(1)}, f32[2,5,2,16,256]{4,3,2,1,0:T(8,128)S(1)}, u32[]{:S(2)}, u32[]{:S(2)}) collective-permute-start(f32[2,5,2,16,256]{4,3,2,1,0:T(8,128)S(1)} %get-tuple-element.48), channel_id=1, source_target_pairs={{0,0},{1,2},{2,1},{3,3},{4,4},{5,6},{6,5},{7,7},{8,8},{9,10},{10,9... | collective-permute-start | bytes 983048 | tf_op jit(solution)/shard_map/ppermute | solution.py:647
  93.9 32.6 %collective-permute-start.13 = (f32[5,8,16,256]{3,2,1,0:T(8,128)S(1)}, f32[5,8,16,256]{3,2,1,0:T(8,128)S(1)}, u32[]{:S(2)}, u32[]{:S(2)}) collective-permute-start(f32[5,8,16,256]{3,2,1,0:T(8,128)S(1)} %get-tuple-element.46), channel_id=1, source_target_pairs={{0,16},{4,20},{8,24},{12,28},{16,0},{20,4},{24,8},{28,12},{1,17},{... | collective-permute-start | bytes 1966088 | tf_op jit(solution)/shard_map/ppermute | solution.py:694
  99.7 25.1 %collective-permute-start.16 = (f32[5,8,16,256]{3,2,1,0:T(8,128)S(1)}, f32[5,8,16,256]{3,2,1,0:T(8,128)S(1)}, u32[]{:S(2)}, u32[]{:S(2)}) collective-permute-start(f32[5,8,16,256]{3,2,1,0:T(8,128)S(1)} %get-tuple-element.50), channel_id=1, source_target_pairs={{0,16},{4,20},{8,24},{12,28},{16,0},{20,4},{24,8},{28,12},{1,17},{... | collective-permute-start | bytes 1966088 | tf_op jit(solution)/shard_map/ppermute | solution.py:694
  106.1 32.4 %collective-permute-start.12 = (f32[5,8,16,256]{3,2,1,0:T(8,128)S(1)}, f32[5,8,16,256]{3,2,1,0:T(8,128)S(1)}, u32[]{:S(2)}, u32[]{:S(2)}) collective-permute-start(f32[5,8,16,256]{3,2,1,0:T(8,128)S(1)} %get-tuple-element.44), channel_id=1, source_target_pairs={{0,16},{4,20},{8,24},{12,28},{16,0},{20,4},{24,8},{28,12},{1,17},{... | collective-permute-start | bytes 1966088 | tf_op jit(solution)/shard_map/ppermute | solution.py:694

commit v4 on v3

--- a/solution.py
+++ b/solution.py
@@ -15,8 +15,8 @@
 scalars = pl.BlockSpec(memory_space=pltpu.SMEM)
 vector = pl.BlockSpec(memory_space=pltpu.VMEM)
 GROUP = 4
-TAILS = 2
-OUTER = 8
+TAILS = 3
+OUTER = 7
 SECTION_VMEM = 28 << 20
 COPY_VMEM = 8 << 20
 
@@ -219,6 +219,18 @@
         hi_s[u, f, :, lanes] = hi
         lo_s[u, f, :, lanes] = (value - hi.astype(jnp.float32)).astype(jnp.bfloat16)
 
+    def tip_value(s, f, tip):
+        high = tip[0] == "high"
+
+        def picked(pair, *at):
+            swapped, other = pair if high else pair[::-1]
+            return jnp.where(flags_ref[ODD] > 0, other[*at], swapped[*at])
+
+        if len(tip_in) == 2:
+            return picked(tip_in, s, f, tip[1])
+        near, far = picked(tip_in[:2], f, tip[1]), picked(tip_in[2:], f, tip[1])
+        return jnp.where(seg == s, near, far)
+
     def flux(at, u, flag):
         inner = u is not None
         tip = plan["tip"].get(at)
@@ -226,20 +238,27 @@
             wait_copies(q_wait[at])
         if inner:
             slot = u % 3
-            edge = []
-            for side, (array, start) in ((0, plan["left"][u]), (1, plan["right"][u])):
-                ref = (left_in, right_in)[side][array]
-                q = tuple(ref[f, start] for f in range(fields))
-                edge.append(angular_of(q, speeds(q), edge_table(0, side), edge_table(1, side)))
+            (array, start), (other, other_start) = plan["left"][u], plan["right"][u]
+            sides = [
+                tuple(left_in[array][f, start] for f in range(fields)),
+                tuple(right_in[other][f, other_start] for f in range(fields)),
+            ]
+            if plan["by_kind"]:
+                inner_edge, outer_edge = sides
+                upper = flags_ref[HALF] > 0
+                sides = [
+                    tuple(jnp.where(upper, i, o) for i, o in zip(inner_edge, outer_edge)),
+                    tuple(jnp.where(upper, o, i) for i, o in zip(inner_edge, outer_edge)),
+                ]
+            edge = [
+                angular_of(q, speeds(q), edge_table(0, side), edge_table(1, side))
+                for side, q in enumerate(sides)
+            ]
         for s in range(2):
             if tip is None:
                 q = tuple(q_s[s, f, at] for f in range(fields))
             else:
-                swap_tip, other_tip = (tip_in[0], tip_in[1]) if tip[0] == "high" else (tip_in[1], tip_in[0])
-                q = tuple(
-                    jnp.where(flags_ref[ODD] > 0, other_tip[s, f, tip[1]], swap_tip[s, f, tip[1]])
-                    for f in range(fields)
-                )
+                q = tuple(tip_value(s, f, tip) for f in range(fields))
             state = speeds(q)
             axial = axial_of(q, state, axial_scale)
             for f in range(fields):
@@ -394,7 +413,7 @@
         low_flag=next((i for i, r in enumerate(ranges) if r[0] == 0), None),
         high_flag=next((i for i, r in enumerate(ranges) if r[1] == planes), None),
         q=q_spans, tip={at: ("low" if p < 0 else "high", p + 2 if p < 0 else p - planes) for at, p in tips_at.items()},
-        table=table_row,
+        table=table_row, by_kind=not mixed,
         base=pieces("base", base_map, tight) if mixed else [],
         left=[(index_of("left", left_map[p][0]), left_map[p][1]) for p in tight],
         right=[(index_of("right", right_map[p][0]), right_map[p][1]) for p in tight],
@@ -479,15 +498,15 @@
         )
         run_copies(loads[-1])
 
+    last_half, swapped = flags_ref[HALF], flags_ref[SWAP_LEFT] + flags_ref[SWAP_RIGHT]
+
     def edges(p, carry):
         for f in range(fields):
-            for ref, flag, start in (
-                (outs[0], flags_ref[SWAP_LEFT], 0), (outs[1], flags_ref[SWAP_RIGHT], rows - 2)
-            ):
-                one = q_s[0, f, p, start : start + 2]
-                two = q_s[1, f, p, start : start + 2]
-                ref[f, p, 0:2] = jnp.where(flag > 0, two, one)
-                ref[f, p, 2:4] = jnp.where(flag > 0, one, two)
+            one, two = (
+                jnp.where(last_half > 0, q_s[s, f, p, rows - 2 : rows], q_s[s, f, p, 0:2]) for s in range(2)
+            )
+            outs[0][f, p, 0:2] = jnp.where(swapped > 0, two, one)
+            outs[0][f, p, 2:4] = jnp.where(swapped > 0, one, two)
         return carry
 
     for i, (_, at, size) in enumerate(parts):
@@ -497,7 +516,7 @@
         last = jnp.where(flags_ref[ODD] > 0, 0, planes - 2)
         copies = [
             pltpu.make_async_copy(
-                q_s.at[:, :, pl.ds(start, 2)], outs[2 + i], sems.at[2 * len(parts) + i]
+                q_s.at[1 - seg, :, pl.ds(start, 2)], outs[1 + i], sems.at[2 * len(parts) + i]
             )
             for i, start in enumerate((last, planes - 2 - last))
         ]
@@ -509,10 +528,10 @@
     fields, rows, radii = dims
     planes = far.shape[1]
     f32 = jnp.float32
-    out_shape = [jax.ShapeDtypeStruct((fields, planes, 4, radii), f32)] * 2
-    out_specs = [vector, vector]
+    out_shape = [jax.ShapeDtypeStruct((fields, planes, 4, radii), f32)]
+    out_specs = [vector]
     if tips:
-        out_shape += [jax.ShapeDtypeStruct((2, fields, 2, rows, radii), f32)] * 2
+        out_shape += [jax.ShapeDtypeStruct((fields, 2, rows, radii), f32)] * 2
         out_specs += [anywhere] * 2
     return pl.pallas_call(
         functools.partial(edges_kernel, spans, tips),
@@ -600,6 +619,7 @@
     order = [((r % 2) ^ (r // 2 & 1)) * half + r // 2 for r in range(n)]
     to_left = [(order[r], order[(r - 1) % n]) for r in range(n)]
     to_right = [(order[r], order[(r + 1) % n]) for r in range(n)]
+    beside = [(order[r], order[(r + 1 if r % 2 else r - 1) % n]) for r in range(n)]
 
     def layer_swap(first):
         table = {i: i for i in range(count)}
@@ -655,6 +675,23 @@
         return table
 
     sent_outer = send(span_outer)
+    low_rows, high_rows = conserved[:, :, rows - 2 : rows], conserved[:, :, rows : rows + 2]
+    far_rows = lax.ppermute(jnp.where(kept == 0, low_rows, high_rows), "ang", across)
+    own_rows = jnp.where(kept == 0, high_rows, low_rows)
+    inner_rows = jnp.concatenate(
+        [jnp.where(h == 0, own_rows, far_rows), jnp.where(h == 0, far_rows, own_rows)], axis=2
+    )
+
+    def own_tip(start):
+        block = conserved[:, start : start + 2]
+        return jnp.where(kept == 0, block[:, :, :rows], block[:, :, rows:])
+
+    own_low, own_high = own_tip(0), own_tip(planes - 2)
+    odd_layer = layer % 2 == 1
+    near_tips = (
+        lax.ppermute(jnp.where(odd_layer, own_low, own_high), "ax", layer_swap(0)),
+        lax.ppermute(jnp.where(odd_layer, own_high, own_low), "ax", layer_swap(1)),
+    )
     sent_inner = send(span_inner)
 
     flags, whi, wlo = prepare(flags, filter_matrix, deriv_matrix, table, radius)
@@ -673,22 +710,20 @@
             right_map, flags, planes, dims, final, tips,
         )
 
-    left_o, right_o, tip_one, tip_two = edges_task(span_outer, True, flags, conserved, sent_outer, dims)
-    halo_left, halo_right = trade(left_o, right_o)
+    edge_o, tip_one, tip_two = edges_task(span_outer, True, flags, conserved, sent_outer, dims)
     q_map = listed((conserved, sent_outer), ro)
-    q_map["tips"] = trade_tips(tip_one, tip_two)
-    lefts, rights = listed(halo_left, ro), listed(halo_right, ro)
+    q_map["tips"] = near_tips + trade_tips(tip_one, tip_two)
+    lefts = listed(inner_rows, ((0, planes),))
+    rights = listed(lax.ppermute(edge_o, "ang", beside), ro)
     f_o, left_f, right_f, tip_one, tip_two = section(1.0, one_o, (q_map, lefts, rights), None, tips=True)
     halo_left, halo_right = trade(left_f, right_f)
     f_map = listed(f_o, one_o)
     f_map["tips"] = trade_tips(tip_one, tip_two)
     f_lefts, f_rights = listed(halo_left, one_o), listed(halo_right, one_o)
 
-    left_i, right_i = edges_task(span_inner, False, flags, conserved, sent_inner, dims)
-    halo_left, halo_right = trade(left_i, right_i)
+    (edge_i,) = edges_task(span_inner, False, flags, conserved, sent_inner, dims)
     q_map.update(listed((conserved, sent_inner), ri))
-    lefts.update(listed(halo_left, ri))
-    rights.update(listed(halo_right, ri))
+    rights.update(listed(lax.ppermute(edge_i, "ang", beside), ri))
 
     def give_back(near, far):
         return near, lax.ppermute(far, "ang", across)

time: 141 us -> 146 us (1.035)
  the two profiles are of different devices: /device:TPU:9 before, /device:TPU:0 now
where the time goes in v4:
time: 146 us; the launch traced here: 145 us
  waiting for transfers between devices  64.2 us (44%)
  Pallas kernels  47 us (32%)
  starting transfers between devices  20.4 us (14%)
  local copies, waits for them, and re-layouts  7.39 us (5%)
  other arithmetic  5.99 us (4%)
    pallas_call x6, Pallas kernels, section_task(): pl.pallas_call(functools.partial(section_kernel, plan, factor), out_shape...  32.2 us
    ppermute x2, waiting for transfers between devices, send(): return lax.ppermute(block, 'ang', across)  30.8 us
    ppermute x4, waiting for transfers between devices, give_back(): return (near, lax.ppermute(far, 'ang', across))  22.4 us
    unnamed x10, local copies, waits for them, and re-layouts  6.68 us
    pallas_call x4, Pallas kernels, place_task(): pl.pallas_call(functools.partial(place_kernel, spans, whole is not None),...  6.61 us
    ppermute x1, waiting for transfers between devices, per_device(): rights = listed(lax.ppermute(edge_o, 'ang', beside), ro)  6.57 us
    ppermute x2, waiting for transfers between devices, trade(): left = lax.ppermute(right_edge, 'ang', to_right)  4.39 us
    ppermute x4, starting transfers between devices, give_back(): return (near, lax.ppermute(far, 'ang', across))  4.31 us
  transfers between devices with their start and end apart: 19, of which 6 were waited for; matrix products, arithmetic and copies ran while one was open for 3% of the time, Pallas kernels for 31%

profile of v4, /device:TPU:0, one launch (start us, length us, event | category | flops | bytes accessed | tf_op | source)
XLA Modules:
  0.0 145.4 jit_solution(16103991646901319653)
XLA Ops:
  0.0 2.3 %broadcast_select_fusion = f32[5,24,2,256]{3,2,1,0:T(2,128)} fusion(pred[]{:T(512)S(6)} %eq.41, f32[5,24,32,256]{3,2,1,0:T(8,128)} %refs_8_.1), kind=kLoop, calls=%fused_computation.1 | loop fusion | flops 61440 | bytes 737281 | tf_op jit(solution)/shard_map/jit(_where)/select_n | solution.py:679
  2.3 3.0 %collective-permute-start.2 = (f32[5,24,2,256]{3,2,1,0:T(2,128)}, f32[5,24,2,256]{3,2,1,0:T(2,128)}, u32[]{:S(2)}, u32[]{:S(2)}) collective-permute-start(f32[5,24,2,256]{3,2,1,0:T(2,128)} %broadcast_select_fusion), channel_id=1, source_target_pairs={{0,16},{4,20},{8,24},{12,28},{16,0},{20,4},{24,8},{28,12},{1,17},{... | collective-permute-start | bytes 737288 | tf_op jit(solution)/shard_map/ppermute | solution.py:679
  5.3 1.9 %broadcast_select_fusion.4 = (f32[5,2,16,256]{3,2,1,0:T(8,128)}, f32[5,2,16,256]{3,2,1,0:T(8,128)}) fusion(pred[]{:T(512)} %eq.38, f32[5,24,32,256]{3,2,1,0:T(8,128)} %refs_8_.1, pred[]{:T(512)S(6)} %eq.41), kind=kLoop, calls=%fused_computation.7 | loop fusion | flops 163840 | bytes 983042 | tf_op jit(solution)/shard_map/jit(_where)/select_n | solution.py:693
  7.3 1.6 %collective-permute-start.6 = (f32[5,2,16,256]{3,2,1,0:T(8,128)}, f32[5,2,16,256]{3,2,1,0:T(8,128)S(1)}, u32[]{:S(2)}, u32[]{:S(2)}) collective-permute-start(f32[5,2,16,256]{3,2,1,0:T(8,128)} %get-tuple-element.51), channel_id=1, source_target_pairs={{0,0},{1,2},{2,1},{3,3},{4,4},{5,6},{6,5},{7,7},{8,8},{9,10},{10,9... | collective-permute-start | bytes 491528 | tf_op jit(solution)/shard_map/ppermute | solution.py:693
  8.8 3.6 %collective-permute-start.5 = (f32[5,2,16,256]{3,2,1,0:T(8,128)}, f32[5,2,16,256]{3,2,1,0:T(8,128)S(1)}, u32[]{:S(2)}, u32[]{:S(2)}) collective-permute-start(f32[5,2,16,256]{3,2,1,0:T(8,128)} %get-tuple-element.52), channel_id=1, source_target_pairs={{0,1},{1,0},{2,3},{3,2},{4,5},{5,4},{6,7},{7,6},{8,9},{9,8},{10,11... | collective-permute-start | bytes 491528 | tf_op jit(solution)/shard_map/ppermute | solution.py:692
  12.4 0.1 stack.56
  12.5 2.1 %copy-done = f32[5,24,32,256]{3,2,1,0:T(8,128)S(1)} copy-done((f32[5,24,32,256]{3,2,1,0:T(8,128)S(1)}, f32[5,24,32,256]{3,2,1,0:T(8,128)}, u32[]{:S(2)}) %copy-start) | copy-done | bytes 3932184
  14.6 1.5 %shard_map.38 = f32[5,10,16,256]{3,2,1,0:T(8,128)} custom-call(s32[7]{0:T(128)S(1)} %convert_element_type.80.flags_ref, f32[5,24,32,256]{3,2,1,0:T(8,128)S(1)} %copy-done), custom_call_target="tpu_custom_call" | custom-call | bytes 1638400 | tf_op jit(solution)/shard_map/pallas_call | solution.py:93
  16.2 0.6 collective-permute-start.1
  16.7 0.7 shard_map.37
  17.5 1.6 %collective-permute-start = (f32[5,14,16,256]{3,2,1,0:T(8,128)S(1)}, f32[5,14,16,256]{3,2,1,0:T(8,128)S(1)}, u32[]{:S(2)}, u32[]{:S(2)}) collective-permute-start(f32[5,14,16,256]{3,2,1,0:T(8,128)S(1)} %shard_map.37), channel_id=1, source_target_pairs={{0,16},{4,20},{8,24},{12,28},{16,0},{20,4},{24,8},{28,12},{1,17},{... | collective-permute-start | bytes 3440648 | tf_op jit(solution)/shard_map/ppermute | solution.py:659
  19.2 0.1 fusion.12
  19.9 0.1 broadcast_in_dim.2.table_ref.refs_1_
  20.0 1.2 copy-done.3
  21.2 1.2 copy-done.4
  22.4 3.7 %prepare.1 = (s32[7]{0:T(128)S(1)}, bf16[1024,512]{1,0:T(8,128)(2,1)S(1)}, bf16[1024,512]{1,0:T(8,128)(2,1)S(1)}) custom-call(s32[7]{0:T(128)S(1)} %convert_element_type.80.flags_ref, f32[512,512]{1,0:T(8,128)S(1)} %copy-done.3, f32[512,512]{1,0:T(8,128)S(1)} %copy-done.4, f32[320,128]{1,0:T(8,128)S(1)} %broadcast_in_dim.2.table_ref.refs_1_, ...), custom_call_target="tpu_custom_call" | custom-call | tf_op jit(solution)/shard_map/prepare/pallas_call | solution.py:65
  26.2 11.4 %collective-permute-done.1.far_ref.refs_8_.refs_7_.refs_10_ = f32[5,10,16,256]{3,2,1,0:T(8,128)S(1)} collective-permute-done((f32[5,10,16,256]{3,2,1,0:T(8,128)}, f32[5,10,16,256]{3,2,1,0:T(8,128)S(1)}, u32[]{:S(2)}, u32[]{:S(2)}) %collective-permute-start.1) | collective-permute-done | bytes 819232 | tf_op jit(solution)/shard_map/ppermute | solution.py:659
  37.6 2.1 %copy-done.1 = f32[5,24,32,256]{3,2,1,0:T(8,128)S(1)} copy-done((f32[5,24,32,256]{3,2,1,0:T(8,128)S(1)}, f32[5,24,32,256]{3,2,1,0:T(8,128)}, u32[]{:S(2)}) %copy-start.1) | copy-done | bytes 3932184
  39.7 1.0 shard_map.40
  40.7 19.4 %collective-permute-done.far_ref.refs_6_.refs_10_.refs_8_.refs_9_ = f32[5,14,16,256]{3,2,1,0:T(8,128)S(1)} collective-permute-done((f32[5,14,16,256]{3,2,1,0:T(8,128)S(1)}, f32[5,14,16,256]{3,2,1,0:T(8,128)S(1)}, u32[]{:S(2)}, u32[]{:S(2)}) %collective-permute-start) | collective-permute-done | bytes 1146912 | tf_op jit(solution)/shard_map/ppermute | solution.py:659
  60.2 1.3 shard_map.39
  61.5 1.2 broadcast_select_fusion.3
  62.7 0.2 pad_maximum_fusion.refs_9_.refs_11_
  63.0 0.4 collective-permute-start.7
  63.4 0.7 collective-permute-start.8
  64.0 6.6 %collective-permute-done.3.refs_10_.refs_12_ = f32[5,14,4,256]{3,2,1,0:T(4,128)S(1)} collective-permute-done((f32[5,14,4,256]{3,2,1,0:T(4,128)S(1)}, f32[5,14,4,256]{3,2,1,0:T(4,128)S(1)}, u32[]{:S(2)}, u32[]{:S(2)}) %collective-permute-start.3) | collective-permute-done | bytes 286752 | tf_op jit(solution)/shard_map/ppermute | solution.py:717
  70.6 8.1 %shard_map.41 = (f32[2,5,14,16,256]{4,3,2,1,0:T(8,128)S(1)}, f32[5,14,4,256]{3,2,1,0:T(4,128)S(1)}, f32[5,14,4,256]{3,2,1,0:T(4,128)S(1)}) custom-call(s32[7]{0:T(128)S(1)} %get-tuple-element.27.flags_ref.refs_0_, f32[320,128]{1,0:T(8,128)S(1)} %broadcast_in_dim.2.table_ref.refs_1_, f32[1,256]{1,0:T(1,128)S(1)} %add_multiply_fusion.radius_ref.refs_2_, ...), custom_call_target="tpu_custom_call" | custom-call | flops 7046430720 | bytes 9175040 | tf_op jit(solution)/shard_map/pallas_call | solution.py:447
  78.7 1.7 %collective-permute-start.11 = (f32[5,14,4,256]{3,2,1,0:T(4,128)S(1)}, f32[5,14,4,256]{3,2,1,0:T(4,128)S(1)}, u32[]{:S(2)}, u32[]{:S(2)}) collective-permute-start(f32[5,14,4,256]{3,2,1,0:T(4,128)S(1)} %get-tuple-element.37), channel_id=1, source_target_pairs={{0,12},{16,0},{20,16},{4,20},{8,4},{24,8},{28,24},{12,28},{1,13},{... | collective-permute-start | bytes 860168 | tf_op jit(solution)/shard_map/ppermute | solution.py:663
  80.5 6.4 %shard_map.42 = (f32[2,5,10,16,256]{4,3,2,1,0:T(8,128)S(1)}, f32[5,10,4,256]{3,2,1,0:T(4,128)S(1)}, f32[5,10,4,256]{3,2,1,0:T(4,128)S(1)}, f32[2,5,2,16,256]{4,3,2,1,0:T(8,128)S(1)}, f32[2,5,2,16,256]{4,3,2,1,0:T(8,128)S(1)}) custom-call(s32[7]{0:T(128)S(1)} %get-tuple-element.27.flags_ref.refs_0_, f32[320,128]{1,0:T(8,128)S(1)} %broadcast_in_dim.2.table_ref.refs_1_, ...), custom_call_target="tpu_custom_call" | custom-call | flops 5033164800 | bytes 6553600 | tf_op jit(solution)/shard_map/pallas_call | solution.py:447
  86.9 0.6 collective-permute-start.10
  87.5 1.2 collective-permute-start.12
  88.7 0.3 collective-permute-start.16
  89.0 4.4 %collective-permute-done.10.refs_12_.refs_11_.refs_10_ = f32[5,10,4,256]{3,2,1,0:T(4,128)S(1)} collective-permute-done((f32[5,10,4,256]{3,2,1,0:T(4,128)S(1)}, f32[5,10,4,256]{3,2,1,0:T(4,128)S(1)}, u32[]{:S(2)}, u32[]{:S(2)}) %collective-permute-start.10) | collective-permute-done | bytes 204832 | tf_op jit(solution)/shard_map/ppermute | solution.py:662
  93.4 0.7 collective-permute-start.17
  94.1 4.4 %shard_map.45 = (f32[5,6,16,256]{3,2,1,0:T(8,128)S(1)}, f32[5,6,16,256]{3,2,1,0:T(8,128)S(1)}) custom-call(s32[7]{0:T(128)S(1)} %get-tuple-element.27.flags_ref.refs_0_, f32[320,128]{1,0:T(8,128)S(1)} %broadcast_in_dim.2.table_ref.refs_1_, f32[1,256]{1,0:T(1,128)S(1)} %add_multiply_fusion.radius_ref.refs_2_, ...), custom_call_target="tpu_custom_call" | custom-call | flops 3019898880 | bytes 3932160 | tf_op jit(solution)/shard_map/pallas_call | solution.py:447
  98.5 2.0 %collective-permute-start.15 = (f32[5,6,16,256]{3,2,1,0:T(8,128)S(1)}, f32[5,6,16,256]{3,2,1,0:T(8,128)S(1)}, u32[]{:S(2)}, u32[]{:S(2)}) collective-permute-start(f32[5,6,16,256]{3,2,1,0:T(8,128)S(1)} %get-tuple-element.44), channel_id=1, source_target_pairs={{0,16},{4,20},{8,24},{12,28},{16,0},{20,4},{24,8},{28,12},{1,17},{... | collective-permute-start | bytes 1474568 | tf_op jit(solution)/shard_map/ppermute | solution.py:729
  100.5 4.3 %shard_map.44 = (f32[5,6,16,256]{3,2,1,0:T(8,128)S(1)}, f32[5,6,16,256]{3,2,1,0:T(8,128)S(1)}) custom-call(s32[7]{0:T(128)S(1)} %get-tuple-element.27.flags_ref.refs_0_, f32[320,128]{1,0:T(8,128)S(1)} %broadcast_in_dim.2.table_ref.refs_1_, f32[1,256]{1,0:T(1,128)S(1)} %add_multiply_fusion.radius_ref.refs_2_, ...), custom_call_target="tpu_custom_call" | custom-call | flops 3019898880 | bytes 3932160 | tf_op jit(solution)/shard_map/pallas_call | solution.py:447
  104.9 0.1 collective-permute-start.14
  105.0 4.7 %shard_map.46 = (f32[5,6,16,256]{3,2,1,0:T(8,128)S(1)}, f32[5,6,16,256]{3,2,1,0:T(8,128)S(1)}) custom-call(s32[7]{0:T(128)S(1)} %get-tuple-element.27.flags_ref.refs_0_, f32[320,128]{1,0:T(8,128)S(1)} %broadcast_in_dim.2.table_ref.refs_1_, f32[1,256]{1,0:T(1,128)S(1)} %add_multiply_fusion.radius_ref.refs_2_, ...), custom_call_target="tpu_custom_call" | custom-call | flops 3019898880 | bytes 3932160 | tf_op jit(solution)/shard_map/pallas_call | solution.py:447
  109.7 2.0 %collective-permute-start.18 = (f32[5,6,16,256]{3,2,1,0:T(8,128)S(1)}, f32[5,6,16,256]{3,2,1,0:T(8,128)S(1)}, u32[]{:S(2)}, u32[]{:S(2)}) collective-permute-start(f32[5,6,16,256]{3,2,1,0:T(8,128)S(1)} %get-tuple-element.48), channel_id=1, source_target_pairs={{0,16},{4,20},{8,24},{12,28},{16,0},{20,4},{24,8},{28,12},{1,17},{... | collective-permute-start | bytes 1474568 | tf_op jit(solution)/shard_map/ppermute | solution.py:729
  111.7 4.3 %shard_map.43 = (f32[5,6,16,256]{3,2,1,0:T(8,128)S(1)}, f32[5,6,16,256]{3,2,1,0:T(8,128)S(1)}) custom-call(s32[7]{0:T(128)S(1)} %get-tuple-element.27.flags_ref.refs_0_, f32[320,128]{1,0:T(8,128)S(1)} %broadcast_in_dim.2.table_ref.refs_1_, f32[1,256]{1,0:T(1,128)S(1)} %add_multiply_fusion.radius_ref.refs_2_, ...), custom_call_target="tpu_custom_call" | custom-call | flops 3019898880 | bytes 3932160 | tf_op jit(solution)/shard_map/pallas_call | solution.py:447
  116.1 0.1 collective-permute-start.13
  116.2 17.5 %collective-permute-done.18.two_ref = f32[5,6,16,256]{3,2,1,0:T(8,128)S(1)} collective-permute-done((f32[5,6,16,256]{3,2,1,0:T(8,128)S(1)}, f32[5,6,16,256]{3,2,1,0:T(8,128)S(1)}, u32[]{:S(2)}, u32[]{:S(2)}) %collective-permute-start.18) | collective-permute-done | bytes 491552 | tf_op jit(solution)/shard_map/ppermute | solution.py:729
  133.7 1.7 %shard_map.47.refs_0_ = f32[5,24,32,256]{3,2,1,0:T(8,128)} custom-call(s32[7]{0:T(128)S(1)} %get-tuple-element.27.flags_ref.refs_0_, f32[5,6,16,256]{3,2,1,0:T(8,128)S(1)} %get-tuple-element.47.one_ref, f32[5,6,16,256]{3,2,1,0:T(8,128)S(1)} %collective-permute-done.18.two_ref), custom_call_target="tpu_custom_call" | custom-call | bytes 1966080 | tf_op jit(solution)/shard_map/pallas_call | solution.py:587
  135.4 1.6 %shard_map.48.refs_0_ = f32[5,24,32,256]{3,2,1,0:T(8,128)} custom-call(s32[7]{0:T(128)S(1)} %get-tuple-element.27.flags_ref.refs_0_, f32[5,6,16,256]{3,2,1,0:T(8,128)S(1)} %get-tuple-element.43.one_ref, f32[5,6,16,256]{3,2,1,0:T(8,128)S(1)} %collective-permute-done.15.two_ref, f32[5,24,32,256]{3,2,1,0:T(8,128)} %shard_map.47.refs_0_), custom_call_target="tpu_custom_call", output_to_operand_aliasing={{}: (3, {})} | custom-call | bytes 1966080 | tf_op jit(solution)/shard_map/pallas_call | solution.py:587
  137.1 1.6 %shard_map.49.refs_0_ = f32[5,24,32,256]{3,2,1,0:T(8,128)} custom-call(s32[7]{0:T(128)S(1)} %get-tuple-element.27.flags_ref.refs_0_, f32[5,6,16,256]{3,2,1,0:T(8,128)S(1)} %get-tuple-element.41.one_ref, f32[5,6,16,256]{3,2,1,0:T(8,128)S(1)} %collective-permute-done.14.two_ref, f32[5,24,32,256]{3,2,1,0:T(8,128)} %shard_map.48.refs_0_), custom_call_target="tpu_custom_call", output_to_operand_aliasing={{}: (3, {})} | custom-call | bytes 1966080 | tf_op jit(solution)/shard_map/pallas_call | solution.py:587
  138.7 4.9 %collective-permute-done.13.two_ref = f32[5,6,16,256]{3,2,1,0:T(8,128)S(1)} collective-permute-done((f32[5,6,16,256]{3,2,1,0:T(8,128)S(1)}, f32[5,6,16,256]{3,2,1,0:T(8,128)S(1)}, u32[]{:S(2)}, u32[]{:S(2)}) %collective-permute-start.13) | collective-permute-done | bytes 491552 | tf_op jit(solution)/shard_map/ppermute | solution.py:729
  143.6 1.6 %shard_map.50 = f32[5,24,32,256]{3,2,1,0:T(8,128)} custom-call(s32[7]{0:T(128)S(1)} %get-tuple-element.27.flags_ref.refs_0_, f32[5,6,16,256]{3,2,1,0:T(8,128)S(1)} %get-tuple-element.39.one_ref, f32[5,6,16,256]{3,2,1,0:T(8,128)S(1)} %collective-permute-done.13.two_ref, f32[5,24,32,256]{3,2,1,0:T(8,128)} %shard_map.49.refs_0_), custom_call_target="tpu_custom_call", output_to_operand_aliasing={{}: (3, {})} | custom-call | bytes 1966080 | tf_op jit(solution)/shard_map/pallas_call | solution.py:587
  (41 shorter events, 1.0 us)
Async XLA Ops:
  2.3 59.2 %collective-permute-start.2 = (f32[5,24,2,256]{3,2,1,0:T(2,128)}, f32[5,24,2,256]{3,2,1,0:T(2,128)}, u32[]{:S(2)}, u32[]{:S(2)}) collective-permute-start(f32[5,24,2,256]{3,2,1,0:T(2,128)} %broadcast_select_fusion), channel_id=1, source_target_pairs={{0,16},{4,20},{8,24},{12,28},{16,0},{20,4},{24,8},{28,12},{1,17},{... | collective-permute-start | bytes 737288 | tf_op jit(solution)/shard_map/ppermute | solution.py:679
  7.3 71.5 %collective-permute-start.6 = (f32[5,2,16,256]{3,2,1,0:T(8,128)}, f32[5,2,16,256]{3,2,1,0:T(8,128)S(1)}, u32[]{:S(2)}, u32[]{:S(2)}) collective-permute-start(f32[5,2,16,256]{3,2,1,0:T(8,128)} %get-tuple-element.51), channel_id=1, source_target_pairs={{0,0},{1,2},{2,1},{3,3},{4,4},{5,6},{6,5},{7,7},{8,8},{9,10},{10,9... | collective-permute-start | bytes 491528 | tf_op jit(solution)/shard_map/ppermute | solution.py:693
  8.8 71.6 %collective-permute-start.5 = (f32[5,2,16,256]{3,2,1,0:T(8,128)}, f32[5,2,16,256]{3,2,1,0:T(8,128)S(1)}, u32[]{:S(2)}, u32[]{:S(2)}) collective-permute-start(f32[5,2,16,256]{3,2,1,0:T(8,128)} %get-tuple-element.52), channel_id=1, source_target_pairs={{0,1},{1,0},{2,3},{3,2},{4,5},{5,4},{6,7},{7,6},{8,9},{9,8},{10,11... | collective-permute-start | bytes 491528 | tf_op jit(solution)/shard_map/ppermute | solution.py:692
  12.5 2.1 %copy-start = (f32[5,24,32,256]{3,2,1,0:T(8,128)S(1)}, f32[5,24,32,256]{3,2,1,0:T(8,128)}, u32[]{:S(2)}) copy-start(f32[5,24,32,256]{3,2,1,0:T(8,128)} %refs_8_.1) | copy-start | bytes 11796484
  16.2 21.4 %collective-permute-start.1 = (f32[5,10,16,256]{3,2,1,0:T(8,128)}, f32[5,10,16,256]{3,2,1,0:T(8,128)S(1)}, u32[]{:S(2)}, u32[]{:S(2)}) collective-permute-start(f32[5,10,16,256]{3,2,1,0:T(8,128)} %shard_map.38), channel_id=1, source_target_pairs={{0,16},{4,20},{8,24},{12,28},{16,0},{20,4},{24,8},{28,12},{1,17},{... | collective-permute-start | bytes 2457608 | tf_op jit(solution)/shard_map/ppermute | solution.py:659
  17.5 42.7 %collective-permute-start = (f32[5,14,16,256]{3,2,1,0:T(8,128)S(1)}, f32[5,14,16,256]{3,2,1,0:T(8,128)S(1)}, u32[]{:S(2)}, u32[]{:S(2)}) collective-permute-start(f32[5,14,16,256]{3,2,1,0:T(8,128)S(1)} %shard_map.37), channel_id=1, source_target_pairs={{0,16},{4,20},{8,24},{12,28},{16,0},{20,4},{24,8},{28,12},{1,17},{... | collective-permute-start | bytes 3440648 | tf_op jit(solution)/shard_map/ppermute | solution.py:659
  20.0 1.2 copy-start.3
  21.2 1.2 copy-start.4
  37.6 2.1 %copy-start.1 = (f32[5,24,32,256]{3,2,1,0:T(8,128)S(1)}, f32[5,24,32,256]{3,2,1,0:T(8,128)}, u32[]{:S(2)}) copy-start(f32[5,24,32,256]{3,2,1,0:T(8,128)} %refs_8_.1) | copy-start | bytes 11796484
  39.7 21.9 %copy-start.2 = (f32[5,24,32,256]{3,2,1,0:T(8,128)S(1)}, f32[5,24,32,256]{3,2,1,0:T(8,128)}, u32[]{:S(2)}) copy-start(f32[5,24,32,256]{3,2,1,0:T(8,128)} %refs_8_.1) | copy-start | bytes 11796484
  40.6 22.7 %collective-permute-start.4 = (f32[5,10,4,256]{3,2,1,0:T(4,128)S(1)}, f32[5,10,4,256]{3,2,1,0:T(4,128)S(1)}, u32[]{:S(2)}, u32[]{:S(2)}) collective-permute-start(f32[5,10,4,256]{3,2,1,0:T(4,128)S(1)} %shard_map.40), channel_id=1, source_target_pairs={{0,12},{16,20},{20,16},{4,8},{8,4},{24,28},{28,24},{12,0},{1,13},{... | collective-permute-start | bytes 614408 | tf_op jit(solution)/shard_map/ppermute | solution.py:726
  61.4 9.1 %collective-permute-start.3 = (f32[5,14,4,256]{3,2,1,0:T(4,128)S(1)}, f32[5,14,4,256]{3,2,1,0:T(4,128)S(1)}, u32[]{:S(2)}, u32[]{:S(2)}) collective-permute-start(f32[5,14,4,256]{3,2,1,0:T(4,128)S(1)} %get-tuple-element.30), channel_id=1, source_target_pairs={{0,12},{16,20},{20,16},{4,8},{8,4},{24,28},{28,24},{12,0},{1,13},{... | collective-permute-start | bytes 860168 | tf_op jit(solution)/shard_map/ppermute | solution.py:717
  63.0 17.5 %collective-permute-start.7 = (f32[5,2,16,256]{3,2,1,0:T(8,128)S(1)}, f32[5,2,16,256]{3,2,1,0:T(8,128)S(1)}, u32[]{:S(2)}, u32[]{:S(2)}) collective-permute-start(f32[5,2,16,256]{3,2,1,0:T(8,128)S(1)} %get-tuple-element.32), channel_id=1, source_target_pairs={{0,1},{1,0},{2,3},{3,2},{4,5},{5,4},{6,7},{7,6},{8,9},{9,8},{10,11... | collective-permute-start | bytes 491528 | tf_op jit(solution)/shard_map/ppermute | solution.py:666
  63.4 17.1 %collective-permute-start.8 = (f32[5,2,16,256]{3,2,1,0:T(8,128)S(1)}, f32[5,2,16,256]{3,2,1,0:T(8,128)S(1)}, u32[]{:S(2)}, u32[]{:S(2)}) collective-permute-start(f32[5,2,16,256]{3,2,1,0:T(8,128)S(1)} %get-tuple-element.33), channel_id=1, source_target_pairs={{0,0},{1,2},{2,1},{3,3},{4,4},{5,6},{6,5},{7,7},{8,8},{9,10},{10,9... | collective-permute-start | bytes 491528 | tf_op jit(solution)/shard_map/ppermute | solution.py:667
  78.7 15.4 %collective-permute-start.9 = (f32[5,14,4,256]{3,2,1,0:T(4,128)S(1)}, f32[5,14,4,256]{3,2,1,0:T(4,128)S(1)}, u32[]{:S(2)}, u32[]{:S(2)}) collective-permute-start(f32[5,14,4,256]{3,2,1,0:T(4,128)S(1)} %get-tuple-element.35), channel_id=1, source_target_pairs={{0,16},{16,20},{20,4},{4,8},{8,24},{24,28},{28,12},{12,0},{1,17},{... | collective-permute-start | bytes 860168 | tf_op jit(solution)/shard_map/ppermute | solution.py:662
  78.7 15.4 %collective-permute-start.11 = (f32[5,14,4,256]{3,2,1,0:T(4,128)S(1)}, f32[5,14,4,256]{3,2,1,0:T(4,128)S(1)}, u32[]{:S(2)}, u32[]{:S(2)}) collective-permute-start(f32[5,14,4,256]{3,2,1,0:T(4,128)S(1)} %get-tuple-element.37), channel_id=1, source_target_pairs={{0,12},{16,0},{20,16},{4,20},{8,4},{24,8},{28,24},{12,28},{1,13},{... | collective-permute-start | bytes 860168 | tf_op jit(solution)/shard_map/ppermute | solution.py:663
  86.9 6.5 %collective-permute-start.10 = (f32[5,10,4,256]{3,2,1,0:T(4,128)S(1)}, f32[5,10,4,256]{3,2,1,0:T(4,128)S(1)}, u32[]{:S(2)}, u32[]{:S(2)}) collective-permute-start(f32[5,10,4,256]{3,2,1,0:T(4,128)S(1)} %get-tuple-element.36), channel_id=1, source_target_pairs={{0,16},{16,20},{20,4},{4,8},{8,24},{24,28},{28,12},{12,0},{1,17},{... | collective-permute-start | bytes 614408 | tf_op jit(solution)/shard_map/ppermute | solution.py:662
  87.5 6.6 %collective-permute-start.12 = (f32[5,10,4,256]{3,2,1,0:T(4,128)S(1)}, f32[5,10,4,256]{3,2,1,0:T(4,128)S(1)}, u32[]{:S(2)}, u32[]{:S(2)}) collective-permute-start(f32[5,10,4,256]{3,2,1,0:T(4,128)S(1)} %get-tuple-element.38), channel_id=1, source_target_pairs={{0,12},{16,0},{20,16},{4,20},{8,4},{24,8},{28,24},{12,28},{1,13},{... | collective-permute-start | bytes 614408 | tf_op jit(solution)/shard_map/ppermute | solution.py:663
  88.7 16.3 %collective-permute-start.16 = (f32[2,5,2,16,256]{4,3,2,1,0:T(8,128)S(1)}, f32[2,5,2,16,256]{4,3,2,1,0:T(8,128)S(1)}, u32[]{:S(2)}, u32[]{:S(2)}) collective-permute-start(f32[2,5,2,16,256]{4,3,2,1,0:T(8,128)S(1)} %get-tuple-element.45), channel_id=1, source_target_pairs={{0,1},{1,0},{2,3},{3,2},{4,5},{5,4},{6,7},{7,6},{8,9},{9,8},{10,11... | collective-permute-start | bytes 983048 | tf_op jit(solution)/shard_map/ppermute | solution.py:666
  93.4 11.6 %collective-permute-start.17 = (f32[2,5,2,16,256]{4,3,2,1,0:T(8,128)S(1)}, f32[2,5,2,16,256]{4,3,2,1,0:T(8,128)S(1)}, u32[]{:S(2)}, u32[]{:S(2)}) collective-permute-start(f32[2,5,2,16,256]{4,3,2,1,0:T(8,128)S(1)} %get-tuple-element.46), channel_id=1, source_target_pairs={{0,0},{1,2},{2,1},{3,3},{4,4},{5,6},{6,5},{7,7},{8,8},{9,10},{10,9... | collective-permute-start | bytes 983048 | tf_op jit(solution)/shard_map/ppermute | solution.py:667
  98.5 36.9 %collective-permute-start.15 = (f32[5,6,16,256]{3,2,1,0:T(8,128)S(1)}, f32[5,6,16,256]{3,2,1,0:T(8,128)S(1)}, u32[]{:S(2)}, u32[]{:S(2)}) collective-permute-start(f32[5,6,16,256]{3,2,1,0:T(8,128)S(1)} %get-tuple-element.44), channel_id=1, source_target_pairs={{0,16},{4,20},{8,24},{12,28},{16,0},{20,4},{24,8},{28,12},{1,17},{... | collective-permute-start | bytes 1474568 | tf_op jit(solution)/shard_map/ppermute | solution.py:729
  104.9 32.2 %collective-permute-start.14 = (f32[5,6,16,256]{3,2,1,0:T(8,128)S(1)}, f32[5,6,16,256]{3,2,1,0:T(8,128)S(1)}, u32[]{:S(2)}, u32[]{:S(2)}) collective-permute-start(f32[5,6,16,256]{3,2,1,0:T(8,128)S(1)} %get-tuple-element.42), channel_id=1, source_target_pairs={{0,16},{4,20},{8,24},{12,28},{16,0},{20,4},{24,8},{28,12},{1,17},{... | collective-permute-start | bytes 1474568 | tf_op jit(solution)/shard_map/ppermute | solution.py:729
  109.7 24.0 %collective-permute-start.18 = (f32[5,6,16,256]{3,2,1,0:T(8,128)S(1)}, f32[5,6,16,256]{3,2,1,0:T(8,128)S(1)}, u32[]{:S(2)}, u32[]{:S(2)}) collective-permute-start(f32[5,6,16,256]{3,2,1,0:T(8,128)S(1)} %get-tuple-element.48), channel_id=1, source_target_pairs={{0,16},{4,20},{8,24},{12,28},{16,0},{20,4},{24,8},{28,12},{1,17},{... | collective-permute-start | bytes 1474568 | tf_op jit(solution)/shard_map/ppermute | solution.py:729
  116.1 27.5 %collective-permute-start.13 = (f32[5,6,16,256]{3,2,1,0:T(8,128)S(1)}, f32[5,6,16,256]{3,2,1,0:T(8,128)S(1)}, u32[]{:S(2)}, u32[]{:S(2)}) collective-permute-start(f32[5,6,16,256]{3,2,1,0:T(8,128)S(1)} %get-tuple-element.40), channel_id=1, source_target_pairs={{0,16},{4,20},{8,24},{12,28},{16,0},{20,4},{24,8},{28,12},{1,17},{... | collective-permute-start | bytes 1474568 | tf_op jit(solution)/shard_map/ppermute | solution.py:729
